TPU v7x, 512 devices: a whole 4x8x8 slice. The times are simulated.
512 devices in a mesh: section: 16 (over x, z_hi), tensor: 32 (over y, z_lo, core).
Axes of the slice: x: 4, y: 8, z: 8 (z_hi: 4, z_lo: 2; z = z_hi * 2 + z_lo), core: 2. Of those that a mesh axis runs over, the one named last changes fastest.
Arguments:
- x_in: bfloat16 [16, 512, 4096], P('section', 'tensor'), may hold values from -40 to 40
- grad_out: bfloat16 [16, 512, 4096], P('section', 'tensor'), may hold values from -50 to 50
- gain: float32 [16, 4096], P('section'), may hold values from 0.5 to 1.5
- w_val: bfloat16 [16, 4096, 4096], P('section', 'tensor'), may hold values from -0.09375 to 0.09375
- w_out: bfloat16 [16, 4096, 4096], P('section', 'tensor'), may hold values from -0.09375 to 0.09375
- filt: float32 [16, 3, 4096], P('section', None, 'tensor'), may hold values from -3 to 3
- tail: bfloat16 [16, 2, 4096], P('section', None, 'tensor'), may hold values from -6 to 6
- micro_index: int32 [16], P('section'), may hold values from 0 to 15
Outputs:
- grad_in: bfloat16 [16, 512, 4096], P('section', 'tensor')
- grad_w_val: bfloat16 [16, 4096, 4096], P('section', 'tensor')
- grad_w_out: bfloat16 [16, 4096, 4096], P('section', 'tensor')
- grad_filter: float32 [16, 3, 4096], P('section', None, 'tensor')
- grad_tail: float32 [16, 2, 4096], P('section', None, 'tensor')
- grad_gain: float32 [16, 4096], P('section')
All inputs are finite; a program needn't handle non-finite values.
Results may differ from a plain program's by a relative error of at most 0.023.
Values may be sent and summed in bfloat16 or wider, within the bound.
No kernel may reach another device: no remote copies, remote signals or barrier semaphores. Data moves between devices by JAX's collectives and lax.ppermute only.
A program may use at most 64 MiB of HBM per device.

v0:
```python
import jax
import jax.numpy as jnp
from jax import lax
from jax.sharding import PartitionSpec as P

TAPS = 3


EPSILON = 1e-06


def shifted(block, axis, distance):
    devices = range(lax.axis_size(axis))
    route = [((i - distance) % len(devices), i) for i in devices]
    return lax.ppermute(block, axis, route)


def contract_last(left, right):
    return lax.dot_general(
        left, right, (((1,), (1,)), ((), ())), preferred_element_type=jnp.float32
    )


def contract_first(left, right):
    return lax.dot_general(
        left, right, (((0,), (0,)), ((), ())), preferred_element_type=jnp.float32
    )


def on_device(x_in, grad_out, gain, w_val, w_out, filt, tail, micro_index):
    x_rows = x_in[0]
    cot_rows = grad_out[0]
    gain_row = gain[0]
    val_weight = w_val[0]
    out_weight = w_out[0]
    filters = filt[0]
    tail_rows = tail[0]
    has_tail = micro_index[0] > 0
    x_float = x_rows.astype(jnp.float32)
    inv_rms = lax.rsqrt(jnp.mean(x_float * x_float, axis=-1, keepdims=True) + EPSILON)
    normed = (x_float * inv_rms * gain_row).astype(jnp.bfloat16)
    normed_all = lax.all_gather(normed, "tensor", axis=0, tiled=True)
    seq_len = normed_all.shape[0]
    values = contract_last(normed_all, val_weight).astype(jnp.bfloat16)
    lead_rows = jnp.where(has_tail, tail_rows, jnp.zeros_like(tail_rows))
    extended = jnp.concatenate([lead_rows, values], axis=0).astype(jnp.float32)
    conv_out = filters[0] * extended[TAPS - 1 : TAPS - 1 + seq_len]
    for tap in range(1, TAPS):
        conv_out = conv_out + filters[tap] * extended[TAPS - 1 - tap : TAPS - 1 - tap + seq_len]
    gate_sig = jax.nn.sigmoid(conv_out)
    gated = (conv_out * gate_sig).astype(jnp.bfloat16)
    grad_gated = contract_last(lax.all_gather(cot_rows, "tensor", axis=0, tiled=True), out_weight)
    grad_wo = contract_first(gated, lax.all_gather(cot_rows, "tensor", axis=0, tiled=True))
    grad_conv = grad_gated * gate_sig * (1.0 + conv_out * (1.0 - gate_sig))
    grad_filter = jnp.stack(
        [
            jnp.sum(grad_conv * extended[TAPS - 1 - tap : TAPS - 1 - tap + seq_len], axis=0)
            for tap in range(TAPS)
        ]
    )
    padded = jnp.pad(grad_conv, ((TAPS - 1, TAPS - 1), (0, 0)))
    grad_ext = filters[0] * padded[0 : seq_len + TAPS - 1]
    for tap in range(1, TAPS):
        grad_ext = grad_ext + filters[tap] * padded[tap : tap + seq_len + TAPS - 1]
    grad_values = grad_ext[TAPS - 1 :].astype(jnp.bfloat16)
    grad_tail = jnp.where(has_tail, grad_ext[: TAPS - 1], jnp.zeros_like(grad_ext[: TAPS - 1]))
    grad_wv = contract_first(grad_values, normed_all)
    grad_normed = lax.psum_scatter(
        jnp.dot(grad_values, val_weight, preferred_element_type=jnp.float32).astype(jnp.bfloat16),
        "tensor",
        scatter_dimension=0,
        tiled=True,
    ).astype(jnp.float32)
    gain_term = jnp.sum(grad_normed * x_float * inv_rms, axis=0)
    grad_gain = lax.psum(gain_term, "tensor")
    scaled = gain_row * grad_normed
    grad_local = (
        cot_rows.astype(jnp.float32)
        + inv_rms * scaled
        - x_float * inv_rms**3 * jnp.mean(scaled * x_float, axis=-1, keepdims=True)
    )
    received = shifted(grad_local.astype(jnp.bfloat16), "section", -1)
    return (
        received[None],
        grad_wv.astype(jnp.bfloat16)[None],
        grad_wo.astype(jnp.bfloat16)[None],
        grad_filter[None],
        grad_tail[None],
        grad_gain[None],
    )


def solution(mesh):
    placed = (
        P("section", "tensor", None),
        P("section", "tensor", None),
        P("section", None),
        P("section", "tensor", None),
        P("section", "tensor", None),
        P("section", None, "tensor"),
        P("section", None, "tensor"),
        P("section"),
    )
    return jax.shard_map(
        on_device,
        mesh=mesh,
        in_specs=placed,
        out_specs=(
            P("section", "tensor", None),
            P("section", "tensor", None),
            P("section", "tensor", None),
            P("section", None, "tensor"),
            P("section", None, "tensor"),
            P("section", None),
        ),
        check_vma=False,
    )
```

profile of v0, /device:TPU:32, one launch (start us, length us, event | category | flops | bytes accessed | tf_op | source)
XLA Modules:
  0.0 413.5 jit_solution(13749967059140600081)
XLA Ops:
  7.2 1.2 fusion.18
  8.4 1.7 fusion.20
  10.1 0.0 all-gather.6.cloned.1.call-start
  10.2 0.7 all-gather.6.cloned.1.call-update
  10.9 0.0 reduce-scatter.2.cloned.1.call-start
  11.6 0.7 fusion.27
  12.2 0.7 slice_bitcast_fusion.2
  12.9 69.8 %all-gather.4.cloned.1.call-done = bf16[512,4096]{1,0:T(8,128)(2,1)} async-done(((bf16[16,4096]{1,0:T(8,128)(2,1)}), bf16[512,4096]{1,0:T(8,128)(2,1)}) %all-gather.4.cloned.1.call-update) | async-done | bytes 4194320 | tf_op jit(solution)/shard_map/all_gather | solution.py:42
  82.7 3.4 convolution_convert_fusion.3
  86.2 0.1 multiply_add_fusion.1
  86.3 67.6 %all-gather.6.cloned.1.call-done = bf16[1,512,4096]{2,1,0:T(8,128)(2,1)} async-done(((bf16[1,16,4096]{2,1,0:T(8,128)(2,1)}), bf16[1,512,4096]{2,1,0:T(8,128)(2,1)}) %all-gather.6.cloned.1.call-update) | async-done | bytes 4194320 | tf_op jit(solution)/shard_map/all_gather | solution.py:52
  153.9 3.5 multiply_reduce_fusion.2
  157.4 0.1 multiply_add_fusion
  157.5 3.2 convolution_convert_fusion
  160.8 0.6 copy.14
  161.4 4.2 %fusion.1 = bf16[1,128,4096]{2,1,0:T(8,128)(2,1)} fusion(bf16[1,512,4096]{2,1,0:T(8,128)(2,1)} %all-gather.6.cloned.1.call-done, f32[512,128]{1,0:T(8,128)S(1)} %multiply_add_fusion.1), kind=kOutput, calls=%fused_computation.4 | convolution fusion | flops 537722880 | bytes 5505024 | tf_op jit(solution)/shard_map/dot_general | solution.py:25
  165.6 1.7 fusion
  167.3 120.2 %reduce-scatter.2.cloned.1.call-done = bf16[16,4096]{1,0:T(8,128)(2,1)} async-done(((bf16[512,4096]{1,0:T(8,128)(2,1)}), bf16[16,4096]{1,0:T(8,128)(2,1)}) %reduce-scatter.2.cloned.1.call-update) | async-done | bytes 131088 | tf_op jit(solution)/shard_map/reduce_scatter | solution.py:68
  287.6 1.2 fusion.24
  288.7 1.0 fusion.17
  289.8 7.5 %collective-permute-start = (bf16[16,4096]{1,0:T(8,128)(2,1)S(1)}, bf16[16,4096]{1,0:T(8,128)(2,1)S(1)}, u32[]{:S(2)}, u32[]{:S(2)}) collective-permute-start(bf16[16,4096]{1,0:T(8,128)(2,1)S(1)} %fusion.17), channel_id=1, source_target_pairs={{32,0},{64,32},{96,64},{128,96},{160,128},{192,160},{224,192},{256... | collective-permute-start | bytes 393224 | tf_op jit(solution)/shard_map/ppermute | solution.py:15
  297.3 0.6 fusion.26
  297.9 108.5 %psum.7 = f32[1,4096]{1,0:T(1,128)} all-reduce(f32[1,4096]{1,0:T(1,128)S(1)} %bitcast.60), channel_id=1, replica_groups=mesh['section'=16,'tensor'=32] {'tensor'}, use_global_device_ids=true, to_apply=%region_7.8 | all-reduce | flops 4096 | bytes 32768 | tf_op jit(solution)/shard_map/psum | solution.py:75
  406.3 0.7 copy.17
  (20 shorter events, 0.2 us)
Async XLA Ops:
  7.2 75.6 %copy-start = (bf16[1,128,4096]{2,1,0:T(8,128)(2,1)S(1)}, bf16[1,128,4096]{2,1,0:T(8,128)(2,1)}, u32[]{:S(2)}) copy-start(bf16[1,128,4096]{2,1,0:T(8,128)(2,1)} %param.11) | copy-start | bytes 3145732
  7.2 146.8 %copy-start.5 = (bf16[1,128,4096]{2,1,0:T(8,128)(2,1)S(1)}, bf16[1,128,4096]{2,1,0:T(8,128)(2,1)}, u32[]{:S(2)}) copy-start(bf16[1,128,4096]{2,1,0:T(8,128)(2,1)} %param.12) | copy-start | bytes 3145732
  7.2 75.5 %all-gather.4.cloned.1.call-start = ((), (), s32[]{:S(2)}) async-start(), calls=%async_computation.1 | async-start | bytes 4325376 | tf_op jit(solution)/shard_map/all_gather | solution.py:42
  10.1 143.8 %all-gather.6.cloned.1.call-start = ((), (), s32[]{:S(2)}) async-start(), calls=%async_computation.3 | async-start | bytes 4325376 | tf_op jit(solution)/shard_map/all_gather | solution.py:52
  10.9 276.7 %reduce-scatter.2.cloned.1.call-start = ((), (), s32[]{:S(2)}) async-start(), calls=%async_computation.2 | async-start | bytes 4325376 | tf_op jit(solution)/shard_map/reduce_scatter | solution.py:68
  160.8 4.8 %copy-start.1 = (bf16[512,4096]{1,0:T(8,128)(2,1)S(1)}, bf16[512,4096]{1,0:T(8,128)(2,1)}, u32[]{:S(2)}) copy-start(bf16[512,4096]{1,0:T(8,128)(2,1)} %all-gather.4.cloned.1.call-done) | copy-start | bytes 12582916
  161.3 126.2 %copy-start.2 = (bf16[1,16,4096]{2,1,0:T(8,128)(2,1)S(1)}, bf16[1,16,4096]{2,1,0:T(8,128)(2,1)}, u32[]{:S(2)}) copy-start(bf16[1,16,4096]{2,1,0:T(8,128)(2,1)} %param.8) | copy-start | bytes 393220
  161.3 126.2 %copy-start.4 = (f32[1,4096]{1,0:T(1,128)S(1)}, f32[1,4096]{1,0:T(1,128)}, u32[]{:S(2)}) copy-start(f32[1,4096]{1,0:T(1,128)} %param.10) | copy-start | bytes 49156
  165.6 123.1 %copy-start.3 = (bf16[1,16,4096]{2,1,0:T(8,128)(2,1)S(1)}, bf16[1,16,4096]{2,1,0:T(8,128)(2,1)}, u32[]{:S(2)}) copy-start(bf16[1,16,4096]{2,1,0:T(8,128)(2,1)} %param.9) | copy-start | bytes 393220
  289.8 116.6 %collective-permute-start = (bf16[16,4096]{1,0:T(8,128)(2,1)S(1)}, bf16[16,4096]{1,0:T(8,128)(2,1)S(1)}, u32[]{:S(2)}, u32[]{:S(2)}) collective-permute-start(bf16[16,4096]{1,0:T(8,128)(2,1)S(1)} %fusion.17), channel_id=1, source_target_pairs={{32,0},{64,32},{96,64},{128,96},{160,128},{192,160},{224,192},{256... | collective-permute-start | bytes 393224 | tf_op jit(solution)/shard_map/ppermute | solution.py:15
Sparse Core Ops, SparseCore 0:
  10.7 71.9 all-gather.3
  84.9 69.0 all-gather.5
  160.9 126.6 reduce-scatter.1
where the time goes:
time: 414 us
  waiting for transfers between devices  258 us (62%)
  blocking collectives  108 us (26%)
  matrix products  16.1 us (4%)
  between operations  14.5 us (4%)
  starting transfers between devices  7.63 us (2%)
  other arithmetic  6.52 us (2%)
    reduce_scatter x1, waiting for transfers between devices, on_device(): lax.psum_scatter(jnp.dot(grad_values, val_weight, preferred_element_type=...  120 us
    psum x1, blocking collectives, on_device(): grad_gain = lax.psum(gain_term, 'tensor')  108 us
    all_gather x1, waiting for transfers between devices, on_device(): normed_all = lax.all_gather(normed, 'tensor', axis=0, tiled=True)  69.8 us
    all_gather x1, waiting for transfers between devices, on_device(): lax.all_gather(cot_rows, 'tensor', axis=0, tiled=True)  67.6 us
  transfers between devices with their start and end apart: 4, of which 3 were waited for; matrix products, arithmetic and copies ran while one was open for 3% of the time, Pallas kernels for 0%

commit v1 on v0

v1 whole, which is shorter than its diff:
```python
import jax
import jax.numpy as jnp
from jax import lax
from jax.sharding import Mesh, PartitionSpec as P

TAPS = 3
EPSILON = 1e-06
Y, Z, CORE = 8, 2, 2
TENSOR = ("y", "z", "core")
F32, BF16 = jnp.float32, jnp.bfloat16


def contract(left, right, dims):
    return lax.dot_general(left, right, (dims, ((), ())), preferred_element_type=F32)


def to_previous(block, flip_z=False):
    sections = lax.axis_size("section")
    route = []
    for s in range(sections):
        for z in range(Z):
            target = ((s - 1) % sections, 1 - z if flip_z else z)
            route.append((s * Z + z, target[0] * Z + target[1]))
    return lax.ppermute(block, ("section", "z"), route)


def summed_in_pairs(total, steps):
    for axis, apart in steps:
        devices = range(lax.axis_size(axis))
        total = total + lax.ppermute(total, axis, [(i, i ^ apart) for i in devices])
    return total


def on_device(x_in, grad_out, gain, w_val, w_out, filt, tail, micro_index):
    x_rows, cot_rows, gain_row = x_in[0], grad_out[0], gain[0]
    val_weight, out_weight = w_val[0], w_out[0]
    filters, tail_rows = filt[0], tail[0]
    has_tail = micro_index[0] > 0
    rows, width = x_rows.shape
    channels = val_weight.shape[0]
    tokens = rows * Y * Z * CORE

    x_float = x_rows.astype(F32)
    inv_rms = lax.rsqrt(jnp.mean(x_float * x_float, axis=-1, keepdims=True) + EPSILON)
    normed = (x_float * inv_rms * gain_row).astype(BF16)
    both = jnp.concatenate([normed, cot_rows], axis=0)
    both = lax.all_gather(both, "z", axis=0, tiled=True)
    both = lax.all_gather(both, ("y", "core"), axis=0, tiled=True)

    next_rows = to_previous(jnp.concatenate([x_rows, cot_rows], axis=0))
    next_gain = to_previous(gain_row[None])

    weights = jnp.concatenate([val_weight, out_weight], axis=0)
    products = contract(both, weights, ((1,), (1,)))
    products = products.reshape(Y, CORE, Z, 2, rows, 2, channels)

    def in_token_order(block):
        return block.transpose(0, 2, 1, 3, 4).reshape(tokens, channels)

    values = in_token_order(products[:, :, :, 0, :, 0]).astype(BF16)
    grad_gated = in_token_order(products[:, :, :, 1, :, 1])

    lead_rows = jnp.where(has_tail, tail_rows, jnp.zeros_like(tail_rows))
    extended = jnp.concatenate([lead_rows, values], axis=0).astype(F32)
    conv_out = filters[0] * extended[TAPS - 1 : TAPS - 1 + tokens]
    for tap in range(1, TAPS):
        conv_out = conv_out + filters[tap] * extended[TAPS - 1 - tap : TAPS - 1 - tap + tokens]
    gate_sig = jax.nn.sigmoid(conv_out)
    gated = (conv_out * gate_sig).astype(BF16)
    grad_conv = grad_gated * gate_sig * (1.0 + conv_out * (1.0 - gate_sig))
    grad_filter = jnp.stack(
        [
            jnp.sum(grad_conv * extended[TAPS - 1 - tap : TAPS - 1 - tap + tokens], axis=0)
            for tap in range(TAPS)
        ]
    )
    padded = jnp.pad(grad_conv, ((TAPS - 1, TAPS - 1), (0, 0)))
    grad_ext = filters[0] * padded[0 : tokens + TAPS - 1]
    for tap in range(1, TAPS):
        grad_ext = grad_ext + filters[tap] * padded[tap : tap + tokens + TAPS - 1]
    grad_values = grad_ext[TAPS - 1 :].astype(BF16)
    grad_tail = jnp.where(has_tail, grad_ext[: TAPS - 1], jnp.zeros_like(grad_ext[: TAPS - 1]))

    placed = grad_values.reshape(Y, Z, CORE, rows, channels)
    placed = jnp.where(lax.axis_index("z") == 0, placed, placed[:, ::-1])
    placed = placed.transpose(2, 0, 1, 3, 4).reshape(CORE, tokens // CORE, channels)
    own_core = lax.axis_index("core") == 0
    kept = jnp.where(own_core, placed[0], placed[1])
    given = jnp.where(own_core, placed[1], placed[0])
    share = contract(given, val_weight, ((1,), (0,))).astype(BF16)
    share = lax.ppermute(share, "core", [(0, 1), (1, 0)])
    share = contract(kept, val_weight, ((1,), (0,))) + share.astype(F32)
    share = lax.psum_scatter(share.astype(BF16), "y", scatter_dimension=0, tiled=True)

    def in_gathered_order(block):
        return block.reshape(Y, Z, CORE, rows, channels).transpose(0, 2, 1, 3, 4)

    zeros = jnp.zeros((Y, CORE, Z, rows, channels), BF16)
    factors = jnp.stack(
        [
            jnp.concatenate([in_gathered_order(grad_values), zeros], axis=-1),
            jnp.concatenate([zeros, in_gathered_order(gated)], axis=-1),
        ],
        axis=3,
    ).reshape(2 * tokens, 2 * channels)
    grad_weights = contract(factors, both, ((0,), (0,)))
    grad_wv, grad_wo = grad_weights[:channels], grad_weights[channels:]
    gain_term = jnp.sum(grad_wv * val_weight.astype(F32), axis=0) / gain_row
    grad_gain = summed_in_pairs(gain_term[None], (("core", 1), ("z", 1), ("y", 1), ("y", 2), ("y", 4)))

    grad_normed = to_previous(share[:rows]).astype(F32) + to_previous(share[rows:], True).astype(F32)
    x_float = next_rows[:rows].astype(F32)
    cot_float = next_rows[rows:].astype(F32)
    inv_rms = lax.rsqrt(jnp.mean(x_float * x_float, axis=-1, keepdims=True) + EPSILON)
    scaled = next_gain * grad_normed
    received = (
        cot_float
        + inv_rms * scaled
        - x_float * inv_rms**3 * jnp.mean(scaled * x_float, axis=-1, keepdims=True)
    ).astype(BF16)
    return (
        received[None],
        grad_wv.astype(BF16)[None],
        grad_wo.astype(BF16)[None],
        grad_filter[None],
        grad_tail[None],
        grad_gain,
    )


def solution(mesh):
    sections = mesh.shape["section"]
    split = Mesh(mesh.devices.reshape(sections, Y, Z, CORE), ("section", *TENSOR))
    by_rows = P("section", TENSOR, None)
    by_columns = P("section", None, TENSOR)
    whole = P("section", None)
    return jax.shard_map(
        on_device,
        mesh=split,
        in_specs=(by_rows, by_rows, whole, by_rows, by_rows, by_columns, by_columns, P("section")),
        out_specs=(by_rows, by_rows, by_rows, by_columns, by_columns, whole),
        check_vma=False,
    )
```

time: 414 us -> 175 us (0.42)
  the two profiles are of different devices: /device:TPU:32 before, /device:TPU:24 now
where the time goes in v1:
time: 175 us; the launch traced here: 174 us
  waiting for transfers between devices  84.2 us (48%)
  starting transfers between devices  38.6 us (22%)
  matrix products  15 us (9%)
  between operations  15 us (9%)
  blocking collectives  9.43 us (5%)
  other arithmetic  6.89 us (4%)
  local copies, waits for them, and re-layouts  5.09 us (3%)
    all_gather x1, waiting for transfers between devices, on_device(): both = lax.all_gather(both, ('y', 'core'), axis=0, tiled=True)  59.8 us
    ppermute x4, starting transfers between devices, to_previous(): return lax.ppermute(block, ('section', 'z'), route)  23.5 us
    dot_general x4, matrix products, contract(): lax.dot_general(left, right, (dims, ((), ())), preferred_element_type=F32)  15 us
    ppermute x5, starting transfers between devices, summed_in_pairs(): total = total + lax.ppermute(total, axis, [(i, i ^ apart) for i in devices])  12.9 us
    reduce_scatter x1, waiting for transfers between devices, on_device(): lax.psum_scatter(share.astype(BF16), 'y', scatter_dimension=0, tiled=True)  11.8 us
    all_gather x1, blocking collectives, on_device(): both = lax.all_gather(both, 'z', axis=0, tiled=True)  9.43 us
    ppermute x5, waiting for transfers between devices, summed_in_pairs(): total = total + lax.ppermute(total, axis, [(i, i ^ apart) for i in devices])  8.61 us
    ppermute x1, waiting for transfers between devices, on_device(): share = lax.ppermute(share, 'core', [(0, 1), (1, 0)])  3.91 us
  transfers between devices with their start and end apart: 12, of which 6 were waited for; matrix products, arithmetic and copies ran while one was open for 7% of the time, Pallas kernels for 0%

profile of v1, /device:TPU:24, one launch (start us, length us, event | category | flops | bytes accessed | tf_op | source)
XLA Modules:
  0.0 174.3 jit_solution(17473329758743696122)
XLA Ops:
  7.2 1.1 fusion.6
  8.3 1.0 fusion.8
  9.3 1.0 pad_maximum_fusion.2
  10.3 9.4 %all_gather.6 = bf16[64,4096]{1,0:T(8,128)(2,1)} all-gather(bf16[32,4096]{1,0:T(8,128)(2,1)S(1)} %get-tuple-element.36), channel_id=1, replica_groups=mesh['section'=16,'y'=8,'z'=2,'core'=2] {'z'}, dimensions={0}, use_global_device_ids=true | all-gather | bytes 786432 | tf_op jit(solution)/shard_map/all_gather | solution.py:47
  21.8 59.8 %all-gather.2.cloned.1.call-done = bf16[1024,4096]{1,0:T(8,128)(2,1)} async-done(((bf16[64,4096]{1,0:T(8,128)(2,1)}), bf16[1024,4096]{1,0:T(8,128)(2,1)}) %all-gather.2.cloned.1.call-update) | async-done | bytes 8388624 | tf_op jit(solution)/shard_map/all_gather | solution.py:48
  81.6 6.3 %fusion = f32[1024,256]{1,0:T(8,128)S(1)} fusion(bf16[1024,4096]{1,0:T(8,128)(2,1)} %all-gather.2.cloned.1.call-done, bf16[128,4096]{1,0:T(8,128)(2,1)} %bitcast.91, bf16[128,4096]{1,0:T(8,128)(2,1)} %bitcast.72), kind=kOutput, calls=%fused_computation.3 | convolution fusion | flops 2151677952 | bytes 11534336 | tf_op jit(solution)/shard_map/dot_general | solution.py:14
  90.2 2.1 %collective-permute-start.2 = (bf16[256,4096]{1,0:T(8,128)(2,1)S(1)}, bf16[256,4096]{1,0:T(8,128)(2,1)S(1)}, u32[]{:S(2)}, u32[]{:S(2)}) collective-permute-start(bf16[256,4096]{1,0:T(8,128)(2,1)S(1)} %convolution_convert_fusion), channel_id=1, source_target_pairs={{0,1},{1,0},{2,3},{3,2},{4,5},{5,4},{6,7},{7,6},{8,9},{9,8},{10,11... | collective-permute-start | bytes 6291464 | tf_op jit(solution)/shard_map/ppermute | solution.py:91
  92.4 3.9 %collective-permute-done.2 = bf16[256,4096]{1,0:T(8,128)(2,1)S(1)} collective-permute-done((bf16[256,4096]{1,0:T(8,128)(2,1)S(1)}, bf16[256,4096]{1,0:T(8,128)(2,1)S(1)}, u32[]{:S(2)}, u32[]{:S(2)}) %collective-permute-start.2) | collective-permute-done | bytes 2097184 | tf_op jit(solution)/shard_map/ppermute | solution.py:91
  96.3 2.1 %add_convert_fusion = bf16[256,4096]{1,0:T(8,128)(2,1)} fusion(bf16[256,4096]{1,0:T(8,128)(2,1)S(1)} %collective-permute-done.2, bf16[256,128]{1,0:T(8,128)(2,1)S(1)} %bitcast.82, bf16[1,128,4096]{2,1,0:T(8,128)(2,1)S(1)} %copy-done), kind=kOutput, calls=%fused_computation.1 | convolution fusion | flops 271581184 | bytes 5308416 | tf_op jit(solution)/shard_map/dot_general | solution.py:14
  98.7 5.9 %fusion.28 = f32[256,4096]{1,0:T(8,128)S(1)} fusion(bf16[1024,256]{1,0:T(8,128)(2,1)S(1)} %bitcast.73, bf16[1024,4096]{1,0:T(8,128)(2,1)} %all-gather.2.cloned.1.call-done), kind=kOutput, calls=%fused_computation.65 | convolution fusion | flops 2147483648 | bytes 13107200 | tf_op jit(solution)/shard_map/dot_general | solution.py:14
  105.0 2.1 %collective-permute-start.5 = (f32[1,4096]{1,0:T(1,128)S(1)}, f32[1,4096]{1,0:T(1,128)S(1)}, u32[]{:S(2)}, u32[]{:S(2)}) collective-permute-start(f32[1,4096]{1,0:T(1,128)S(1)} %div.20), channel_id=1, source_target_pairs={{0,1},{1,0},{2,3},{3,2},{4,5},{5,4},{6,7},{7,6},{8,9},{9,8},{10,11... | collective-permute-start | bytes 49160 | tf_op jit(solution)/shard_map/ppermute | solution.py:30
  108.1 3.5 %collective-permute-start.6 = (f32[1,4096]{1,0:T(1,128)S(1)}, f32[1,4096]{1,0:T(1,128)S(1)}, u32[]{:S(2)}, u32[]{:S(2)}) collective-permute-start(f32[1,4096]{1,0:T(1,128)S(1)} %add.80), channel_id=1, source_target_pairs={{0,2},{2,0},{1,3},{3,1},{4,6},{6,4},{5,7},{7,5},{8,10},{10,8},{9,1... | collective-permute-start | bytes 49160 | tf_op jit(solution)/shard_map/ppermute | solution.py:30
  111.6 7.8 %collective-permute-start.1 = (f32[1,4096]{1,0:T(1,128)S(1)}, f32[1,4096]{1,0:T(1,128)S(1)}, u32[]{:S(2)}, u32[]{:S(2)}) collective-permute-start(f32[1,4096]{1,0:T(1,128)S(1)} %copy-done.1), channel_id=1, source_target_pairs={{0,480},{2,482},{32,0},{34,2},{64,32},{66,34},{96,64},{98,66},{128... | collective-permute-start | bytes 49160 | tf_op jit(solution)/shard_map/ppermute | solution.py:24
  119.5 3.9 %collective-permute-start = (bf16[32,4096]{1,0:T(8,128)(2,1)S(1)}, bf16[32,4096]{1,0:T(8,128)(2,1)S(1)}, u32[]{:S(2)}, u32[]{:S(2)}) collective-permute-start(bf16[32,4096]{1,0:T(8,128)(2,1)S(1)} %get-tuple-element.35), channel_id=1, source_target_pairs={{0,480},{2,482},{32,0},{34,2},{64,32},{66,34},{96,64},{98,66},{128... | collective-permute-start | bytes 786440 | tf_op jit(solution)/shard_map/ppermute | solution.py:24
  123.4 1.9 %collective-permute-start.7 = (f32[1,4096]{1,0:T(1,128)S(1)}, f32[1,4096]{1,0:T(1,128)S(1)}, u32[]{:S(2)}, u32[]{:S(2)}) collective-permute-start(f32[1,4096]{1,0:T(1,128)S(1)} %add.81), channel_id=1, source_target_pairs={{0,4},{4,0},{8,12},{12,8},{16,20},{20,16},{24,28},{28,24},{1,5},{5... | collective-permute-start | bytes 49160 | tf_op jit(solution)/shard_map/ppermute | solution.py:30
  125.3 1.6 fusion.5
  126.9 2.1 %collective-permute-done.7 = f32[1,4096]{1,0:T(1,128)S(1)} collective-permute-done((f32[1,4096]{1,0:T(1,128)S(1)}, f32[1,4096]{1,0:T(1,128)S(1)}, u32[]{:S(2)}, u32[]{:S(2)}) %collective-permute-start.7) | collective-permute-done | bytes 16416 | tf_op jit(solution)/shard_map/ppermute | solution.py:30
  129.1 1.9 %collective-permute-start.8 = (f32[1,4096]{1,0:T(1,128)S(1)}, f32[1,4096]{1,0:T(1,128)S(1)}, u32[]{:S(2)}, u32[]{:S(2)}) collective-permute-start(f32[1,4096]{1,0:T(1,128)S(1)} %add.82), channel_id=1, source_target_pairs={{0,8},{4,12},{8,0},{12,4},{16,24},{20,28},{24,16},{28,20},{1,9},{5... | collective-permute-start | bytes 49160 | tf_op jit(solution)/shard_map/ppermute | solution.py:30
  131.0 11.8 %reduce-scatter.2.cloned.1.call-done = bf16[32,4096]{1,0:T(8,128)(2,1)} async-done(((bf16[256,4096]{1,0:T(8,128)(2,1)}), bf16[32,4096]{1,0:T(8,128)(2,1)}) %reduce-scatter.2.cloned.1.call-update) | async-done | bytes 262160 | tf_op jit(solution)/shard_map/reduce_scatter | solution.py:93
  142.8 1.0 fusion.27
  143.8 8.7 %collective-permute-start.3 = (bf16[16,4096]{1,0:T(8,128)(2,1)S(1)}, bf16[16,4096]{1,0:T(8,128)(2,1)S(1)}, u32[]{:S(2)}, u32[]{:S(2)}) collective-permute-start(bf16[16,4096]{1,0:T(8,128)(2,1)S(1)} %get-tuple-element.33), channel_id=1, source_target_pairs={{0,480},{2,482},{32,0},{34,2},{64,32},{66,34},{96,64},{98,66},{128... | collective-permute-start | bytes 393224 | tf_op jit(solution)/shard_map/ppermute | solution.py:24
  152.5 3.1 %collective-permute-start.4 = (bf16[16,4096]{1,0:T(8,128)(2,1)S(1)}, bf16[16,4096]{1,0:T(8,128)(2,1)S(1)}, u32[]{:S(2)}, u32[]{:S(2)}) collective-permute-start(bf16[16,4096]{1,0:T(8,128)(2,1)S(1)} %get-tuple-element.34), channel_id=1, source_target_pairs={{0,482},{2,480},{32,2},{34,0},{64,34},{66,32},{96,66},{98,64},{128... | collective-permute-start | bytes 393224 | tf_op jit(solution)/shard_map/ppermute | solution.py:24
  156.2 3.4 %collective-permute-start.9 = (f32[1,4096]{1,0:T(1,128)S(1)}, f32[1,4096]{1,0:T(1,128)S(1)}, u32[]{:S(2)}, u32[]{:S(2)}) collective-permute-start(f32[1,4096]{1,0:T(1,128)S(1)} %add.83), channel_id=1, source_target_pairs={{0,16},{4,20},{8,24},{12,28},{16,0},{20,4},{24,8},{28,12},{1,17},{... | collective-permute-start | bytes 49160 | tf_op jit(solution)/shard_map/ppermute | solution.py:30
  160.2 5.6 %collective-permute-done.9 = f32[1,4096]{1,0:T(1,128)S(1)} collective-permute-done((f32[1,4096]{1,0:T(1,128)S(1)}, f32[1,4096]{1,0:T(1,128)S(1)}, u32[]{:S(2)}, u32[]{:S(2)}) %collective-permute-start.9) | collective-permute-done | bytes 16416 | tf_op jit(solution)/shard_map/ppermute | solution.py:30
  (49 shorter events, 8.1 us)
Async XLA Ops:
  7.2 74.5 %all-gather.2.cloned.1.call-start = ((), (), s32[]{:S(2)}) async-start(), calls=%async_computation.1 | async-start | bytes 8912896 | tf_op jit(solution)/shard_map/all_gather | solution.py:48
  19.8 123.1 %reduce-scatter.2.cloned.1.call-start = ((), (), s32[]{:S(2)}) async-start(), calls=%async_computation.2 | async-start | bytes 2359296 | tf_op jit(solution)/shard_map/reduce_scatter | solution.py:93
  87.9 1.6 copy-start
  90.2 6.1 %collective-permute-start.2 = (bf16[256,4096]{1,0:T(8,128)(2,1)S(1)}, bf16[256,4096]{1,0:T(8,128)(2,1)S(1)}, u32[]{:S(2)}, u32[]{:S(2)}) collective-permute-start(bf16[256,4096]{1,0:T(8,128)(2,1)S(1)} %convolution_convert_fusion), channel_id=1, source_target_pairs={{0,1},{1,0},{2,3},{3,2},{4,5},{5,4},{6,7},{7,6},{8,9},{9,8},{10,11... | collective-permute-start | bytes 6291464 | tf_op jit(solution)/shard_map/ppermute | solution.py:91
  98.7 6.2 %copy-start.1 = (f32[1,4096]{1,0:T(1,128)S(1)}, f32[1,4096]{1,0:T(1,128)}, u32[]{:S(2)}) copy-start(f32[1,4096]{1,0:T(1,128)} %param.10) | copy-start | bytes 49156
  105.0 3.1 %collective-permute-start.5 = (f32[1,4096]{1,0:T(1,128)S(1)}, f32[1,4096]{1,0:T(1,128)S(1)}, u32[]{:S(2)}, u32[]{:S(2)}) collective-permute-start(f32[1,4096]{1,0:T(1,128)S(1)} %div.20), channel_id=1, source_target_pairs={{0,1},{1,0},{2,3},{3,2},{4,5},{5,4},{6,7},{7,6},{8,9},{9,8},{10,11... | collective-permute-start | bytes 49160 | tf_op jit(solution)/shard_map/ppermute | solution.py:30
  108.1 15.3 %collective-permute-start.6 = (f32[1,4096]{1,0:T(1,128)S(1)}, f32[1,4096]{1,0:T(1,128)S(1)}, u32[]{:S(2)}, u32[]{:S(2)}) collective-permute-start(f32[1,4096]{1,0:T(1,128)S(1)} %add.80), channel_id=1, source_target_pairs={{0,2},{2,0},{1,3},{3,1},{4,6},{6,4},{5,7},{7,5},{8,10},{10,8},{9,1... | collective-permute-start | bytes 49160 | tf_op jit(solution)/shard_map/ppermute | solution.py:30
  111.6 54.7 %collective-permute-start.1 = (f32[1,4096]{1,0:T(1,128)S(1)}, f32[1,4096]{1,0:T(1,128)S(1)}, u32[]{:S(2)}, u32[]{:S(2)}) collective-permute-start(f32[1,4096]{1,0:T(1,128)S(1)} %copy-done.1), channel_id=1, source_target_pairs={{0,480},{2,482},{32,0},{34,2},{64,32},{66,34},{96,64},{98,66},{128... | collective-permute-start | bytes 49160 | tf_op jit(solution)/shard_map/ppermute | solution.py:24
  119.5 46.9 %collective-permute-start = (bf16[32,4096]{1,0:T(8,128)(2,1)S(1)}, bf16[32,4096]{1,0:T(8,128)(2,1)S(1)}, u32[]{:S(2)}, u32[]{:S(2)}) collective-permute-start(bf16[32,4096]{1,0:T(8,128)(2,1)S(1)} %get-tuple-element.35), channel_id=1, source_target_pairs={{0,480},{2,482},{32,0},{34,2},{64,32},{66,34},{96,64},{98,66},{128... | collective-permute-start | bytes 786440 | tf_op jit(solution)/shard_map/ppermute | solution.py:24
  123.4 5.6 %collective-permute-start.7 = (f32[1,4096]{1,0:T(1,128)S(1)}, f32[1,4096]{1,0:T(1,128)S(1)}, u32[]{:S(2)}, u32[]{:S(2)}) collective-permute-start(f32[1,4096]{1,0:T(1,128)S(1)} %add.81), channel_id=1, source_target_pairs={{0,4},{4,0},{8,12},{12,8},{16,20},{20,16},{24,28},{28,24},{1,5},{5... | collective-permute-start | bytes 49160 | tf_op jit(solution)/shard_map/ppermute | solution.py:30
  129.1 27.1 %collective-permute-start.8 = (f32[1,4096]{1,0:T(1,128)S(1)}, f32[1,4096]{1,0:T(1,128)S(1)}, u32[]{:S(2)}, u32[]{:S(2)}) collective-permute-start(f32[1,4096]{1,0:T(1,128)S(1)} %add.82), channel_id=1, source_target_pairs={{0,8},{4,12},{8,0},{12,4},{16,24},{20,28},{24,16},{28,20},{1,9},{5... | collective-permute-start | bytes 49160 | tf_op jit(solution)/shard_map/ppermute | solution.py:30
  143.8 22.6 %collective-permute-start.3 = (bf16[16,4096]{1,0:T(8,128)(2,1)S(1)}, bf16[16,4096]{1,0:T(8,128)(2,1)S(1)}, u32[]{:S(2)}, u32[]{:S(2)}) collective-permute-start(bf16[16,4096]{1,0:T(8,128)(2,1)S(1)} %get-tuple-element.33), channel_id=1, source_target_pairs={{0,480},{2,482},{32,0},{34,2},{64,32},{66,34},{96,64},{98,66},{128... | collective-permute-start | bytes 393224 | tf_op jit(solution)/shard_map/ppermute | solution.py:24
  152.5 13.9 %collective-permute-start.4 = (bf16[16,4096]{1,0:T(8,128)(2,1)S(1)}, bf16[16,4096]{1,0:T(8,128)(2,1)S(1)}, u32[]{:S(2)}, u32[]{:S(2)}) collective-permute-start(bf16[16,4096]{1,0:T(8,128)(2,1)S(1)} %get-tuple-element.34), channel_id=1, source_target_pairs={{0,482},{2,480},{32,2},{34,0},{64,34},{66,32},{96,66},{98,64},{128... | collective-permute-start | bytes 393224 | tf_op jit(solution)/shard_map/ppermute | solution.py:24
  156.2 9.5 %collective-permute-start.9 = (f32[1,4096]{1,0:T(1,128)S(1)}, f32[1,4096]{1,0:T(1,128)S(1)}, u32[]{:S(2)}, u32[]{:S(2)}) collective-permute-start(f32[1,4096]{1,0:T(1,128)S(1)} %add.83), channel_id=1, source_target_pairs={{0,16},{4,20},{8,24},{12,28},{16,0},{20,4},{24,8},{28,12},{1,17},{... | collective-permute-start | bytes 49160 | tf_op jit(solution)/shard_map/ppermute | solution.py:30
Sparse Core Ops, SparseCore 0:
  19.9 61.6 all-gather.1
  98.5 44.2 reduce-scatter.1

commit v2 on v1

--- a/solution.py
+++ b/solution.py
@@ -7,6 +7,7 @@
 EPSILON = 1e-06
 Y, Z, CORE = 8, 2, 2
 TENSOR = ("y", "z", "core")
+SWAP = ((0, 1), (1, 0))
 F32, BF16 = jnp.float32, jnp.bfloat16
 
 
@@ -49,6 +50,8 @@
 
     next_rows = to_previous(jnp.concatenate([x_rows, cot_rows], axis=0))
     next_gain = to_previous(gain_row[None])
+    pair_weight = lax.ppermute(val_weight, "core", SWAP)
+    both, next_rows, next_gain, pair_weight = lax.optimization_barrier((both, next_rows, next_gain, pair_weight))
 
     weights = jnp.concatenate([val_weight, out_weight], axis=0)
     products = contract(both, weights, ((1,), (1,)))
@@ -87,9 +90,12 @@
     own_core = lax.axis_index("core") == 0
     kept = jnp.where(own_core, placed[0], placed[1])
     given = jnp.where(own_core, placed[1], placed[0])
-    share = contract(given, val_weight, ((1,), (0,))).astype(BF16)
-    share = lax.ppermute(share, "core", [(0, 1), (1, 0)])
-    share = contract(kept, val_weight, ((1,), (0,))) + share.astype(F32)
+    taken = lax.ppermute(given, "core", SWAP)
+    share = contract(
+        jnp.concatenate([kept, taken], axis=1),
+        jnp.concatenate([val_weight, pair_weight], axis=0),
+        ((1,), (0,)),
+    )
     share = lax.psum_scatter(share.astype(BF16), "y", scatter_dimension=0, tiled=True)
 
     def in_gathered_order(block):
@@ -107,6 +113,8 @@
     grad_wv, grad_wo = grad_weights[:channels], grad_weights[channels:]
     gain_term = jnp.sum(grad_wv * val_weight.astype(F32), axis=0) / gain_row
     grad_gain = summed_in_pairs(gain_term[None], (("core", 1), ("z", 1), ("y", 1), ("y", 2), ("y", 4)))
+
+    share, grad_gain = lax.optimization_barrier((share, grad_gain))
 
     grad_normed = to_previous(share[:rows]).astype(F32) + to_previous(share[rows:], True).astype(F32)
     x_float = next_rows[:rows].astype(F32)

time: 175 us -> 165 us (0.943)
  the two profiles are of different devices: /device:TPU:24 before, /device:TPU:16 now
where the time goes in v2:
time: 165 us
  waiting for transfers between devices  64 us (39%)
  starting transfers between devices  49.8 us (30%)
  between operations  15 us (9%)
  matrix products  14.3 us (9%)
  blocking collectives  9.43 us (6%)
  other arithmetic  6.89 us (4%)
  local copies, waits for them, and re-layouts  5.1 us (3%)
    all_gather x1, waiting for transfers between devices, on_device(): both = lax.all_gather(both, ('y', 'core'), axis=0, tiled=True)  29.4 us
    ppermute x4, starting transfers between devices, to_previous(): return lax.ppermute(block, ('section', 'z'), route)  26.9 us
    ppermute x5, starting transfers between devices, summed_in_pairs(): total = total + lax.ppermute(total, axis, [(i, i ^ apart) for i in devices])  18.8 us
    ppermute x4, waiting for transfers between devices, to_previous(): return lax.ppermute(block, ('section', 'z'), route)  17.1 us
    dot_general x3, matrix products, contract(): lax.dot_general(left, right, (dims, ((), ())), preferred_element_type=F32)  14.3 us
    ppermute x5, waiting for transfers between devices, summed_in_pairs(): total = total + lax.ppermute(total, axis, [(i, i ^ apart) for i in devices])  10.3 us
    all_gather x1, blocking collectives, on_device(): both = lax.all_gather(both, 'z', axis=0, tiled=True)  9.43 us
    reduce_scatter x1, waiting for transfers between devices, on_device(): lax.psum_scatter(share.astype(BF16), 'y', scatter_dimension=0, tiled=True)  6.1 us
  transfers between devices with their start and end apart: 13, of which 11 were waited for; matrix products, arithmetic and copies ran while one was open for 7% of the time, Pallas kernels for 0%

profile of v2, /device:TPU:16, one launch (start us, length us, event | category | flops | bytes accessed | tf_op | source)
XLA Modules:
  0.0 164.5 jit_solution(16205053201557336734)
XLA Ops:
  10.3 9.4 %all_gather.6 = bf16[64,4096]{1,0:T(8,128)(2,1)} all-gather(bf16[32,4096]{1,0:T(8,128)(2,1)S(1)} %get-tuple-element.50), channel_id=1, replica_groups=mesh['section'=16,'y'=8,'z'=2,'core'=2] {'z'}, dimensions={0}, use_global_device_ids=true | all-gather | bytes 786432 | tf_op jit(solution)/shard_map/all_gather | solution.py:48
  19.8 1.9 %collective-permute-start.2 = (bf16[128,4096]{1,0:T(8,128)(2,1)}, bf16[128,4096]{1,0:T(8,128)(2,1)S(1)}, u32[]{:S(2)}, u32[]{:S(2)}) collective-permute-start(bf16[128,4096]{1,0:T(8,128)(2,1)} %bitcast.68), channel_id=1, source_target_pairs={{0,1},{1,0},{2,3},{3,2},{4,5},{5,4},{6,7},{7,6},{8,9},{9,8},{10,11... | collective-permute-start | bytes 3145736 | tf_op jit(solution)/shard_map/ppermute | solution.py:53
  21.7 12.5 %collective-permute-start.1 = (f32[1,4096]{1,0:T(1,128)}, f32[1,4096]{1,0:T(1,128)S(1)}, u32[]{:S(2)}, u32[]{:S(2)}) collective-permute-start(f32[1,4096]{1,0:T(1,128)} %param.10), channel_id=1, source_target_pairs={{0,480},{2,482},{32,0},{34,2},{64,32},{66,34},{96,64},{98,66},{128... | collective-permute-start | bytes 49160 | tf_op jit(solution)/shard_map/ppermute | solution.py:25
  34.3 2.5 %collective-permute-start = (bf16[32,4096]{1,0:T(8,128)(2,1)S(1)}, bf16[32,4096]{1,0:T(8,128)(2,1)S(1)}, u32[]{:S(2)}, u32[]{:S(2)}) collective-permute-start(bf16[32,4096]{1,0:T(8,128)(2,1)S(1)} %get-tuple-element.49), channel_id=1, source_target_pairs={{0,480},{2,482},{32,0},{34,2},{64,32},{66,34},{96,64},{98,66},{128... | collective-permute-start | bytes 786440 | tf_op jit(solution)/shard_map/ppermute | solution.py:25
  38.8 12.4 %collective-permute-done = bf16[32,4096]{1,0:T(8,128)(2,1)S(1)} collective-permute-done((bf16[32,4096]{1,0:T(8,128)(2,1)S(1)}, bf16[32,4096]{1,0:T(8,128)(2,1)S(1)}, u32[]{:S(2)}, u32[]{:S(2)}) %collective-permute-start) | collective-permute-done | bytes 262176 | tf_op jit(solution)/shard_map/ppermute | solution.py:25
  51.1 29.4 %all-gather.2.cloned.1.call-done = bf16[1024,4096]{1,0:T(8,128)(2,1)} async-done(((bf16[64,4096]{1,0:T(8,128)(2,1)}), bf16[1024,4096]{1,0:T(8,128)(2,1)}) %all-gather.2.cloned.1.call-update) | async-done | bytes 8388624 | tf_op jit(solution)/shard_map/all_gather | solution.py:49
  80.5 6.3 %fusion = f32[1024,256]{1,0:T(8,128)S(1)} fusion(bf16[1024,4096]{1,0:T(8,128)(2,1)} %all-gather.2.cloned.1.call-done, bf16[128,4096]{1,0:T(8,128)(2,1)} %bitcast.69, bf16[128,4096]{1,0:T(8,128)(2,1)} %bitcast.85), kind=kOutput, calls=%fused_computation.3 | convolution fusion | flops 2151677952 | bytes 11534336 | tf_op jit(solution)/shard_map/dot_general | solution.py:15
  88.4 2.1 %collective-permute-start.3 = (bf16[256,128]{1,0:T(8,128)(2,1)S(1)}, bf16[256,128]{1,0:T(8,128)(2,1)S(1)}, u32[]{:S(2)}, u32[]{:S(2)}) collective-permute-start(bf16[256,128]{1,0:T(8,128)(2,1)S(1)} %bitcast.81), channel_id=1, source_target_pairs={{0,1},{1,0},{2,3},{3,2},{4,5},{5,4},{6,7},{7,6},{8,9},{9,8},{10,11... | collective-permute-start | bytes 196616 | tf_op jit(solution)/shard_map/ppermute | solution.py:93
  91.6 2.1 %convolution_convert_fusion = bf16[256,4096]{1,0:T(8,128)(2,1)} fusion(bf16[128,4096]{1,0:T(8,128)(2,1)S(1)} %bitcast.70, bf16[128,4096]{1,0:T(8,128)(2,1)S(1)} %copy-done.3, bf16[256,128]{1,0:T(8,128)(2,1)S(1)} %collective-permute-done.3, bf16[256,128]{1,0:T(8,128)(2,1)S(1)} %bitcast.80), kind=kOutput, calls=%fused_computation | convolution fusion | flops 542375936 | bytes 4325376 | tf_op jit(solution)/shard_map/dot_general | solution.py:15
  94.0 5.9 %fusion.26 = f32[256,4096]{1,0:T(8,128)S(1)} fusion(bf16[1024,256]{1,0:T(8,128)(2,1)S(1)} %bitcast.64, bf16[1024,4096]{1,0:T(8,128)(2,1)} %all-gather.2.cloned.1.call-done), kind=kOutput, calls=%fused_computation.66 | convolution fusion | flops 2147483648 | bytes 13107200 | tf_op jit(solution)/shard_map/dot_general | solution.py:15
  100.3 2.1 %collective-permute-start.4 = (f32[1,4096]{1,0:T(1,128)S(1)}, f32[1,4096]{1,0:T(1,128)S(1)}, u32[]{:S(2)}, u32[]{:S(2)}) collective-permute-start(f32[1,4096]{1,0:T(1,128)S(1)} %div.19), channel_id=1, source_target_pairs={{0,1},{1,0},{2,3},{3,2},{4,5},{5,4},{6,7},{7,6},{8,9},{9,8},{10,11... | collective-permute-start | bytes 49160 | tf_op jit(solution)/shard_map/ppermute | solution.py:31
  103.4 3.6 %collective-permute-start.5 = (f32[1,4096]{1,0:T(1,128)S(1)}, f32[1,4096]{1,0:T(1,128)S(1)}, u32[]{:S(2)}, u32[]{:S(2)}) collective-permute-start(f32[1,4096]{1,0:T(1,128)S(1)} %add.74), channel_id=1, source_target_pairs={{0,2},{2,0},{1,3},{3,1},{4,6},{6,4},{5,7},{7,5},{8,10},{10,8},{9,1... | collective-permute-start | bytes 49160 | tf_op jit(solution)/shard_map/ppermute | solution.py:31
  106.9 2.1 %collective-permute-done.5 = f32[1,4096]{1,0:T(1,128)S(1)} collective-permute-done((f32[1,4096]{1,0:T(1,128)S(1)}, f32[1,4096]{1,0:T(1,128)S(1)}, u32[]{:S(2)}, u32[]{:S(2)}) %collective-permute-start.5) | collective-permute-done | bytes 16416 | tf_op jit(solution)/shard_map/ppermute | solution.py:31
  109.0 4.6 %collective-permute-start.6 = (f32[1,4096]{1,0:T(1,128)S(1)}, f32[1,4096]{1,0:T(1,128)S(1)}, u32[]{:S(2)}, u32[]{:S(2)}) collective-permute-start(f32[1,4096]{1,0:T(1,128)S(1)} %add.75), channel_id=1, source_target_pairs={{0,4},{4,0},{8,12},{12,8},{16,20},{20,16},{24,28},{28,24},{1,5},{5... | collective-permute-start | bytes 49160 | tf_op jit(solution)/shard_map/ppermute | solution.py:31
  113.6 1.8 %collective-permute-done.6 = f32[1,4096]{1,0:T(1,128)S(1)} collective-permute-done((f32[1,4096]{1,0:T(1,128)S(1)}, f32[1,4096]{1,0:T(1,128)S(1)}, u32[]{:S(2)}, u32[]{:S(2)}) %collective-permute-start.6) | collective-permute-done | bytes 16416 | tf_op jit(solution)/shard_map/ppermute | solution.py:31
  115.5 3.4 %collective-permute-start.7 = (f32[1,4096]{1,0:T(1,128)S(1)}, f32[1,4096]{1,0:T(1,128)S(1)}, u32[]{:S(2)}, u32[]{:S(2)}) collective-permute-start(f32[1,4096]{1,0:T(1,128)S(1)} %add.76), channel_id=1, source_target_pairs={{0,8},{4,12},{8,0},{12,4},{16,24},{20,28},{24,16},{28,20},{1,9},{5... | collective-permute-start | bytes 49160 | tf_op jit(solution)/shard_map/ppermute | solution.py:31
  118.9 1.6 fusion.4
  122.0 5.0 %collective-permute-start.8 = (f32[1,4096]{1,0:T(1,128)S(1)}, f32[1,4096]{1,0:T(1,128)S(1)}, u32[]{:S(2)}, u32[]{:S(2)}) collective-permute-start(f32[1,4096]{1,0:T(1,128)S(1)} %add.77), channel_id=1, source_target_pairs={{0,16},{4,20},{8,24},{12,28},{16,0},{20,4},{24,8},{28,12},{1,17},{... | collective-permute-start | bytes 49160 | tf_op jit(solution)/shard_map/ppermute | solution.py:31
  127.7 4.0 %collective-permute-done.8 = f32[1,4096]{1,0:T(1,128)S(1)} collective-permute-done((f32[1,4096]{1,0:T(1,128)S(1)}, f32[1,4096]{1,0:T(1,128)S(1)}, u32[]{:S(2)}, u32[]{:S(2)}) %collective-permute-start.8) | collective-permute-done | bytes 16416 | tf_op jit(solution)/shard_map/ppermute | solution.py:31
  132.3 6.1 %reduce-scatter.2.cloned.1.call-done = bf16[32,4096]{1,0:T(8,128)(2,1)} async-done(((bf16[256,4096]{1,0:T(8,128)(2,1)}), bf16[32,4096]{1,0:T(8,128)(2,1)}) %reduce-scatter.2.cloned.1.call-update) | async-done | bytes 262160 | tf_op jit(solution)/shard_map/reduce_scatter | solution.py:99
  139.4 7.9 %collective-permute-start.10 = (bf16[16,4096]{1,0:T(8,128)(2,1)S(1)}, bf16[16,4096]{1,0:T(8,128)(2,1)S(1)}, u32[]{:S(2)}, u32[]{:S(2)}) collective-permute-start(bf16[16,4096]{1,0:T(8,128)(2,1)S(1)} %get-tuple-element.46), channel_id=1, source_target_pairs={{0,482},{2,480},{32,2},{34,0},{64,34},{66,32},{96,66},{98,64},{128... | collective-permute-start | bytes 393224 | tf_op jit(solution)/shard_map/ppermute | solution.py:25
  147.3 4.0 %collective-permute-start.9 = (bf16[16,4096]{1,0:T(8,128)(2,1)S(1)}, bf16[16,4096]{1,0:T(8,128)(2,1)S(1)}, u32[]{:S(2)}, u32[]{:S(2)}) collective-permute-start(bf16[16,4096]{1,0:T(8,128)(2,1)S(1)} %get-tuple-element.45), channel_id=1, source_target_pairs={{0,480},{2,482},{32,0},{34,2},{64,32},{66,34},{96,64},{98,66},{128... | collective-permute-start | bytes 393224 | tf_op jit(solution)/shard_map/ppermute | solution.py:25
  151.9 1.8 %collective-permute-done.10 = bf16[16,4096]{1,0:T(8,128)(2,1)S(1)} collective-permute-done((bf16[16,4096]{1,0:T(8,128)(2,1)S(1)}, bf16[16,4096]{1,0:T(8,128)(2,1)S(1)}, u32[]{:S(2)}, u32[]{:S(2)}) %collective-permute-start.10) | collective-permute-done | bytes 131104 | tf_op jit(solution)/shard_map/ppermute | solution.py:25
  153.7 3.0 %collective-permute-done.9 = bf16[16,4096]{1,0:T(8,128)(2,1)S(1)} collective-permute-done((bf16[16,4096]{1,0:T(8,128)(2,1)S(1)}, bf16[16,4096]{1,0:T(8,128)(2,1)S(1)}, u32[]{:S(2)}, u32[]{:S(2)}) %collective-permute-start.9) | collective-permute-done | bytes 131104 | tf_op jit(solution)/shard_map/ppermute | solution.py:25
  (54 shorter events, 13.9 us)
Async XLA Ops:
  7.2 73.4 %all-gather.2.cloned.1.call-start = ((), (), s32[]{:S(2)}) async-start(), calls=%async_computation.1 | async-start | bytes 8912896 | tf_op jit(solution)/shard_map/all_gather | solution.py:49
  19.8 118.6 %reduce-scatter.2.cloned.1.call-start = ((), (), s32[]{:S(2)}) async-start(), calls=%async_computation.2 | async-start | bytes 2359296 | tf_op jit(solution)/shard_map/reduce_scatter | solution.py:99
  19.8 31.3 %collective-permute-start.2 = (bf16[128,4096]{1,0:T(8,128)(2,1)}, bf16[128,4096]{1,0:T(8,128)(2,1)S(1)}, u32[]{:S(2)}, u32[]{:S(2)}) collective-permute-start(bf16[128,4096]{1,0:T(8,128)(2,1)} %bitcast.68), channel_id=1, source_target_pairs={{0,1},{1,0},{2,3},{3,2},{4,5},{5,4},{6,7},{7,6},{8,9},{9,8},{10,11... | collective-permute-start | bytes 3145736 | tf_op jit(solution)/shard_map/ppermute | solution.py:53
  21.7 17.0 %collective-permute-start.1 = (f32[1,4096]{1,0:T(1,128)}, f32[1,4096]{1,0:T(1,128)S(1)}, u32[]{:S(2)}, u32[]{:S(2)}) collective-permute-start(f32[1,4096]{1,0:T(1,128)} %param.10), channel_id=1, source_target_pairs={{0,480},{2,482},{32,0},{34,2},{64,32},{66,34},{96,64},{98,66},{128... | collective-permute-start | bytes 49160 | tf_op jit(solution)/shard_map/ppermute | solution.py:25
  34.3 16.8 %collective-permute-start = (bf16[32,4096]{1,0:T(8,128)(2,1)S(1)}, bf16[32,4096]{1,0:T(8,128)(2,1)S(1)}, u32[]{:S(2)}, u32[]{:S(2)}) collective-permute-start(bf16[32,4096]{1,0:T(8,128)(2,1)S(1)} %get-tuple-element.49), channel_id=1, source_target_pairs={{0,480},{2,482},{32,0},{34,2},{64,32},{66,34},{96,64},{98,66},{128... | collective-permute-start | bytes 786440 | tf_op jit(solution)/shard_map/ppermute | solution.py:25
  51.1 29.4 %copy-start.2 = (bf16[128,4096]{1,0:T(8,128)(2,1)}, bf16[128,4096]{1,0:T(8,128)(2,1)S(1)}, u32[]{:S(2)}) copy-start(bf16[128,4096]{1,0:T(8,128)(2,1)S(1)} %collective-permute-done.2) | copy-start | bytes 3145732
  86.8 4.8 %copy-start = (bf16[1,128,4096]{2,1,0:T(8,128)(2,1)S(1)}, bf16[1,128,4096]{2,1,0:T(8,128)(2,1)}, u32[]{:S(2)}) copy-start(bf16[1,128,4096]{2,1,0:T(8,128)(2,1)} %param.11) | copy-start | bytes 3145732
  87.4 4.2 %copy-start.3 = (bf16[128,4096]{1,0:T(8,128)(2,1)S(1)}, bf16[128,4096]{1,0:T(8,128)(2,1)}, u32[]{:S(2)}) copy-start(bf16[128,4096]{1,0:T(8,128)(2,1)} %copy-done.2) | copy-start | bytes 3145732
  88.4 3.1 %collective-permute-start.3 = (bf16[256,128]{1,0:T(8,128)(2,1)S(1)}, bf16[256,128]{1,0:T(8,128)(2,1)S(1)}, u32[]{:S(2)}, u32[]{:S(2)}) collective-permute-start(bf16[256,128]{1,0:T(8,128)(2,1)S(1)} %bitcast.81), channel_id=1, source_target_pairs={{0,1},{1,0},{2,3},{3,2},{4,5},{5,4},{6,7},{7,6},{8,9},{9,8},{10,11... | collective-permute-start | bytes 196616 | tf_op jit(solution)/shard_map/ppermute | solution.py:93
  94.0 6.2 %copy-start.1 = (f32[1,4096]{1,0:T(1,128)S(1)}, f32[1,4096]{1,0:T(1,128)}, u32[]{:S(2)}) copy-start(f32[1,4096]{1,0:T(1,128)} %param.10) | copy-start | bytes 49156
  100.3 3.1 %collective-permute-start.4 = (f32[1,4096]{1,0:T(1,128)S(1)}, f32[1,4096]{1,0:T(1,128)S(1)}, u32[]{:S(2)}, u32[]{:S(2)}) collective-permute-start(f32[1,4096]{1,0:T(1,128)S(1)} %div.19), channel_id=1, source_target_pairs={{0,1},{1,0},{2,3},{3,2},{4,5},{5,4},{6,7},{7,6},{8,9},{9,8},{10,11... | collective-permute-start | bytes 49160 | tf_op jit(solution)/shard_map/ppermute | solution.py:31
  103.4 5.6 %collective-permute-start.5 = (f32[1,4096]{1,0:T(1,128)S(1)}, f32[1,4096]{1,0:T(1,128)S(1)}, u32[]{:S(2)}, u32[]{:S(2)}) collective-permute-start(f32[1,4096]{1,0:T(1,128)S(1)} %add.74), channel_id=1, source_target_pairs={{0,2},{2,0},{1,3},{3,1},{4,6},{6,4},{5,7},{7,5},{8,10},{10,8},{9,1... | collective-permute-start | bytes 49160 | tf_op jit(solution)/shard_map/ppermute | solution.py:31
  109.0 6.4 %collective-permute-start.6 = (f32[1,4096]{1,0:T(1,128)S(1)}, f32[1,4096]{1,0:T(1,128)S(1)}, u32[]{:S(2)}, u32[]{:S(2)}) collective-permute-start(f32[1,4096]{1,0:T(1,128)S(1)} %add.75), channel_id=1, source_target_pairs={{0,4},{4,0},{8,12},{12,8},{16,20},{20,16},{24,28},{28,24},{1,5},{5... | collective-permute-start | bytes 49160 | tf_op jit(solution)/shard_map/ppermute | solution.py:31
  115.5 6.5 %collective-permute-start.7 = (f32[1,4096]{1,0:T(1,128)S(1)}, f32[1,4096]{1,0:T(1,128)S(1)}, u32[]{:S(2)}, u32[]{:S(2)}) collective-permute-start(f32[1,4096]{1,0:T(1,128)S(1)} %add.76), channel_id=1, source_target_pairs={{0,8},{4,12},{8,0},{12,4},{16,24},{20,28},{24,16},{28,20},{1,9},{5... | collective-permute-start | bytes 49160 | tf_op jit(solution)/shard_map/ppermute | solution.py:31
  122.0 9.7 %collective-permute-start.8 = (f32[1,4096]{1,0:T(1,128)S(1)}, f32[1,4096]{1,0:T(1,128)S(1)}, u32[]{:S(2)}, u32[]{:S(2)}) collective-permute-start(f32[1,4096]{1,0:T(1,128)S(1)} %add.77), channel_id=1, source_target_pairs={{0,16},{4,20},{8,24},{12,28},{16,0},{20,4},{24,8},{28,12},{1,17},{... | collective-permute-start | bytes 49160 | tf_op jit(solution)/shard_map/ppermute | solution.py:31
  139.4 14.3 %collective-permute-start.10 = (bf16[16,4096]{1,0:T(8,128)(2,1)S(1)}, bf16[16,4096]{1,0:T(8,128)(2,1)S(1)}, u32[]{:S(2)}, u32[]{:S(2)}) collective-permute-start(bf16[16,4096]{1,0:T(8,128)(2,1)S(1)} %get-tuple-element.46), channel_id=1, source_target_pairs={{0,482},{2,480},{32,2},{34,0},{64,34},{66,32},{96,66},{98,64},{128... | collective-permute-start | bytes 393224 | tf_op jit(solution)/shard_map/ppermute | solution.py:25
  147.3 9.3 %collective-permute-start.9 = (bf16[16,4096]{1,0:T(8,128)(2,1)S(1)}, bf16[16,4096]{1,0:T(8,128)(2,1)S(1)}, u32[]{:S(2)}, u32[]{:S(2)}) collective-permute-start(bf16[16,4096]{1,0:T(8,128)(2,1)S(1)} %get-tuple-element.45), channel_id=1, source_target_pairs={{0,480},{2,482},{32,0},{34,2},{64,32},{66,34},{96,64},{98,66},{128... | collective-permute-start | bytes 393224 | tf_op jit(solution)/shard_map/ppermute | solution.py:25
Sparse Core Ops, SparseCore 0:
  19.9 60.5 all-gather.1
  93.8 44.5 reduce-scatter.1

commit v3 on v1

v3 whole, which is shorter than its diff:
```python
import jax
import jax.numpy as jnp
from jax import lax
from jax.sharding import Mesh, PartitionSpec as P

TAPS = 3
EPSILON = 1e-06
Y, Z, CORE = 8, 2, 2
TENSOR = ("y", "z", "core")
SWAP = ((0, 1), (1, 0))
F32, BF16 = jnp.float32, jnp.bfloat16


def contract(left, right, dims):
    return lax.dot_general(left, right, (dims, ((), ())), preferred_element_type=F32)


def along(block, axis, distance):
    devices = lax.axis_size(axis)
    return lax.ppermute(block, axis, [(i, (i + distance) % devices) for i in range(devices)])


def summed_in_pairs(total, steps):
    for axis, apart in steps:
        devices = range(lax.axis_size(axis))
        total = total + lax.ppermute(total, axis, [(i, i ^ apart) for i in devices])
    return total


def own_first(pair, axis):
    return jnp.where(lax.axis_index(axis) == 0, pair, pair[::-1])


def from_own_y(block):
    return lax.dynamic_slice_in_dim(jnp.concatenate([block, block]), lax.axis_index("y"), Y)


def from_first_y(block):
    return lax.dynamic_slice_in_dim(jnp.concatenate([block, block]), (Y - lax.axis_index("y")) % Y, Y)


def gathered(own, mate):
    found = {(0, 0): own, (1, 0): mate}
    ahead, behind = [own, mate], [own, mate]
    half = Y // 2
    for step in range(1, half):
        for z in range(Z):
            ahead[z] = along(ahead[z], "y", -1)
            behind[z] = along(behind[z], "y", 1)
            found[z, step], found[z, Y - step] = ahead[z], behind[z]
    found[0, half] = along(ahead[0], "y", -1)
    found[1, half] = along(behind[1], "y", 1)
    return found


def reduced(share):
    half = Y // 2
    up, down = share[half], share[half + 1]
    for step in range(1, half):
        up = along(up, "y", 1)
        up = (share[half - step].astype(F32) + up.astype(F32)).astype(BF16)
    for step in range(half + 2, Y):
        down = along(down, "y", -1)
        down = (share[step].astype(F32) + down.astype(F32)).astype(BF16)
    return share[0].astype(F32) + along(up, "y", 1).astype(F32) + along(down, "y", -1).astype(F32)


def on_device(x_in, grad_out, gain, w_val, w_out, filt, tail, micro_index):
    x_rows, cot_rows, gain_row = x_in[0], grad_out[0], gain[0]
    val_weight, out_weight = w_val[0], w_out[0]
    filters, tail_rows = filt[0], tail[0]
    has_tail = micro_index[0] > 0
    rows, width = x_rows.shape
    channels = val_weight.shape[0]
    tokens = rows * Y * Z * CORE

    x_float = x_rows.astype(F32)
    inv_rms = lax.rsqrt(jnp.mean(x_float * x_float, axis=-1, keepdims=True) + EPSILON)
    normed = (x_float * inv_rms * gain_row).astype(BF16)

    own = jnp.concatenate([normed, cot_rows], axis=0)
    mate = lax.ppermute(own, "z", SWAP)
    blocks = gathered(own, mate)

    val_core = lax.ppermute(val_weight, "core", SWAP)
    out_core = lax.ppermute(out_weight, "core", SWAP)
    mate_done, val_sent = lax.optimization_barrier((mate, val_weight))
    val_z = lax.ppermute(val_sent, "z", SWAP)
    val_z_core = lax.ppermute(val_z, "core", SWAP)
    weights = jnp.concatenate([val_weight, val_core, out_weight, out_core], axis=0)

    def products(places):
        found = contract(jnp.concatenate([blocks[p] for p in places], axis=0), weights, ((1,), (1,)))
        found = found.reshape(len(places), 2, rows, 2, CORE, channels)
        return {p: (found[i, 0, :, 0], found[i, 1, :, 1]) for i, p in enumerate(places)}

    half = Y // 2
    early = [(z, y) for z in range(Z) for y in range(Y) if min(y, Y - y) < half - 1]
    late = [(z, y) for z in range(Z) for y in range(Y) if min(y, Y - y) >= half - 1]
    by_place = {**products(early), **products(late)}
    found = jnp.stack(
        [jnp.stack([jnp.stack([by_place[z, y][k] for y in range(Y)]) for z in range(Z)]) for k in range(2)]
    )
    kept, given = found[..., 0, :], found[..., 1, :]
    taken = lax.ppermute(given, "core", SWAP)
    found = own_first(jnp.stack([kept, taken]), "core")
    found = own_first(found.transpose(2, 0, 1, 3, 4, 5), "z")
    found = from_first_y(found.transpose(3, 0, 1, 2, 4, 5))
    found = found.transpose(3, 0, 1, 2, 4, 5).reshape(2, tokens, channels)
    values, grad_gated = found[0].astype(BF16), found[1]

    lead_rows = jnp.where(has_tail, tail_rows, jnp.zeros_like(tail_rows))
    extended = jnp.concatenate([lead_rows, values], axis=0).astype(F32)
    conv_out = filters[0] * extended[TAPS - 1 : TAPS - 1 + tokens]
    for tap in range(1, TAPS):
        conv_out = conv_out + filters[tap] * extended[TAPS - 1 - tap : TAPS - 1 - tap + tokens]
    gate_sig = jax.nn.sigmoid(conv_out)
    gated = (conv_out * gate_sig).astype(BF16)
    grad_conv = grad_gated * gate_sig * (1.0 + conv_out * (1.0 - gate_sig))
    grad_filter = jnp.stack(
        [
            jnp.sum(grad_conv * extended[TAPS - 1 - tap : TAPS - 1 - tap + tokens], axis=0)
            for tap in range(TAPS)
        ]
    )
    padded = jnp.pad(grad_conv, ((TAPS - 1, TAPS - 1), (0, 0)))
    grad_ext = filters[0] * padded[0 : tokens + TAPS - 1]
    for tap in range(1, TAPS):
        grad_ext = grad_ext + filters[tap] * padded[tap : tap + tokens + TAPS - 1]
    grad_values = grad_ext[TAPS - 1 :].astype(BF16)
    grad_tail = jnp.where(has_tail, grad_ext[: TAPS - 1], jnp.zeros_like(grad_ext[: TAPS - 1]))

    factors = jnp.concatenate([grad_values, gated], axis=-1).reshape(Y, Z, CORE, rows, 2 * channels)
    factors = from_own_y(factors).transpose(2, 1, 0, 3, 4)
    factors = own_first(factors, "core").transpose(1, 0, 2, 3, 4)
    factors = own_first(factors, "z").transpose(1, 0, 2, 3, 4)
    taken = lax.ppermute(factors[1], "core", SWAP)
    kept = factors[0]
    of_values = jnp.concatenate([kept[..., :channels], taken[..., :channels]], axis=-1)
    of_gated = jnp.concatenate([kept[..., channels:], taken[..., channels:]], axis=-1)

    taken = lax.ppermute(of_values[1], "z", SWAP)
    share = contract(
        jnp.concatenate([of_values[0], taken], axis=-1).reshape(Y * rows, 2 * CORE * channels),
        jnp.concatenate([val_weight, val_core, val_z, val_z_core], axis=0),
        ((1,), (0,)),
    )
    grad_normed = reduced(share.astype(BF16).reshape(Y, rows, width))

    zeros = jnp.zeros_like(of_values)
    sided = jnp.stack(
        [jnp.concatenate([of_values, zeros], axis=-1), jnp.concatenate([zeros, of_gated], axis=-1)], axis=2
    ).reshape(2 * tokens // CORE, 2 * CORE * channels)
    every = jnp.concatenate([blocks[z, y] for z in range(Z) for y in range(Y)], axis=0)
    grad_weights = contract(sided, every, ((0,), (0,))).reshape(2, CORE, channels, width)
    gain_term = jnp.sum(
        grad_weights[0] * jnp.stack([val_weight, val_core]).astype(F32), axis=(0, 1)
    ) / gain_row
    grad_gain = summed_in_pairs(gain_term[None], (("core", 1), ("z", 1), ("y", 1), ("y", 2), ("y", 4)))
    grad_weights = grad_weights[:, 0] + lax.ppermute(grad_weights[:, 1].astype(BF16), "core", SWAP).astype(F32)

    scaled = gain_row * grad_normed
    grad_local = (
        cot_rows.astype(F32)
        + inv_rms * scaled
        - x_float * inv_rms**3 * jnp.mean(scaled * x_float, axis=-1, keepdims=True)
    )
    received = along(grad_local.astype(BF16), "section", -1)
    return (
        received[None],
        grad_weights[0].astype(BF16)[None],
        grad_weights[1].astype(BF16)[None],
        grad_filter[None],
        grad_tail[None],
        grad_gain,
    )


def solution(mesh):
    sections = mesh.shape["section"]
    split = Mesh(mesh.devices.reshape(sections, Y, Z, CORE), ("section", *TENSOR))
    by_rows = P("section", TENSOR, None)
    by_columns = P("section", None, TENSOR)
    whole = P("section", None)
    return jax.shard_map(
        on_device,
        mesh=split,
        in_specs=(by_rows, by_rows, whole, by_rows, by_rows, by_columns, by_columns, P("section")),
        out_specs=(by_rows, by_rows, by_rows, by_columns, by_columns, whole),
        check_vma=False,
    )
```

time: 175 us -> 202 us (1.15)
  the two profiles are of different devices: /device:TPU:24 before, /device:TPU:16 now
where the time goes in v3:
time: 202 us; the launch traced here: 201 us
  starting transfers between devices  127 us (63%)
  waiting for transfers between devices  25.9 us (13%)
  local copies, waits for them, and re-layouts  22.8 us (11%)
  matrix products  12.9 us (6%)
  other arithmetic  9.94 us (5%)
  between operations  2.18 us (1%)
    ppermute x22, starting transfers between devices, along(): lax.ppermute(block, axis, [(i, (i + distance) % devices) for i in range(d...  84.6 us
    ppermute x5, starting transfers between devices, summed_in_pairs(): total = total + lax.ppermute(total, axis, [(i, i ^ apart) for i in devices])  20.7 us
    unnamed x47, local copies, waits for them, and re-layouts  18.7 us
    dot_general x4, matrix products, contract(): lax.dot_general(left, right, (dims, ((), ())), preferred_element_type=F32)  12.9 us
    ppermute x22, waiting for transfers between devices, along(): lax.ppermute(block, axis, [(i, (i + distance) % devices) for i in range(d...  10.2 us
    ppermute x5, waiting for transfers between devices, summed_in_pairs(): total = total + lax.ppermute(total, axis, [(i, i ^ apart) for i in devices])  9.07 us
    ppermute x1, starting transfers between devices, on_device(): mate = lax.ppermute(own, 'z', SWAP)  4.28 us
  transfers between devices with their start and end apart: 36, of which 13 were waited for; matrix products, arithmetic and copies ran while one was open for 18% of the time, Pallas kernels for 0%

profile of v3, /device:TPU:16, one launch (start us, length us, event | category | flops | bytes accessed | tf_op | source)
XLA Modules:
  0.0 201.2 jit_solution(14463476965092105352)
XLA Ops:
  6.8 3.5 %collective-permute-start.2 = (bf16[32,4096]{1,0:T(8,128)(2,1)S(1)}, bf16[32,4096]{1,0:T(8,128)(2,1)S(1)}, u32[]{:S(2)}, u32[]{:S(2)}) collective-permute-start(bf16[32,4096]{1,0:T(8,128)(2,1)S(1)} %pad_maximum_fusion.9), channel_id=1, source_target_pairs={{0,4},{4,8},{8,12},{12,16},{16,20},{20,24},{24,28},{28,0},{1,5},{5... | collective-permute-start | bytes 786440 | tf_op jit(solution)/shard_map/ppermute | solution.py:20
  10.2 4.3 %collective-permute-start.4 = (bf16[32,4096]{1,0:T(8,128)(2,1)S(1)}, bf16[32,4096]{1,0:T(8,128)(2,1)S(1)}, u32[]{:S(2)}, u32[]{:S(2)}) collective-permute-start(bf16[32,4096]{1,0:T(8,128)(2,1)S(1)} %pad_maximum_fusion.9), channel_id=1, source_target_pairs={{0,2},{2,0},{1,3},{3,1},{4,6},{6,4},{5,7},{7,5},{8,10},{10,8},{9,1... | collective-permute-start | bytes 786440 | tf_op jit(solution)/shard_map/ppermute | solution.py:82
  20.3 4.4 %collective-permute-start.5 = (bf16[32,4096]{1,0:T(8,128)(2,1)S(1)}, bf16[32,4096]{1,0:T(8,128)(2,1)S(1)}, u32[]{:S(2)}, u32[]{:S(2)}) collective-permute-start(bf16[32,4096]{1,0:T(8,128)(2,1)S(1)} %collective-permute-done.4), channel_id=1, source_target_pairs={{0,28},{4,0},{8,4},{12,8},{16,12},{20,16},{24,20},{28,24},{1,29},{... | collective-permute-start | bytes 786440 | tf_op jit(solution)/shard_map/ppermute | solution.py:20
  26.9 3.6 %collective-permute-start.1 = (bf16[32,4096]{1,0:T(8,128)(2,1)S(1)}, bf16[32,4096]{1,0:T(8,128)(2,1)S(1)}, u32[]{:S(2)}, u32[]{:S(2)}) collective-permute-start(bf16[32,4096]{1,0:T(8,128)(2,1)S(1)} %collective-permute-done), channel_id=1, source_target_pairs={{0,28},{4,0},{8,4},{12,8},{16,12},{20,16},{24,20},{28,24},{1,29},{... | collective-permute-start | bytes 786440 | tf_op jit(solution)/shard_map/ppermute | solution.py:20
  30.5 3.4 %collective-permute-start.3 = (bf16[32,4096]{1,0:T(8,128)(2,1)S(1)}, bf16[32,4096]{1,0:T(8,128)(2,1)S(1)}, u32[]{:S(2)}, u32[]{:S(2)}) collective-permute-start(bf16[32,4096]{1,0:T(8,128)(2,1)S(1)} %collective-permute-done.2), channel_id=1, source_target_pairs={{0,4},{4,8},{8,12},{12,16},{16,20},{20,24},{24,28},{28,0},{1,5},{5... | collective-permute-start | bytes 786440 | tf_op jit(solution)/shard_map/ppermute | solution.py:20
  38.8 4.9 %collective-permute-start.8 = (bf16[32,4096]{1,0:T(8,128)(2,1)S(1)}, bf16[32,4096]{1,0:T(8,128)(2,1)S(1)}, u32[]{:S(2)}, u32[]{:S(2)}) collective-permute-start(bf16[32,4096]{1,0:T(8,128)(2,1)S(1)} %collective-permute-done.7), channel_id=1, source_target_pairs={{0,4},{4,8},{8,12},{12,16},{16,20},{20,24},{24,28},{28,0},{1,5},{5... | collective-permute-start | bytes 786440 | tf_op jit(solution)/shard_map/ppermute | solution.py:20
  50.7 5.1 %collective-permute-start.13 = (bf16[32,4096]{1,0:T(8,128)(2,1)S(1)}, bf16[32,4096]{1,0:T(8,128)(2,1)S(1)}, u32[]{:S(2)}, u32[]{:S(2)}) collective-permute-start(bf16[32,4096]{1,0:T(8,128)(2,1)S(1)} %collective-permute-done.3), channel_id=1, source_target_pairs={{0,4},{4,8},{8,12},{12,16},{16,20},{20,24},{24,28},{28,0},{1,5},{5... | collective-permute-start | bytes 786440 | tf_op jit(solution)/shard_map/ppermute | solution.py:20
  57.8 5.1 %collective-permute-start.15 = (bf16[32,4096]{1,0:T(8,128)(2,1)S(1)}, bf16[32,4096]{1,0:T(8,128)(2,1)S(1)}, u32[]{:S(2)}, u32[]{:S(2)}) collective-permute-start(bf16[32,4096]{1,0:T(8,128)(2,1)S(1)} %collective-permute-done.8), channel_id=1, source_target_pairs={{0,4},{4,8},{8,12},{12,16},{16,20},{20,24},{24,28},{28,0},{1,5},{5... | collective-permute-start | bytes 786440 | tf_op jit(solution)/shard_map/ppermute | solution.py:20
  63.7 3.4 %collective-permute-start.20 = (bf16[128,4096]{1,0:T(8,128)(2,1)S(1)}, bf16[128,4096]{1,0:T(8,128)(2,1)}, u32[]{:S(2)}, u32[]{:S(2)}) collective-permute-start(bf16[128,4096]{1,0:T(8,128)(2,1)S(1)} %bitcast.294), channel_id=1, source_target_pairs={{0,2},{2,0},{1,3},{3,1},{4,6},{6,4},{5,7},{7,5},{8,10},{10,8},{9,1... | collective-permute-start | bytes 3145736 | tf_op jit(solution)/shard_map/ppermute | solution.py:88
  67.6 3.3 %collective-permute-start.14 = (bf16[32,4096]{1,0:T(8,128)(2,1)S(1)}, bf16[32,4096]{1,0:T(8,128)(2,1)S(1)}, u32[]{:S(2)}, u32[]{:S(2)}) collective-permute-start(bf16[32,4096]{1,0:T(8,128)(2,1)S(1)} %collective-permute-done.6), channel_id=1, source_target_pairs={{0,28},{4,0},{8,4},{12,8},{16,12},{20,16},{24,20},{28,24},{1,29},{... | collective-permute-start | bytes 786440 | tf_op jit(solution)/shard_map/ppermute | solution.py:20
  70.9 3.5 %collective-permute-start.16 = (bf16[32,4096]{1,0:T(8,128)(2,1)S(1)}, bf16[32,4096]{1,0:T(8,128)(2,1)S(1)}, u32[]{:S(2)}, u32[]{:S(2)}) collective-permute-start(bf16[32,4096]{1,0:T(8,128)(2,1)S(1)} %collective-permute-done.15), channel_id=1, source_target_pairs={{0,4},{4,8},{8,12},{12,16},{16,20},{20,24},{24,28},{28,0},{1,5},{5... | collective-permute-start | bytes 786440 | tf_op jit(solution)/shard_map/ppermute | solution.py:20
  88.0 4.8 %fusion.8 = f32[192,512]{1,0:T(8,128)S(1)} fusion(bf16[192,4096]{1,0:T(8,128)(2,1)} %copy-done.4, bf16[128,4096]{1,0:T(8,128)(2,1)} %copy-done.7, bf16[128,4096]{1,0:T(8,128)(2,1)} %bitcast.317, bf16[128,4096]{1,0:T(8,128)(2,1)S(1)} %collective-permute-done.9, bf16[128,4096]{1,0:T(8,128)(2,1)S(1)} %bitcast.296), kind=kOutput, calls=%fused_computation.19 | convolution fusion | flops 822083584 | bytes 6160384 | tf_op jit(solution)/shard_map/dot_general | solution.py:15
  110.6 3.8 %collective-permute-done.19 = bf16[8,16,256]{2,1,0:T(8,128)(2,1)S(1)} collective-permute-done((bf16[8,16,256]{2,1,0:T(8,128)(2,1)S(1)}, bf16[8,16,256]{2,1,0:T(8,128)(2,1)S(1)}, u32[]{:S(2)}, u32[]{:S(2)}) %collective-permute-start.19) | collective-permute-done | bytes 65568 | tf_op jit(solution)/shard_map/ppermute | solution.py:142
  116.3 3.4 %collective-permute-start.22 = (bf16[16,4096]{1,0:T(8,128)(2,1)S(1)}, bf16[16,4096]{1,0:T(8,128)(2,1)S(1)}, u32[]{:S(2)}, u32[]{:S(2)}) collective-permute-start(bf16[16,4096]{1,0:T(8,128)(2,1)S(1)} %get-tuple-element.37), channel_id=1, source_target_pairs={{0,4},{4,8},{8,12},{12,16},{16,20},{20,24},{24,28},{28,0},{1,5},{5... | collective-permute-start | bytes 393224 | tf_op jit(solution)/shard_map/ppermute | solution.py:20
  123.2 4.3 %collective-permute-start.23 = (bf16[16,4096]{1,0:T(8,128)(2,1)S(1)}, bf16[16,4096]{1,0:T(8,128)(2,1)S(1)}, u32[]{:S(2)}, u32[]{:S(2)}) collective-permute-start(bf16[16,4096]{1,0:T(8,128)(2,1)S(1)} %add_convert_fusion.4), channel_id=1, source_target_pairs={{0,4},{4,8},{8,12},{12,16},{16,20},{20,24},{24,28},{28,0},{1,5},{5... | collective-permute-start | bytes 393224 | tf_op jit(solution)/shard_map/ppermute | solution.py:20
  130.5 5.3 %collective-permute-start.24 = (bf16[16,4096]{1,0:T(8,128)(2,1)S(1)}, bf16[16,4096]{1,0:T(8,128)(2,1)S(1)}, u32[]{:S(2)}, u32[]{:S(2)}) collective-permute-start(bf16[16,4096]{1,0:T(8,128)(2,1)S(1)} %add_convert_fusion.3), channel_id=1, source_target_pairs={{0,4},{4,8},{8,12},{12,16},{16,20},{20,24},{24,28},{28,0},{1,5},{5... | collective-permute-start | bytes 393224 | tf_op jit(solution)/shard_map/ppermute | solution.py:20
  135.8 4.7 %fusion.43 = f32[512,4096]{1,0:T(8,128)S(1)} fusion(bf16[512,512]{1,0:T(8,128)(2,1)S(1)} %bitcast.290, bf16[512,4096]{1,0:T(8,128)(2,1)} %get-tuple-element.68), kind=kOutput, calls=%fused_computation.200 | convolution fusion | flops 2147483648 | bytes 13107200 | tf_op jit(solution)/shard_map/dot_general | solution.py:15
  146.1 4.3 %collective-permute-start.25 = (bf16[16,4096]{1,0:T(8,128)(2,1)S(1)}, bf16[16,4096]{1,0:T(8,128)(2,1)S(1)}, u32[]{:S(2)}, u32[]{:S(2)}) collective-permute-start(bf16[16,4096]{1,0:T(8,128)(2,1)S(1)} %get-tuple-element.35), channel_id=1, source_target_pairs={{0,4},{4,8},{8,12},{12,16},{16,20},{20,24},{24,28},{28,0},{1,5},{5... | collective-permute-start | bytes 393224 | tf_op jit(solution)/shard_map/ppermute | solution.py:20
  157.2 3.5 %collective-permute-start.32 = (f32[1,4096]{1,0:T(1,128)S(1)}, f32[1,4096]{1,0:T(1,128)S(1)}, u32[]{:S(2)}, u32[]{:S(2)}) collective-permute-start(f32[1,4096]{1,0:T(1,128)S(1)} %add.102), channel_id=1, source_target_pairs={{0,2},{2,0},{1,3},{3,1},{4,6},{6,4},{5,7},{7,5},{8,10},{10,8},{9,1... | collective-permute-start | bytes 49160 | tf_op jit(solution)/shard_map/ppermute | solution.py:26
  162.8 4.3 %collective-permute-start.33 = (f32[1,4096]{1,0:T(1,128)S(1)}, f32[1,4096]{1,0:T(1,128)S(1)}, u32[]{:S(2)}, u32[]{:S(2)}) collective-permute-start(f32[1,4096]{1,0:T(1,128)S(1)} %add.103), channel_id=1, source_target_pairs={{0,4},{4,0},{8,12},{12,8},{16,20},{20,16},{24,28},{28,24},{1,5},{5... | collective-permute-start | bytes 49160 | tf_op jit(solution)/shard_map/ppermute | solution.py:26
  168.9 6.1 %collective-permute-start.34 = (f32[1,4096]{1,0:T(1,128)S(1)}, f32[1,4096]{1,0:T(1,128)S(1)}, u32[]{:S(2)}, u32[]{:S(2)}) collective-permute-start(f32[1,4096]{1,0:T(1,128)S(1)} %add.104), channel_id=1, source_target_pairs={{0,8},{4,12},{8,0},{12,4},{16,24},{20,28},{24,16},{28,20},{1,9},{5... | collective-permute-start | bytes 49160 | tf_op jit(solution)/shard_map/ppermute | solution.py:26
  175.4 12.3 %collective-permute-start.29 = (bf16[16,4096]{1,0:T(8,128)(2,1)S(1)}, bf16[16,4096]{1,0:T(8,128)(2,1)S(1)}, u32[]{:S(2)}, u32[]{:S(2)}) collective-permute-start(bf16[16,4096]{1,0:T(8,128)(2,1)S(1)} %fusion.21), channel_id=1, source_target_pairs={{0,480},{32,0},{64,32},{96,64},{128,96},{160,128},{192,160},{224,1... | collective-permute-start | bytes 393224 | tf_op jit(solution)/shard_map/ppermute | solution.py:20
  188.2 4.7 %collective-permute-start.35 = (f32[1,4096]{1,0:T(1,128)S(1)}, f32[1,4096]{1,0:T(1,128)S(1)}, u32[]{:S(2)}, u32[]{:S(2)}) collective-permute-start(f32[1,4096]{1,0:T(1,128)S(1)} %add.105), channel_id=1, source_target_pairs={{0,16},{4,20},{8,24},{12,28},{16,0},{20,4},{24,8},{28,12},{1,17},{... | collective-permute-start | bytes 49160 | tf_op jit(solution)/shard_map/ppermute | solution.py:26
  193.5 4.3 %collective-permute-done.35 = f32[1,4096]{1,0:T(1,128)S(1)} collective-permute-done((f32[1,4096]{1,0:T(1,128)S(1)}, f32[1,4096]{1,0:T(1,128)S(1)}, u32[]{:S(2)}, u32[]{:S(2)}) %collective-permute-start.35) | collective-permute-done | bytes 16416 | tf_op jit(solution)/shard_map/ppermute | solution.py:26
  (157 shorter events, 88.9 us)
Async XLA Ops:
  4.4 22.5 %collective-permute-start = (bf16[32,4096]{1,0:T(8,128)(2,1)S(1)}, bf16[32,4096]{1,0:T(8,128)(2,1)S(1)}, u32[]{:S(2)}, u32[]{:S(2)}) collective-permute-start(bf16[32,4096]{1,0:T(8,128)(2,1)S(1)} %pad_maximum_fusion.9), channel_id=1, source_target_pairs={{0,28},{4,0},{8,4},{12,8},{16,12},{20,16},{24,20},{28,24},{1,29},{... | collective-permute-start | bytes 786440 | tf_op jit(solution)/shard_map/ppermute | solution.py:20
  6.8 23.8 %collective-permute-start.2 = (bf16[32,4096]{1,0:T(8,128)(2,1)S(1)}, bf16[32,4096]{1,0:T(8,128)(2,1)S(1)}, u32[]{:S(2)}, u32[]{:S(2)}) collective-permute-start(bf16[32,4096]{1,0:T(8,128)(2,1)S(1)} %pad_maximum_fusion.9), channel_id=1, source_target_pairs={{0,4},{4,8},{8,12},{12,16},{16,20},{20,24},{24,28},{28,0},{1,5},{5... | collective-permute-start | bytes 786440 | tf_op jit(solution)/shard_map/ppermute | solution.py:20
  10.2 10.0 %collective-permute-start.4 = (bf16[32,4096]{1,0:T(8,128)(2,1)S(1)}, bf16[32,4096]{1,0:T(8,128)(2,1)S(1)}, u32[]{:S(2)}, u32[]{:S(2)}) collective-permute-start(bf16[32,4096]{1,0:T(8,128)(2,1)S(1)} %pad_maximum_fusion.9), channel_id=1, source_target_pairs={{0,2},{2,0},{1,3},{3,1},{4,6},{6,4},{5,7},{7,5},{8,10},{10,8},{9,1... | collective-permute-start | bytes 786440 | tf_op jit(solution)/shard_map/ppermute | solution.py:82
  14.5 69.8 %collective-permute-start.9 = (bf16[128,4096]{1,0:T(8,128)(2,1)}, bf16[128,4096]{1,0:T(8,128)(2,1)S(1)}, u32[]{:S(2)}, u32[]{:S(2)}) collective-permute-start(bf16[128,4096]{1,0:T(8,128)(2,1)} %bitcast.293), channel_id=1, source_target_pairs={{0,1},{1,0},{2,3},{3,2},{4,5},{5,4},{6,7},{7,6},{8,9},{9,8},{10,11... | collective-permute-start | bytes 3145736 | tf_op jit(solution)/shard_map/ppermute | solution.py:85
  20.3 30.4 %collective-permute-start.5 = (bf16[32,4096]{1,0:T(8,128)(2,1)S(1)}, bf16[32,4096]{1,0:T(8,128)(2,1)S(1)}, u32[]{:S(2)}, u32[]{:S(2)}) collective-permute-start(bf16[32,4096]{1,0:T(8,128)(2,1)S(1)} %collective-permute-done.4), channel_id=1, source_target_pairs={{0,28},{4,0},{8,4},{12,8},{16,12},{20,16},{24,20},{28,24},{1,29},{... | collective-permute-start | bytes 786440 | tf_op jit(solution)/shard_map/ppermute | solution.py:20
  24.7 14.2 %collective-permute-start.7 = (bf16[32,4096]{1,0:T(8,128)(2,1)S(1)}, bf16[32,4096]{1,0:T(8,128)(2,1)S(1)}, u32[]{:S(2)}, u32[]{:S(2)}) collective-permute-start(bf16[32,4096]{1,0:T(8,128)(2,1)S(1)} %collective-permute-done.4), channel_id=1, source_target_pairs={{0,4},{4,8},{8,12},{12,16},{16,20},{20,24},{24,28},{28,0},{1,5},{5... | collective-permute-start | bytes 786440 | tf_op jit(solution)/shard_map/ppermute | solution.py:20
  30.5 18.2 %collective-permute-start.3 = (bf16[32,4096]{1,0:T(8,128)(2,1)S(1)}, bf16[32,4096]{1,0:T(8,128)(2,1)S(1)}, u32[]{:S(2)}, u32[]{:S(2)}) collective-permute-start(bf16[32,4096]{1,0:T(8,128)(2,1)S(1)} %collective-permute-done.2), channel_id=1, source_target_pairs={{0,4},{4,8},{8,12},{12,16},{16,20},{20,24},{24,28},{28,0},{1,5},{5... | collective-permute-start | bytes 786440 | tf_op jit(solution)/shard_map/ppermute | solution.py:20
  38.8 17.0 %collective-permute-start.8 = (bf16[32,4096]{1,0:T(8,128)(2,1)S(1)}, bf16[32,4096]{1,0:T(8,128)(2,1)S(1)}, u32[]{:S(2)}, u32[]{:S(2)}) collective-permute-start(bf16[32,4096]{1,0:T(8,128)(2,1)S(1)} %collective-permute-done.7), channel_id=1, source_target_pairs={{0,4},{4,8},{8,12},{12,16},{16,20},{20,24},{24,28},{28,0},{1,5},{5... | collective-permute-start | bytes 786440 | tf_op jit(solution)/shard_map/ppermute | solution.py:20
  46.1 11.7 %collective-permute-start.12 = (bf16[32,4096]{1,0:T(8,128)(2,1)S(1)}, bf16[32,4096]{1,0:T(8,128)(2,1)S(1)}, u32[]{:S(2)}, u32[]{:S(2)}) collective-permute-start(bf16[32,4096]{1,0:T(8,128)(2,1)S(1)} %collective-permute-done.11), channel_id=1, source_target_pairs={{0,28},{4,0},{8,4},{12,8},{16,12},{20,16},{24,20},{28,24},{1,29},{... | collective-permute-start | bytes 786440 | tf_op jit(solution)/shard_map/ppermute | solution.py:20
  48.8 35.6 %collective-permute-start.10 = (bf16[128,4096]{1,0:T(8,128)(2,1)}, bf16[128,4096]{1,0:T(8,128)(2,1)S(1)}, u32[]{:S(2)}, u32[]{:S(2)}) collective-permute-start(bf16[128,4096]{1,0:T(8,128)(2,1)} %bitcast.316), channel_id=1, source_target_pairs={{0,1},{1,0},{2,3},{3,2},{4,5},{5,4},{6,7},{7,6},{8,9},{9,8},{10,11... | collective-permute-start | bytes 3145736 | tf_op jit(solution)/shard_map/ppermute | solution.py:86
  50.7 13.0 %collective-permute-start.13 = (bf16[32,4096]{1,0:T(8,128)(2,1)S(1)}, bf16[32,4096]{1,0:T(8,128)(2,1)S(1)}, u32[]{:S(2)}, u32[]{:S(2)}) collective-permute-start(bf16[32,4096]{1,0:T(8,128)(2,1)S(1)} %collective-permute-done.3), channel_id=1, source_target_pairs={{0,4},{4,8},{8,12},{12,16},{16,20},{20,24},{24,28},{28,0},{1,5},{5... | collective-permute-start | bytes 786440 | tf_op jit(solution)/shard_map/ppermute | solution.py:20
  55.8 11.8 %collective-permute-start.6 = (bf16[32,4096]{1,0:T(8,128)(2,1)S(1)}, bf16[32,4096]{1,0:T(8,128)(2,1)S(1)}, u32[]{:S(2)}, u32[]{:S(2)}) collective-permute-start(bf16[32,4096]{1,0:T(8,128)(2,1)S(1)} %collective-permute-done.5), channel_id=1, source_target_pairs={{0,28},{4,0},{8,4},{12,8},{16,12},{20,16},{24,20},{28,24},{1,29},{... | collective-permute-start | bytes 786440 | tf_op jit(solution)/shard_map/ppermute | solution.py:20
  57.8 13.2 %collective-permute-start.15 = (bf16[32,4096]{1,0:T(8,128)(2,1)S(1)}, bf16[32,4096]{1,0:T(8,128)(2,1)S(1)}, u32[]{:S(2)}, u32[]{:S(2)}) collective-permute-start(bf16[32,4096]{1,0:T(8,128)(2,1)S(1)} %collective-permute-done.8), channel_id=1, source_target_pairs={{0,4},{4,8},{8,12},{12,16},{16,20},{20,24},{24,28},{28,0},{1,5},{5... | collective-permute-start | bytes 786440 | tf_op jit(solution)/shard_map/ppermute | solution.py:20
  63.7 37.6 %collective-permute-start.20 = (bf16[128,4096]{1,0:T(8,128)(2,1)S(1)}, bf16[128,4096]{1,0:T(8,128)(2,1)}, u32[]{:S(2)}, u32[]{:S(2)}) collective-permute-start(bf16[128,4096]{1,0:T(8,128)(2,1)S(1)} %bitcast.294), channel_id=1, source_target_pairs={{0,2},{2,0},{1,3},{3,1},{4,6},{6,4},{5,7},{7,5},{8,10},{10,8},{9,1... | collective-permute-start | bytes 3145736 | tf_op jit(solution)/shard_map/ppermute | solution.py:88
  67.6 11.2 %collective-permute-start.14 = (bf16[32,4096]{1,0:T(8,128)(2,1)S(1)}, bf16[32,4096]{1,0:T(8,128)(2,1)S(1)}, u32[]{:S(2)}, u32[]{:S(2)}) collective-permute-start(bf16[32,4096]{1,0:T(8,128)(2,1)S(1)} %collective-permute-done.6), channel_id=1, source_target_pairs={{0,28},{4,0},{8,4},{12,8},{16,12},{20,16},{24,20},{28,24},{1,29},{... | collective-permute-start | bytes 786440 | tf_op jit(solution)/shard_map/ppermute | solution.py:20
  70.9 10.4 %collective-permute-start.16 = (bf16[32,4096]{1,0:T(8,128)(2,1)S(1)}, bf16[32,4096]{1,0:T(8,128)(2,1)S(1)}, u32[]{:S(2)}, u32[]{:S(2)}) collective-permute-start(bf16[32,4096]{1,0:T(8,128)(2,1)S(1)} %collective-permute-done.15), channel_id=1, source_target_pairs={{0,4},{4,8},{8,12},{12,16},{16,20},{20,24},{24,28},{28,0},{1,5},{5... | collective-permute-start | bytes 786440 | tf_op jit(solution)/shard_map/ppermute | solution.py:20
  101.3 13.1 %collective-permute-start.21 = (bf16[128,4096]{1,0:T(8,128)(2,1)}, bf16[128,4096]{1,0:T(8,128)(2,1)S(1)}, u32[]{:S(2)}, u32[]{:S(2)}) collective-permute-start(bf16[128,4096]{1,0:T(8,128)(2,1)} %collective-permute-done.20), channel_id=1, source_target_pairs={{0,1},{1,0},{2,3},{3,2},{4,5},{5,4},{6,7},{7,6},{8,9},{9,8},{10,11... | collective-permute-start | bytes 3145736 | tf_op jit(solution)/shard_map/ppermute | solution.py:89
  127.7 12.8 %collective-permute-start.26 = (bf16[16,4096]{1,0:T(8,128)(2,1)S(1)}, bf16[16,4096]{1,0:T(8,128)(2,1)S(1)}, u32[]{:S(2)}, u32[]{:S(2)}) collective-permute-start(bf16[16,4096]{1,0:T(8,128)(2,1)S(1)} %get-tuple-element.38), channel_id=1, source_target_pairs={{0,28},{4,0},{8,4},{12,8},{16,12},{20,16},{24,20},{28,24},{1,29},{... | collective-permute-start | bytes 393224 | tf_op jit(solution)/shard_map/ppermute | solution.py:20
  130.5 10.0 %collective-permute-start.24 = (bf16[16,4096]{1,0:T(8,128)(2,1)S(1)}, bf16[16,4096]{1,0:T(8,128)(2,1)S(1)}, u32[]{:S(2)}, u32[]{:S(2)}) collective-permute-start(bf16[16,4096]{1,0:T(8,128)(2,1)S(1)} %add_convert_fusion.3), channel_id=1, source_target_pairs={{0,4},{4,8},{8,12},{12,16},{16,20},{20,24},{24,28},{28,0},{1,5},{5... | collective-permute-start | bytes 393224 | tf_op jit(solution)/shard_map/ppermute | solution.py:20
  144.1 54.3 %collective-permute-start.30 = (bf16[2,128,4096]{2,1,0:T(8,128)(2,1)S(1)}, bf16[2,128,4096]{2,1,0:T(8,128)(2,1)S(1)}, u32[]{:S(2)}, u32[]{:S(2)}) collective-permute-start(bf16[2,128,4096]{2,1,0:T(8,128)(2,1)S(1)} %fusion.7), channel_id=1, source_target_pairs={{0,1},{1,0},{2,3},{3,2},{4,5},{5,4},{6,7},{7,6},{8,9},{9,8},{10,11... | collective-permute-start | bytes 6291464 | tf_op jit(solution)/shard_map/ppermute | solution.py:160
  146.1 28.9 %collective-permute-start.25 = (bf16[16,4096]{1,0:T(8,128)(2,1)S(1)}, bf16[16,4096]{1,0:T(8,128)(2,1)S(1)}, u32[]{:S(2)}, u32[]{:S(2)}) collective-permute-start(bf16[16,4096]{1,0:T(8,128)(2,1)S(1)} %get-tuple-element.35), channel_id=1, source_target_pairs={{0,4},{4,8},{8,12},{12,16},{16,20},{20,24},{24,28},{28,0},{1,5},{5... | collective-permute-start | bytes 393224 | tf_op jit(solution)/shard_map/ppermute | solution.py:20
  150.5 24.5 %collective-permute-start.28 = (bf16[16,4096]{1,0:T(8,128)(2,1)S(1)}, bf16[16,4096]{1,0:T(8,128)(2,1)S(1)}, u32[]{:S(2)}, u32[]{:S(2)}) collective-permute-start(bf16[16,4096]{1,0:T(8,128)(2,1)S(1)} %add_convert_fusion), channel_id=1, source_target_pairs={{0,28},{4,0},{8,4},{12,8},{16,12},{20,16},{24,20},{28,24},{1,29},{... | collective-permute-start | bytes 393224 | tf_op jit(solution)/shard_map/ppermute | solution.py:20
  168.9 19.3 %collective-permute-start.34 = (f32[1,4096]{1,0:T(1,128)S(1)}, f32[1,4096]{1,0:T(1,128)S(1)}, u32[]{:S(2)}, u32[]{:S(2)}) collective-permute-start(f32[1,4096]{1,0:T(1,128)S(1)} %add.104), channel_id=1, source_target_pairs={{0,8},{4,12},{8,0},{12,4},{16,24},{20,28},{24,16},{28,20},{1,9},{5... | collective-permute-start | bytes 49160 | tf_op jit(solution)/shard_map/ppermute | solution.py:26
  175.4 23.0 %collective-permute-start.29 = (bf16[16,4096]{1,0:T(8,128)(2,1)S(1)}, bf16[16,4096]{1,0:T(8,128)(2,1)S(1)}, u32[]{:S(2)}, u32[]{:S(2)}) collective-permute-start(bf16[16,4096]{1,0:T(8,128)(2,1)S(1)} %fusion.21), channel_id=1, source_target_pairs={{0,480},{32,0},{64,32},{96,64},{128,96},{160,128},{192,160},{224,1... | collective-permute-start | bytes 393224 | tf_op jit(solution)/shard_map/ppermute | solution.py:20
  (21 other events, 256.4 us)

commit v4 on v3

v4 whole, which is shorter than its diff:
```python
import jax
import jax.numpy as jnp
from jax import lax
from jax.experimental import pallas as pl
from jax.experimental.pallas import tpu as pltpu
from jax.sharding import Mesh, PartitionSpec as P

TAPS = 3
EPSILON = 1e-06
Y, Z, CORE = 8, 2, 2
TENSOR = ("y", "z", "core")
SWAP = ((0, 1), (1, 0))
F32, BF16 = jnp.float32, jnp.bfloat16


def contract(left, right, dims):
    return lax.dot_general(left, right, (dims, ((), ())), preferred_element_type=F32)


def along(block, axis, distance):
    devices = lax.axis_size(axis)
    return lax.ppermute(block, axis, [(i, (i + distance) % devices) for i in range(devices)])


def with_partner(total, axis, apart):
    devices = range(lax.axis_size(axis))
    return total + lax.ppermute(total, axis, [(i, i ^ apart) for i in devices])


def gathered(own):
    half, rows = Y // 2, own.shape[0] // 2
    found = {0: own}
    ahead = behind = own
    for step in range(1, half):
        ahead, behind = along(ahead, "y", -1), along(behind, "y", 1)
        found[step], found[Y - step] = ahead, behind
    found[half] = (along(ahead[:rows], "y", -1), along(behind[rows:], "y", 1))
    return found


def reduced(share, partial):
    half = Y // 2
    up, down = along(share[half], "y", 1), share[half + 1]
    up, partial = lax.optimization_barrier((up, partial))
    kept_val, kept_out, given, total = partial
    taken = lax.ppermute(given, "core", SWAP)
    beside = ((("core", 1), ("z", 1)), (("y", 1),), (("y", 2),))
    for step in range(1, half):
        up = along((share[half - step].astype(F32) + up.astype(F32)).astype(BF16), "y", 1)
        if step > 1:
            down = (share[half + step].astype(F32) + down.astype(F32)).astype(BF16)
        down = along(down, "y", -1)
        for axis, apart in beside[step - 1]:
            total = with_partner(total, axis, apart)
        up, down, total = lax.optimization_barrier((up, down, total))
    up, taken = lax.optimization_barrier((up, taken))
    grad_wv = (kept_val + taken[0].astype(F32)).astype(BF16)
    grad_wo = (kept_out + taken[1].astype(F32)).astype(BF16)
    return share[0].astype(F32) + up.astype(F32) + down.astype(F32), grad_wv, grad_wo, total


def vmem_params(mib):
    return pltpu.CompilerParams(vmem_limit_bytes=mib << 20)


def sorted_products(products, rows, channels):
    def body(*refs):
        kept, given = refs[-2:]
        for y in range(Y):
            for z in range(Z):
                for kind in range(2):
                    if y < Y // 2:
                        source, at = refs[y], (2 * z + kind) * rows
                    elif y > Y // 2:
                        source, at = refs[y + 1], (2 * z + kind) * rows
                    else:
                        source, at = refs[y + z], kind * rows
                    for core, target in enumerate((kept, given)):
                        column = (2 * kind + core) * channels
                        target[kind, z, y] = source[at : at + rows, column : column + channels]

    operands = [*products[: Y // 2], *products[Y // 2], *products[Y // 2 + 1 :]]
    shape = jax.ShapeDtypeStruct((2, Z, Y, rows, channels), F32)
    return pl.pallas_call(
        body,
        out_shape=(shape, shape),
        compiler_params=vmem_params(16),
        cost_estimate=pl.CostEstimate(flops=0, bytes_accessed=4 << 20, transcendentals=0),
        name="sorted_products",
    )(*operands)


def through_gate(place, kept, taken, filters, lead_rows):
    rows, channels = kept.shape[-2:]
    tokens = rows * Y * Z * CORE
    edge = 8

    def body(place, kept, taken, filters, lead, own, other, near_z, grad_filter, grad_lead, ext, cot, back, val, gat):
        def start(core, z, y):
            at_y = lax.rem(place[0] + y, Y)
            at_z = place[1] if z == 0 else 1 - place[1]
            at_core = place[2] if core == 0 else 1 - place[2]
            return pl.multiple_of(((at_y * Z + at_z) * CORE + at_core) * rows, rows)

        ext[0:edge] = jnp.zeros((edge, channels), F32)
        ext[edge - TAPS + 1 : edge] = lead[...]
        for core, source in enumerate((kept, taken)):
            for z in range(Z):
                for y in range(Y):
                    at = start(core, z, y)
                    ext[pl.ds(edge + at, rows)] = source[0, z, y].astype(BF16).astype(F32)
                    cot[pl.ds(at, rows)] = source[1, z, y]
        taps = [filters[k : k + 1, :] for k in range(TAPS)]
        delayed = [ext[edge - k : edge - k + tokens] for k in range(TAPS)]
        conv_out = taps[0] * delayed[0]
        for k in range(1, TAPS):
            conv_out = conv_out + taps[k] * delayed[k]
        gate_sig = jax.nn.sigmoid(conv_out)
        gat[...] = (conv_out * gate_sig).astype(BF16)
        grad_conv = cot[...] * gate_sig * (1.0 + conv_out * (1.0 - gate_sig))
        for k in range(TAPS):
            grad_filter[k : k + 1, :] = jnp.sum(grad_conv * delayed[k], axis=0, keepdims=True)
        back[0:edge] = jnp.zeros((edge, channels), F32)
        back[edge + tokens : edge + tokens + edge] = jnp.zeros((edge, channels), F32)
        back[edge : edge + tokens] = grad_conv
        grad_values = taps[0] * back[edge : edge + tokens]
        first = edge - TAPS + 1
        grad_head = taps[0] * back[first:edge]
        for k in range(1, TAPS):
            grad_values = grad_values + taps[k] * back[edge + k : edge + k + tokens]
            grad_head = grad_head + taps[k] * back[first + k : edge + k]
        grad_lead[...] = grad_head
        val[...] = grad_values.astype(BF16)
        for z in range(Z):
            for y in range(Y):
                block = slice(y * rows, (y + 1) * rows)
                at = start(0, z, y)
                own[0, z, block] = val[pl.ds(at, rows)]
                own[1, z, block] = gat[pl.ds(at, rows)]
                if z == 1:
                    near_z[0, block] = val[pl.ds(at, rows)]
                at = start(1, z, y)
                other[0, z, block] = val[pl.ds(at, rows)]
                other[1, z, block] = gat[pl.ds(at, rows)]
                if z == 1:
                    near_z[1, block] = val[pl.ds(at, rows)]

    vmem = pl.BlockSpec(memory_space=pltpu.VMEM)
    quarter = (Y * rows, channels)
    return pl.pallas_call(
        body,
        in_specs=[pl.BlockSpec(memory_space=pltpu.SMEM)] + [vmem] * 4,
        out_specs=[vmem] * 5,
        out_shape=(
            jax.ShapeDtypeStruct((2, Z, *quarter), BF16),
            jax.ShapeDtypeStruct((2, Z, *quarter), BF16),
            jax.ShapeDtypeStruct((CORE, *quarter), BF16),
            jax.ShapeDtypeStruct((TAPS, channels), F32),
            jax.ShapeDtypeStruct((TAPS - 1, channels), F32),
        ),
        scratch_shapes=[
            pltpu.VMEM((edge + tokens, channels), F32),
            pltpu.VMEM((tokens, channels), F32),
            pltpu.VMEM((edge + tokens + edge, channels), F32),
            pltpu.VMEM((tokens, channels), BF16),
            pltpu.VMEM((tokens, channels), BF16),
        ],
        compiler_params=vmem_params(16),
        cost_estimate=pl.CostEstimate(flops=4 << 20, bytes_accessed=4 << 20, transcendentals=1 << 16),
        name="through_gate",
    )(place, kept, taken, filters, lead_rows)


def weight_gradients(found, own, taken, val_pair, gain_row, rows):
    width = gain_row.shape[-1]
    channels = own.shape[-1]
    column = 512

    def body(*refs):
        blocks, (own, taken, val_own, val_core, gain, *kept, given, term) = refs[: Y + 1], refs[Y + 1 :]

        def rows_of(kind):
            parts = []
            for z in range(Z):
                for y in range(Y):
                    at = (2 * z + kind) * rows
                    if y < Y // 2:
                        parts.append(blocks[y][at : at + rows])
                    elif y > Y // 2:
                        parts.append(blocks[y + 1][at : at + rows])
                    else:
                        parts.append(blocks[y + z][kind * rows : (kind + 1) * rows])
            return jnp.concatenate(parts, axis=0)

        for kind in range(2):
            factor = jnp.concatenate(
                [ref[kind].reshape(Z * Y * rows, channels) for ref in (own, taken)], axis=1
            )
            grad = contract(factor, rows_of(kind), ((0,), (0,)))
            kept[kind][...] = grad[:channels]
            given[kind] = grad[channels:].astype(BF16)
            if kind == 0:
                total = jnp.sum(grad[:channels] * val_own[...].astype(F32), axis=0, keepdims=True)
                total += jnp.sum(grad[channels:] * val_core[...].astype(F32), axis=0, keepdims=True)
                term[...] = total / gain[...]

    operands = [found[y] for y in range(Y // 2)] + list(found[Y // 2]) + [found[y] for y in range(Y // 2 + 1, Y)]
    by_column = lambda count: pl.BlockSpec((count, column), lambda i: (0, i))
    whole = pl.BlockSpec(own.shape, lambda i: (0, 0, 0, 0))
    stacked = pl.BlockSpec((2, channels, column), lambda i: (0, 0, i))
    return pl.pallas_call(
        body,
        grid=(width // column,),
        in_specs=[by_column(o.shape[0]) for o in operands]
        + [whole, whole, by_column(channels), by_column(channels), by_column(1)],
        out_specs=[by_column(channels), by_column(channels), stacked, by_column(1)],
        out_shape=(
            jax.ShapeDtypeStruct((channels, width), F32),
            jax.ShapeDtypeStruct((channels, width), F32),
            jax.ShapeDtypeStruct((2, channels, width), BF16),
            jax.ShapeDtypeStruct((1, width), F32),
        ),
        compiler_params=vmem_params(24),
        cost_estimate=pl.CostEstimate(flops=1 << 30, bytes_accessed=13 << 20, transcendentals=0),
        name="weight_gradients",
    )(*operands, own, taken, *val_pair, gain_row)


def on_device(x_in, grad_out, gain, w_val, w_out, filt, tail, micro_index):
    x_rows, cot_rows, gain_row = x_in[0], grad_out[0], gain[0]
    val_weight, out_weight = w_val[0], w_out[0]
    filters, tail_rows = filt[0], tail[0]
    has_tail = micro_index[0] > 0
    rows, width = x_rows.shape
    channels = val_weight.shape[0]

    x_float = x_rows.astype(F32)
    inv_rms = lax.rsqrt(jnp.mean(x_float * x_float, axis=-1, keepdims=True) + EPSILON)
    normed = (x_float * inv_rms * gain_row).astype(BF16)

    own = jnp.concatenate([normed, cot_rows], axis=0)
    mate = lax.ppermute(own, "z", SWAP)
    found = gathered(jnp.concatenate([own, mate], axis=0))

    val_core = lax.ppermute(val_weight, "core", SWAP)
    out_core = lax.ppermute(out_weight, "core", SWAP)
    val_sent, mate_done = lax.optimization_barrier((val_weight, mate))
    val_z = lax.ppermute(val_sent, "z", SWAP)
    val_z_core = lax.ppermute(val_z, "core", SWAP)
    weights = lax.optimization_barrier(
        jnp.concatenate([val_weight, val_core, out_weight, out_core], axis=0)
    )

    def product(block):
        return contract(block, weights, ((1,), (1,)))

    products = [
        tuple(product(b) for b in found[y]) if y == Y // 2 else product(found[y]) for y in range(Y)
    ]
    kept, given = sorted_products(products, rows, channels)
    taken = lax.ppermute(given, "core", SWAP)
    val_z, val_z_core, kept = lax.optimization_barrier((val_z, val_z_core, kept))
    val_weights = jnp.concatenate([val_weight, val_core, val_z, val_z_core], axis=0)
    val_weights, kept = lax.optimization_barrier((val_weights, kept))

    place = jnp.stack([lax.axis_index(axis) for axis in TENSOR]).astype(jnp.int32)
    lead_rows = jnp.where(has_tail, tail_rows, jnp.zeros_like(tail_rows)).astype(F32)
    own, other, near_z, grad_filter, grad_lead = through_gate(place, kept, taken, filters, lead_rows)
    grad_tail = jnp.where(has_tail, grad_lead, jnp.zeros_like(grad_lead))

    near_z_core = near_z[1]
    taken = lax.ppermute(other, "core", SWAP)
    from_z = lax.ppermute(near_z[0], "z", SWAP)
    from_z_core = lax.ppermute(near_z_core, ("z", "core"), [(i, i ^ 3) for i in range(Z * CORE)])
    share = contract(
        jnp.concatenate([own[0, 0], taken[0, 0], from_z, from_z_core], axis=1), val_weights, ((1,), (0,))
    )
    partial = weight_gradients(found, own, taken, (val_weight, val_core), gain_row[None], rows)
    grad_normed, grad_wv, grad_wo, gain_term = reduced(share.astype(BF16).reshape(Y, rows, width), partial)
    grad_gain = with_partner(gain_term, "y", 4)

    scaled = gain_row * grad_normed
    grad_local = (
        cot_rows.astype(F32)
        + inv_rms * scaled
        - x_float * inv_rms**3 * jnp.mean(scaled * x_float, axis=-1, keepdims=True)
    )
    received = along(grad_local.astype(BF16), "section", -1)
    return (
        received[None],
        grad_wv[None],
        grad_wo[None],
        grad_filter[None],
        grad_tail[None],
        grad_gain,
    )


def solution(mesh):
    sections = mesh.shape["section"]
    split = Mesh(mesh.devices.reshape(sections, Y, Z, CORE), ("section", *TENSOR))
    by_rows = P("section", TENSOR, None)
    by_columns = P("section", None, TENSOR)
    whole = P("section", None)
    return jax.shard_map(
        on_device,
        mesh=split,
        in_specs=(by_rows, by_rows, whole, by_rows, by_rows, by_columns, by_columns, P("section")),
        out_specs=(by_rows, by_rows, by_rows, by_columns, by_columns, whole),
        check_vma=False,
    )
```

time: 202 us -> 167 us (0.83)
  the two profiles are of different devices: /device:TPU:16 before, /device:TPU:24 now
where the time goes in v4:
time: 167 us; the launch traced here: 166 us
  starting transfers between devices  105 us (63%)
  waiting for transfers between devices  28.6 us (17%)
  matrix products  13.2 us (8%)
  other arithmetic  10.8 us (6%)
  Pallas kernels  4.89 us (3%)
  local copies, waits for them, and re-layouts  2 us (1%)
  between operations  1.86 us (1%)
    ppermute x16, starting transfers between devices, along(): lax.ppermute(block, axis, [(i, (i + distance) % devices) for i in range(d...  64.1 us
    ppermute x5, starting transfers between devices, with_partner(): return total + lax.ppermute(total, axis, [(i, i ^ apart) for i in devices])  14.5 us
    dot_general x10, matrix products, contract(): lax.dot_general(left, right, (dims, ((), ())), preferred_element_type=F32)  13.2 us
    ppermute x5, waiting for transfers between devices, with_partner(): return total + lax.ppermute(total, axis, [(i, i ^ apart) for i in devices])  12.8 us
    ppermute x16, waiting for transfers between devices, along(): lax.ppermute(block, axis, [(i, (i + distance) % devices) for i in range(d...  12 us
    ppermute x1, starting transfers between devices, on_device(): mate = lax.ppermute(own, 'z', SWAP)  4.28 us
    pallas_call x1, Pallas kernels, weight_gradients(): pl.pallas_call(body, grid=(width // column,), in_specs=[by_column(o.shape...  3.81 us
    ppermute x1, starting transfers between devices, on_device(): val_z = lax.ppermute(val_sent, 'z', SWAP)  3.63 us
  transfers between devices with their start and end apart: 31, of which 13 were waited for; matrix products, arithmetic and copies ran while one was open for 13% of the time, Pallas kernels for 2%

profile of v4, /device:TPU:24, one launch (start us, length us, event | category | flops | bytes accessed | tf_op | source)
XLA Modules:
  0.0 166.1 jit_solution(17911457474856818998)
XLA Ops:
  3.6 4.3 %collective-permute-start.1 = (bf16[32,4096]{1,0:T(8,128)(2,1)S(1)}, bf16[32,4096]{1,0:T(8,128)(2,1)S(1)}, u32[]{:S(2)}, u32[]{:S(2)}) collective-permute-start(bf16[32,4096]{1,0:T(8,128)(2,1)S(1)} %pad_maximum_fusion.4), channel_id=1, source_target_pairs={{0,2},{2,0},{1,3},{3,1},{4,6},{6,4},{5,7},{7,5},{8,10},{10,8},{9,1... | collective-permute-start | bytes 786440 | tf_op jit(solution)/shard_map/ppermute | solution.py:242
  9.9 2.4 %collective-permute-start.4 = (bf16[128,4096]{1,0:T(8,128)(2,1)}, bf16[128,4096]{1,0:T(8,128)(2,1)}, u32[]{:S(2)}, u32[]{:S(2)}) collective-permute-start(bf16[128,4096]{1,0:T(8,128)(2,1)} %bitcast.76), channel_id=1, source_target_pairs={{0,1},{1,0},{2,3},{3,2},{4,5},{5,4},{6,7},{7,6},{8,9},{9,8},{10,11... | collective-permute-start | bytes 3145736 | tf_op jit(solution)/shard_map/ppermute | solution.py:246
  15.2 4.7 %collective-permute-start.9 = (bf16[64,4096]{1,0:T(8,128)(2,1)S(1)}, bf16[64,4096]{1,0:T(8,128)(2,1)S(1)}, u32[]{:S(2)}, u32[]{:S(2)}) collective-permute-start(bf16[64,4096]{1,0:T(8,128)(2,1)S(1)} %pad_maximum_fusion.3.refs_0_), channel_id=1, source_target_pairs={{0,4},{4,8},{8,12},{12,16},{16,20},{20,24},{24,28},{28,0},{1,5},{5... | collective-permute-start | bytes 1572872 | tf_op jit(solution)/shard_map/ppermute | solution.py:22
  23.9 3.6 %collective-permute-start.2 = (bf16[128,4096]{1,0:T(8,128)(2,1)}, bf16[128,4096]{1,0:T(8,128)(2,1)S(1)}, u32[]{:S(2)}, u32[]{:S(2)}) collective-permute-start(bf16[128,4096]{1,0:T(8,128)(2,1)} %bitcast.64), channel_id=1, source_target_pairs={{0,2},{2,0},{1,3},{3,1},{4,6},{6,4},{5,7},{7,5},{8,10},{10,8},{9,1... | collective-permute-start | bytes 3145736 | tf_op jit(solution)/shard_map/ppermute | solution.py:248
  27.5 2.9 %collective-permute-done.9.refs_8_ = bf16[64,4096]{1,0:T(8,128)(2,1)S(1)} collective-permute-done((bf16[64,4096]{1,0:T(8,128)(2,1)S(1)}, bf16[64,4096]{1,0:T(8,128)(2,1)S(1)}, u32[]{:S(2)}, u32[]{:S(2)}) %collective-permute-start.9) | collective-permute-done | bytes 524320 | tf_op jit(solution)/shard_map/ppermute | solution.py:22
  30.4 5.6 %collective-permute-start.10 = (bf16[64,4096]{1,0:T(8,128)(2,1)S(1)}, bf16[64,4096]{1,0:T(8,128)(2,1)S(1)}, u32[]{:S(2)}, u32[]{:S(2)}) collective-permute-start(bf16[64,4096]{1,0:T(8,128)(2,1)S(1)} %collective-permute-done.9.refs_8_), channel_id=1, source_target_pairs={{0,4},{4,8},{8,12},{12,16},{16,20},{20,24},{24,28},{28,0},{1,5},{5... | collective-permute-start | bytes 1572872 | tf_op jit(solution)/shard_map/ppermute | solution.py:22
  45.8 5.6 %collective-permute-start.11 = (bf16[64,4096]{1,0:T(8,128)(2,1)S(1)}, bf16[64,4096]{1,0:T(8,128)(2,1)S(1)}, u32[]{:S(2)}, u32[]{:S(2)}) collective-permute-start(bf16[64,4096]{1,0:T(8,128)(2,1)S(1)} %collective-permute-done.10.refs_7_), channel_id=1, source_target_pairs={{0,4},{4,8},{8,12},{12,16},{16,20},{20,24},{24,28},{28,0},{1,5},{5... | collective-permute-start | bytes 1572872 | tf_op jit(solution)/shard_map/ppermute | solution.py:22
  60.3 5.6 %collective-permute-start.12 = (bf16[32,4096]{1,0:T(8,128)(2,1)S(1)}, bf16[32,4096]{1,0:T(8,128)(2,1)S(1)}, u32[]{:S(2)}, u32[]{:S(2)}) collective-permute-start(bf16[32,4096]{1,0:T(8,128)(2,1)S(1)} %slice.73), channel_id=1, source_target_pairs={{0,4},{4,8},{8,12},{12,16},{16,20},{20,24},{24,28},{28,0},{1,5},{5... | collective-permute-start | bytes 786440 | tf_op jit(solution)/shard_map/ppermute | solution.py:22
  72.0 3.4 %collective-permute-done.8.refs_4_ = bf16[32,4096]{1,0:T(8,128)(2,1)S(1)} collective-permute-done((bf16[32,4096]{1,0:T(8,128)(2,1)S(1)}, bf16[32,4096]{1,0:T(8,128)(2,1)S(1)}, u32[]{:S(2)}, u32[]{:S(2)}) %collective-permute-start.8) | collective-permute-done | bytes 262176 | tf_op jit(solution)/shard_map/ppermute | solution.py:22
  81.3 2.8 %collective-permute-start.15 = (bf16[128,128]{1,0:T(8,128)(2,1)S(1)}, bf16[128,128]{1,0:T(8,128)(2,1)S(1)}, u32[]{:S(2)}, u32[]{:S(2)}) collective-permute-start(bf16[128,128]{1,0:T(8,128)(2,1)S(1)} %get-tuple-element.86), channel_id=1, source_target_pairs={{0,2},{2,0},{1,3},{3,1},{4,6},{6,4},{5,7},{7,5},{8,10},{10,8},{9,1... | collective-permute-start | bytes 98312 | tf_op jit(solution)/shard_map/ppermute | solution.py:273
  84.1 2.5 %collective-permute-start.16 = (bf16[128,128]{1,0:T(8,128)(2,1)S(1)}, bf16[128,128]{1,0:T(8,128)(2,1)S(1)}, u32[]{:S(2)}, u32[]{:S(2)}) collective-permute-start(bf16[128,128]{1,0:T(8,128)(2,1)S(1)} %get-tuple-element.87), channel_id=1, source_target_pairs={{0,3},{1,2},{2,1},{3,0},{4,7},{5,6},{6,5},{7,4},{8,11},{9,10},{10,... | collective-permute-start | bytes 98312 | tf_op jit(solution)/shard_map/ppermute | solution.py:274
  86.6 2.6 %collective-permute-start.14 = (bf16[2,2,128,128]{3,2,1,0:T(8,128)(2,1)S(1)}, bf16[2,2,128,128]{3,2,1,0:T(8,128)(2,1)S(1)}, u32[]{:S(2)}, u32[]{:S(2)}) collective-permute-start(bf16[2,2,128,128]{3,2,1,0:T(8,128)(2,1)S(1)} %get-tuple-element.47), channel_id=1, source_target_pairs={{0,1},{1,0},{2,3},{3,2},{4,5},{5,4},{6,7},{7,6},{8,9},{9,8},{10,11... | collective-permute-start | bytes 393224 | tf_op jit(solution)/shard_map/ppermute | solution.py:272
  92.9 4.1 %collective-permute-start.19 = (bf16[16,4096]{1,0:T(8,128)(2,1)S(1)}, bf16[16,4096]{1,0:T(8,128)(2,1)S(1)}, u32[]{:S(2)}, u32[]{:S(2)}) collective-permute-start(bf16[16,4096]{1,0:T(8,128)(2,1)S(1)} %get-tuple-element.84), channel_id=1, source_target_pairs={{0,28},{4,0},{8,4},{12,8},{16,12},{20,16},{24,20},{28,24},{1,29},{... | collective-permute-start | bytes 393224 | tf_op jit(solution)/shard_map/ppermute | solution.py:22
  96.9 3.8 %weight_gradients.1 = (f32[128,4096]{1,0:T(8,128)S(1)}, f32[128,4096]{1,0:T(8,128)S(1)}, bf16[2,128,4096]{2,1,0:T(8,128)(2,1)S(1)}, f32[1,4096]{1,0:T(1,128)S(1)}) custom-call(bf16[64,4096]{1,0:T(8,128)(2,1)S(1)} %pad_maximum_fusion.3.refs_0_, bf16[64,4096]{1,0:T(8,128)(2,1)S(1)} %collective-permute-done.5.refs_1_, ...), custom_call_target="tpu_custom_call" | custom-call | flops 1073741824 | bytes 13631488 | tf_op jit(solution)/shard_map/weight_gradients/pallas_call | solution.py:211
  100.8 3.1 %collective-permute-start.18 = (bf16[16,4096]{1,0:T(8,128)(2,1)S(1)}, bf16[16,4096]{1,0:T(8,128)(2,1)S(1)}, u32[]{:S(2)}, u32[]{:S(2)}) collective-permute-start(bf16[16,4096]{1,0:T(8,128)(2,1)S(1)} %add_convert_fusion.4), channel_id=1, source_target_pairs={{0,4},{4,8},{8,12},{12,16},{16,20},{20,24},{24,28},{28,0},{1,5},{5... | collective-permute-start | bytes 393224 | tf_op jit(solution)/shard_map/ppermute | solution.py:22
  107.1 2.8 %collective-permute-start.21 = (f32[1,4096]{1,0:T(1,128)S(1)}, f32[1,4096]{1,0:T(1,128)S(1)}, u32[]{:S(2)}, u32[]{:S(2)}) collective-permute-start(f32[1,4096]{1,0:T(1,128)S(1)} %add.58), channel_id=1, source_target_pairs={{0,2},{2,0},{1,3},{3,1},{4,6},{6,4},{5,7},{7,5},{8,10},{10,8},{9,1... | collective-permute-start | bytes 49160 | tf_op jit(solution)/shard_map/ppermute | solution.py:27
  112.8 2.7 %collective-permute-start.23 = (bf16[16,4096]{1,0:T(8,128)(2,1)S(1)}, bf16[16,4096]{1,0:T(8,128)(2,1)S(1)}, u32[]{:S(2)}, u32[]{:S(2)}) collective-permute-start(bf16[16,4096]{1,0:T(8,128)(2,1)S(1)} %get-tuple-element.82), channel_id=1, source_target_pairs={{0,28},{4,0},{8,4},{12,8},{16,12},{20,16},{24,20},{28,24},{1,29},{... | collective-permute-start | bytes 393224 | tf_op jit(solution)/shard_map/ppermute | solution.py:22
  115.5 4.3 %collective-permute-start.22 = (bf16[16,4096]{1,0:T(8,128)(2,1)S(1)}, bf16[16,4096]{1,0:T(8,128)(2,1)S(1)}, u32[]{:S(2)}, u32[]{:S(2)}) collective-permute-start(bf16[16,4096]{1,0:T(8,128)(2,1)S(1)} %get-tuple-element.83), channel_id=1, source_target_pairs={{0,4},{4,8},{8,12},{12,16},{16,20},{20,24},{24,28},{28,0},{1,5},{5... | collective-permute-start | bytes 393224 | tf_op jit(solution)/shard_map/ppermute | solution.py:22
  121.8 3.7 %collective-permute-done.24 = f32[1,4096]{1,0:T(1,128)S(1)} collective-permute-done((f32[1,4096]{1,0:T(1,128)S(1)}, f32[1,4096]{1,0:T(1,128)S(1)}, u32[]{:S(2)}, u32[]{:S(2)}) %collective-permute-start.24) | collective-permute-done | bytes 16416 | tf_op jit(solution)/shard_map/ppermute | solution.py:27
  127.5 5.1 %collective-permute-start.25 = (bf16[16,4096]{1,0:T(8,128)(2,1)S(1)}, bf16[16,4096]{1,0:T(8,128)(2,1)S(1)}, u32[]{:S(2)}, u32[]{:S(2)}) collective-permute-start(bf16[16,4096]{1,0:T(8,128)(2,1)S(1)} %get-tuple-element.81), channel_id=1, source_target_pairs={{0,4},{4,8},{8,12},{12,16},{16,20},{20,24},{24,28},{28,0},{1,5},{5... | collective-permute-start | bytes 393224 | tf_op jit(solution)/shard_map/ppermute | solution.py:22
  134.6 4.6 %collective-permute-done.27 = f32[1,4096]{1,0:T(1,128)S(1)} collective-permute-done((f32[1,4096]{1,0:T(1,128)S(1)}, f32[1,4096]{1,0:T(1,128)S(1)}, u32[]{:S(2)}, u32[]{:S(2)}) %collective-permute-start.27) | collective-permute-done | bytes 16416 | tf_op jit(solution)/shard_map/ppermute | solution.py:27
  139.3 5.9 %collective-permute-start.30 = (f32[1,4096]{1,0:T(1,128)S(1)}, f32[1,4096]{1,0:T(1,128)S(1)}, u32[]{:S(2)}, u32[]{:S(2)}) collective-permute-start(f32[1,4096]{1,0:T(1,128)S(1)} %add.65), channel_id=1, source_target_pairs={{0,16},{4,20},{8,24},{12,28},{16,0},{20,4},{24,8},{28,12},{1,17},{... | collective-permute-start | bytes 49160 | tf_op jit(solution)/shard_map/ppermute | solution.py:27
  146.3 2.5 %collective-permute-done.30 = f32[1,4096]{1,0:T(1,128)S(1)} collective-permute-done((f32[1,4096]{1,0:T(1,128)S(1)}, f32[1,4096]{1,0:T(1,128)S(1)}, u32[]{:S(2)}, u32[]{:S(2)}) %collective-permute-start.30) | collective-permute-done | bytes 16416 | tf_op jit(solution)/shard_map/ppermute | solution.py:27
  149.8 11.7 %collective-permute-start.29 = (bf16[16,4096]{1,0:T(8,128)(2,1)S(1)}, bf16[16,4096]{1,0:T(8,128)(2,1)S(1)}, u32[]{:S(2)}, u32[]{:S(2)}) collective-permute-start(bf16[16,4096]{1,0:T(8,128)(2,1)S(1)} %fusion.9), channel_id=1, source_target_pairs={{0,480},{32,0},{64,32},{96,64},{128,96},{160,128},{192,160},{224,1... | collective-permute-start | bytes 393224 | tf_op jit(solution)/shard_map/ppermute | solution.py:22
  (90 shorter events, 63.8 us)
Async XLA Ops:
  3.6 10.6 %collective-permute-start.1 = (bf16[32,4096]{1,0:T(8,128)(2,1)S(1)}, bf16[32,4096]{1,0:T(8,128)(2,1)S(1)}, u32[]{:S(2)}, u32[]{:S(2)}) collective-permute-start(bf16[32,4096]{1,0:T(8,128)(2,1)S(1)} %pad_maximum_fusion.4), channel_id=1, source_target_pairs={{0,2},{2,0},{1,3},{3,1},{4,6},{6,4},{5,7},{7,5},{8,10},{10,8},{9,1... | collective-permute-start | bytes 786440 | tf_op jit(solution)/shard_map/ppermute | solution.py:242
  7.9 30.1 %collective-permute-start = (bf16[128,4096]{1,0:T(8,128)(2,1)}, bf16[128,4096]{1,0:T(8,128)(2,1)S(1)}, u32[]{:S(2)}, u32[]{:S(2)}) collective-permute-start(bf16[128,4096]{1,0:T(8,128)(2,1)} %bitcast.63), channel_id=1, source_target_pairs={{0,1},{1,0},{2,3},{3,2},{4,5},{5,4},{6,7},{7,6},{8,9},{9,8},{10,11... | collective-permute-start | bytes 3145736 | tf_op jit(solution)/shard_map/ppermute | solution.py:245
  9.9 28.1 %collective-permute-start.4 = (bf16[128,4096]{1,0:T(8,128)(2,1)}, bf16[128,4096]{1,0:T(8,128)(2,1)}, u32[]{:S(2)}, u32[]{:S(2)}) collective-permute-start(bf16[128,4096]{1,0:T(8,128)(2,1)} %bitcast.76), channel_id=1, source_target_pairs={{0,1},{1,0},{2,3},{3,2},{4,5},{5,4},{6,7},{7,6},{8,9},{9,8},{10,11... | collective-permute-start | bytes 3145736 | tf_op jit(solution)/shard_map/ppermute | solution.py:246
  15.2 15.3 %collective-permute-start.9 = (bf16[64,4096]{1,0:T(8,128)(2,1)S(1)}, bf16[64,4096]{1,0:T(8,128)(2,1)S(1)}, u32[]{:S(2)}, u32[]{:S(2)}) collective-permute-start(bf16[64,4096]{1,0:T(8,128)(2,1)S(1)} %pad_maximum_fusion.3.refs_0_), channel_id=1, source_target_pairs={{0,4},{4,8},{8,12},{12,16},{16,20},{20,24},{24,28},{28,0},{1,5},{5... | collective-permute-start | bytes 1572872 | tf_op jit(solution)/shard_map/ppermute | solution.py:22
  19.9 16.2 %collective-permute-start.5 = (bf16[64,4096]{1,0:T(8,128)(2,1)S(1)}, bf16[64,4096]{1,0:T(8,128)(2,1)S(1)}, u32[]{:S(2)}, u32[]{:S(2)}) collective-permute-start(bf16[64,4096]{1,0:T(8,128)(2,1)S(1)} %pad_maximum_fusion.3.refs_0_), channel_id=1, source_target_pairs={{0,28},{4,0},{8,4},{12,8},{16,12},{20,16},{24,20},{28,24},{1,29},{... | collective-permute-start | bytes 1572872 | tf_op jit(solution)/shard_map/ppermute | solution.py:22
  23.9 29.4 %collective-permute-start.2 = (bf16[128,4096]{1,0:T(8,128)(2,1)}, bf16[128,4096]{1,0:T(8,128)(2,1)S(1)}, u32[]{:S(2)}, u32[]{:S(2)}) collective-permute-start(bf16[128,4096]{1,0:T(8,128)(2,1)} %bitcast.64), channel_id=1, source_target_pairs={{0,2},{2,0},{1,3},{3,1},{4,6},{6,4},{5,7},{7,5},{8,10},{10,8},{9,1... | collective-permute-start | bytes 3145736 | tf_op jit(solution)/shard_map/ppermute | solution.py:248
  30.4 15.3 %collective-permute-start.10 = (bf16[64,4096]{1,0:T(8,128)(2,1)S(1)}, bf16[64,4096]{1,0:T(8,128)(2,1)S(1)}, u32[]{:S(2)}, u32[]{:S(2)}) collective-permute-start(bf16[64,4096]{1,0:T(8,128)(2,1)S(1)} %collective-permute-done.9.refs_8_), channel_id=1, source_target_pairs={{0,4},{4,8},{8,12},{12,16},{16,20},{20,24},{24,28},{28,0},{1,5},{5... | collective-permute-start | bytes 1572872 | tf_op jit(solution)/shard_map/ppermute | solution.py:22
  36.1 15.3 %collective-permute-start.6 = (bf16[64,4096]{1,0:T(8,128)(2,1)S(1)}, bf16[64,4096]{1,0:T(8,128)(2,1)S(1)}, u32[]{:S(2)}, u32[]{:S(2)}) collective-permute-start(bf16[64,4096]{1,0:T(8,128)(2,1)S(1)} %collective-permute-done.5.refs_1_), channel_id=1, source_target_pairs={{0,28},{4,0},{8,4},{12,8},{16,12},{20,16},{24,20},{28,24},{1,29},{... | collective-permute-start | bytes 1572872 | tf_op jit(solution)/shard_map/ppermute | solution.py:22
  45.8 14.5 %collective-permute-start.11 = (bf16[64,4096]{1,0:T(8,128)(2,1)S(1)}, bf16[64,4096]{1,0:T(8,128)(2,1)S(1)}, u32[]{:S(2)}, u32[]{:S(2)}) collective-permute-start(bf16[64,4096]{1,0:T(8,128)(2,1)S(1)} %collective-permute-done.10.refs_7_), channel_id=1, source_target_pairs={{0,4},{4,8},{8,12},{12,16},{16,20},{20,24},{24,28},{28,0},{1,5},{5... | collective-permute-start | bytes 1572872 | tf_op jit(solution)/shard_map/ppermute | solution.py:22
  51.4 14.5 %collective-permute-start.7 = (bf16[64,4096]{1,0:T(8,128)(2,1)S(1)}, bf16[64,4096]{1,0:T(8,128)(2,1)S(1)}, u32[]{:S(2)}, u32[]{:S(2)}) collective-permute-start(bf16[64,4096]{1,0:T(8,128)(2,1)S(1)} %collective-permute-done.6.refs_2_), channel_id=1, source_target_pairs={{0,28},{4,0},{8,4},{12,8},{16,12},{20,16},{24,20},{28,24},{1,29},{... | collective-permute-start | bytes 1572872 | tf_op jit(solution)/shard_map/ppermute | solution.py:22
  53.3 25.6 %collective-permute-start.3 = (bf16[128,4096]{1,0:T(8,128)(2,1)S(1)}, bf16[128,4096]{1,0:T(8,128)(2,1)S(1)}, u32[]{:S(2)}, u32[]{:S(2)}) collective-permute-start(bf16[128,4096]{1,0:T(8,128)(2,1)S(1)} %collective-permute-done.2), channel_id=1, source_target_pairs={{0,1},{1,0},{2,3},{3,2},{4,5},{5,4},{6,7},{7,6},{8,9},{9,8},{10,11... | collective-permute-start | bytes 3145736 | tf_op jit(solution)/shard_map/ppermute | solution.py:249
  60.3 10.4 %collective-permute-start.12 = (bf16[32,4096]{1,0:T(8,128)(2,1)S(1)}, bf16[32,4096]{1,0:T(8,128)(2,1)S(1)}, u32[]{:S(2)}, u32[]{:S(2)}) collective-permute-start(bf16[32,4096]{1,0:T(8,128)(2,1)S(1)} %slice.73), channel_id=1, source_target_pairs={{0,4},{4,8},{8,12},{12,16},{16,20},{20,24},{24,28},{28,0},{1,5},{5... | collective-permute-start | bytes 786440 | tf_op jit(solution)/shard_map/ppermute | solution.py:22
  65.9 9.5 %collective-permute-start.8 = (bf16[32,4096]{1,0:T(8,128)(2,1)S(1)}, bf16[32,4096]{1,0:T(8,128)(2,1)S(1)}, u32[]{:S(2)}, u32[]{:S(2)}) collective-permute-start(bf16[32,4096]{1,0:T(8,128)(2,1)S(1)} %slice.72), channel_id=1, source_target_pairs={{0,28},{4,0},{8,4},{12,8},{16,12},{20,16},{24,20},{28,24},{1,29},{... | collective-permute-start | bytes 786440 | tf_op jit(solution)/shard_map/ppermute | solution.py:22
  81.3 8.9 %collective-permute-start.15 = (bf16[128,128]{1,0:T(8,128)(2,1)S(1)}, bf16[128,128]{1,0:T(8,128)(2,1)S(1)}, u32[]{:S(2)}, u32[]{:S(2)}) collective-permute-start(bf16[128,128]{1,0:T(8,128)(2,1)S(1)} %get-tuple-element.86), channel_id=1, source_target_pairs={{0,2},{2,0},{1,3},{3,1},{4,6},{6,4},{5,7},{7,5},{8,10},{10,8},{9,1... | collective-permute-start | bytes 98312 | tf_op jit(solution)/shard_map/ppermute | solution.py:273
  90.9 9.8 %collective-permute-start.17 = (bf16[16,4096]{1,0:T(8,128)(2,1)S(1)}, bf16[16,4096]{1,0:T(8,128)(2,1)S(1)}, u32[]{:S(2)}, u32[]{:S(2)}) collective-permute-start(bf16[16,4096]{1,0:T(8,128)(2,1)S(1)} %get-tuple-element.85), channel_id=1, source_target_pairs={{0,4},{4,8},{8,12},{12,16},{16,20},{20,24},{24,28},{28,0},{1,5},{5... | collective-permute-start | bytes 393224 | tf_op jit(solution)/shard_map/ppermute | solution.py:22
  92.9 19.8 %collective-permute-start.19 = (bf16[16,4096]{1,0:T(8,128)(2,1)S(1)}, bf16[16,4096]{1,0:T(8,128)(2,1)S(1)}, u32[]{:S(2)}, u32[]{:S(2)}) collective-permute-start(bf16[16,4096]{1,0:T(8,128)(2,1)S(1)} %get-tuple-element.84), channel_id=1, source_target_pairs={{0,28},{4,0},{8,4},{12,8},{16,12},{20,16},{24,20},{28,24},{1,29},{... | collective-permute-start | bytes 393224 | tf_op jit(solution)/shard_map/ppermute | solution.py:22
  100.8 11.9 %collective-permute-start.18 = (bf16[16,4096]{1,0:T(8,128)(2,1)S(1)}, bf16[16,4096]{1,0:T(8,128)(2,1)S(1)}, u32[]{:S(2)}, u32[]{:S(2)}) collective-permute-start(bf16[16,4096]{1,0:T(8,128)(2,1)S(1)} %add_convert_fusion.4), channel_id=1, source_target_pairs={{0,4},{4,8},{8,12},{12,16},{16,20},{20,24},{24,28},{28,0},{1,5},{5... | collective-permute-start | bytes 393224 | tf_op jit(solution)/shard_map/ppermute | solution.py:22
  109.9 39.6 %collective-permute-start.28 = (bf16[2,128,4096]{2,1,0:T(8,128)(2,1)S(1)}, bf16[2,128,4096]{2,1,0:T(8,128)(2,1)S(1)}, u32[]{:S(2)}, u32[]{:S(2)}) collective-permute-start(bf16[2,128,4096]{2,1,0:T(8,128)(2,1)S(1)} %get-tuple-element.63), channel_id=1, source_target_pairs={{0,1},{1,0},{2,3},{3,2},{4,5},{5,4},{6,7},{7,6},{8,9},{9,8},{10,11... | collective-permute-start | bytes 6291464 | tf_op jit(solution)/shard_map/ppermute | solution.py:46
  112.8 12.7 %collective-permute-start.23 = (bf16[16,4096]{1,0:T(8,128)(2,1)S(1)}, bf16[16,4096]{1,0:T(8,128)(2,1)S(1)}, u32[]{:S(2)}, u32[]{:S(2)}) collective-permute-start(bf16[16,4096]{1,0:T(8,128)(2,1)S(1)} %get-tuple-element.82), channel_id=1, source_target_pairs={{0,28},{4,0},{8,4},{12,8},{16,12},{20,16},{24,20},{28,24},{1,29},{... | collective-permute-start | bytes 393224 | tf_op jit(solution)/shard_map/ppermute | solution.py:22
  115.5 10.0 %collective-permute-start.22 = (bf16[16,4096]{1,0:T(8,128)(2,1)S(1)}, bf16[16,4096]{1,0:T(8,128)(2,1)S(1)}, u32[]{:S(2)}, u32[]{:S(2)}) collective-permute-start(bf16[16,4096]{1,0:T(8,128)(2,1)S(1)} %get-tuple-element.83), channel_id=1, source_target_pairs={{0,4},{4,8},{8,12},{12,16},{16,20},{20,24},{24,28},{28,0},{1,5},{5... | collective-permute-start | bytes 393224 | tf_op jit(solution)/shard_map/ppermute | solution.py:22
  125.6 13.6 %collective-permute-start.26 = (bf16[16,4096]{1,0:T(8,128)(2,1)S(1)}, bf16[16,4096]{1,0:T(8,128)(2,1)S(1)}, u32[]{:S(2)}, u32[]{:S(2)}) collective-permute-start(bf16[16,4096]{1,0:T(8,128)(2,1)S(1)} %get-tuple-element.80), channel_id=1, source_target_pairs={{0,28},{4,0},{8,4},{12,8},{16,12},{20,16},{24,20},{28,24},{1,29},{... | collective-permute-start | bytes 393224 | tf_op jit(solution)/shard_map/ppermute | solution.py:22
  127.5 11.7 %collective-permute-start.25 = (bf16[16,4096]{1,0:T(8,128)(2,1)S(1)}, bf16[16,4096]{1,0:T(8,128)(2,1)S(1)}, u32[]{:S(2)}, u32[]{:S(2)}) collective-permute-start(bf16[16,4096]{1,0:T(8,128)(2,1)S(1)} %get-tuple-element.81), channel_id=1, source_target_pairs={{0,4},{4,8},{8,12},{12,16},{16,20},{20,24},{24,28},{28,0},{1,5},{5... | collective-permute-start | bytes 393224 | tf_op jit(solution)/shard_map/ppermute | solution.py:22
  139.3 9.5 %collective-permute-start.30 = (f32[1,4096]{1,0:T(1,128)S(1)}, f32[1,4096]{1,0:T(1,128)S(1)}, u32[]{:S(2)}, u32[]{:S(2)}) collective-permute-start(f32[1,4096]{1,0:T(1,128)S(1)} %add.65), channel_id=1, source_target_pairs={{0,16},{4,20},{8,24},{12,28},{16,0},{20,4},{24,8},{28,12},{1,17},{... | collective-permute-start | bytes 49160 | tf_op jit(solution)/shard_map/ppermute | solution.py:27
  149.8 15.6 %collective-permute-start.29 = (bf16[16,4096]{1,0:T(8,128)(2,1)S(1)}, bf16[16,4096]{1,0:T(8,128)(2,1)S(1)}, u32[]{:S(2)}, u32[]{:S(2)}) collective-permute-start(bf16[16,4096]{1,0:T(8,128)(2,1)S(1)} %fusion.9), channel_id=1, source_target_pairs={{0,480},{32,0},{64,32},{96,64},{128,96},{160,128},{192,160},{224,1... | collective-permute-start | bytes 393224 | tf_op jit(solution)/shard_map/ppermute | solution.py:22
  (11 other events, 117.8 us)

commit v5 on v4

--- a/solution.py
+++ b/solution.py
@@ -4,6 +4,7 @@
 from jax.experimental import pallas as pl
 from jax.experimental.pallas import tpu as pltpu
 from jax.sharding import Mesh, PartitionSpec as P
+
 
 TAPS = 3
 EPSILON = 1e-06
@@ -38,25 +39,20 @@
     return found
 
 
-def reduced(share, partial):
-    half = Y // 2
-    up, down = along(share[half], "y", 1), share[half + 1]
-    up, partial = lax.optimization_barrier((up, partial))
-    kept_val, kept_out, given, total = partial
-    taken = lax.ppermute(given, "core", SWAP)
-    beside = ((("core", 1), ("z", 1)), (("y", 1),), (("y", 2),))
-    for step in range(1, half):
-        up = along((share[half - step].astype(F32) + up.astype(F32)).astype(BF16), "y", 1)
-        if step > 1:
-            down = (share[half + step].astype(F32) + down.astype(F32)).astype(BF16)
-        down = along(down, "y", -1)
-        for axis, apart in beside[step - 1]:
-            total = with_partner(total, axis, apart)
-        up, down, total = lax.optimization_barrier((up, down, total))
-    up, taken = lax.optimization_barrier((up, taken))
-    grad_wv = (kept_val + taken[0].astype(F32)).astype(BF16)
-    grad_wo = (kept_out + taken[1].astype(F32)).astype(BF16)
-    return share[0].astype(F32) + up.astype(F32) + down.astype(F32), grad_wv, grad_wo, total
+def reduced(share, total):
+    found = {}
+
+    def send(apart):
+        found[apart] = along(share[apart], "y", apart)
+
+    for apart in range(1, Y):
+        send(apart)
+    for axis, apart in (("core", 1), ("z", 1), ("y", 1), ("y", 2)):
+        total = with_partner(total, axis, apart)
+    grad_normed = share[0].astype(F32)
+    for apart in range(1, Y):
+        grad_normed = grad_normed + found[apart].astype(F32)
+    return grad_normed, total
 
 
 def vmem_params(mib):
@@ -244,7 +240,7 @@
 
     val_core = lax.ppermute(val_weight, "core", SWAP)
     out_core = lax.ppermute(out_weight, "core", SWAP)
-    val_sent, mate_done = lax.optimization_barrier((val_weight, mate))
+    val_sent, _ = lax.optimization_barrier((val_weight, mate))
     val_z = lax.ppermute(val_sent, "z", SWAP)
     val_z_core = lax.ppermute(val_z, "core", SWAP)
     weights = lax.optimization_barrier(
@@ -268,20 +264,26 @@
     own, other, near_z, grad_filter, grad_lead = through_gate(place, kept, taken, filters, lead_rows)
     grad_tail = jnp.where(has_tail, grad_lead, jnp.zeros_like(grad_lead))
 
-    near_z_core = near_z[1]
     taken = lax.ppermute(other, "core", SWAP)
     from_z = lax.ppermute(near_z[0], "z", SWAP)
-    from_z_core = lax.ppermute(near_z_core, ("z", "core"), [(i, i ^ 3) for i in range(Z * CORE)])
+    from_z_core = lax.ppermute(near_z[1], ("z", "core"), [(i, i ^ 3) for i in range(Z * CORE)])
+    partial = weight_gradients(found, own, taken, (val_weight, val_core), gain_row[None], rows)
+    from_z, from_z_core, partial = lax.optimization_barrier((from_z, from_z_core, partial))
+    kept_val, kept_out, given, gain_term = partial
+
     share = contract(
         jnp.concatenate([own[0, 0], taken[0, 0], from_z, from_z_core], axis=1), val_weights, ((1,), (0,))
     )
-    partial = weight_gradients(found, own, taken, (val_weight, val_core), gain_row[None], rows)
-    grad_normed, grad_wv, grad_wo, gain_term = reduced(share.astype(BF16).reshape(Y, rows, width), partial)
+    grad_normed, gain_term = reduced(share.astype(BF16).reshape(Y, rows, width), gain_term)
+    taken = lax.ppermute(given, "core", SWAP)
+    cot_late, taken = lax.optimization_barrier((cot_rows, taken))
+    grad_wv = (kept_val + taken[0].astype(F32)).astype(BF16)
+    grad_wo = (kept_out + taken[1].astype(F32)).astype(BF16)
     grad_gain = with_partner(gain_term, "y", 4)
 
     scaled = gain_row * grad_normed
     grad_local = (
-        cot_rows.astype(F32)
+        cot_late.astype(F32)
         + inv_rms * scaled
         - x_float * inv_rms**3 * jnp.mean(scaled * x_float, axis=-1, keepdims=True)
     )
@@ -302,6 +304,7 @@
     by_rows = P("section", TENSOR, None)
     by_columns = P("section", None, TENSOR)
     whole = P("section", None)
+
     return jax.shard_map(
         on_device,
         mesh=split,

time: 167 us -> 194 us (1.16)
  the two profiles are of different devices: /device:TPU:24 before, /device:TPU:1 now
where the time goes in v5:
time: 194 us; the launch traced here: 193 us
  starting transfers between devices  115 us (59%)
  waiting for transfers between devices  45.6 us (24%)
  matrix products  13.2 us (7%)
  other arithmetic  10.7 us (6%)
  Pallas kernels  4.9 us (3%)
  local copies, waits for them, and re-layouts  2.04 us (1%)
    ppermute x16, starting transfers between devices, along(): lax.ppermute(block, axis, [(i, (i + distance) % devices) for i in range(d...  62 us
    ppermute x16, waiting for transfers between devices, along(): lax.ppermute(block, axis, [(i, (i + distance) % devices) for i in range(d...  29.5 us
    ppermute x5, starting transfers between devices, with_partner(): return total + lax.ppermute(total, axis, [(i, i ^ apart) for i in devices])  18 us
    dot_general x10, matrix products, contract(): lax.dot_general(left, right, (dims, ((), ())), preferred_element_type=F32)  13.2 us
    ppermute x5, waiting for transfers between devices, with_partner(): return total + lax.ppermute(total, axis, [(i, i ^ apart) for i in devices])  8.41 us
    ppermute x2, starting transfers between devices, on_device(): taken = lax.ppermute(given, 'core', SWAP)  6.28 us
    ppermute x1, starting transfers between devices, on_device(): out_core = lax.ppermute(out_weight, 'core', SWAP)  5.85 us
    ppermute x1, waiting for transfers between devices, on_device(): val_z = lax.ppermute(val_sent, 'z', SWAP)  5.81 us
  transfers between devices with their start and end apart: 31, of which 14 were waited for; matrix products, arithmetic and copies ran while one was open for 11% of the time, Pallas kernels for 2%

profile of v5, /device:TPU:1, one launch (start us, length us, event | category | flops | bytes accessed | tf_op | source)
XLA Modules:
  0.0 193.0 jit_solution(1671795409084246950)
XLA Ops:
  3.6 4.8 %collective-permute-start.1 = (bf16[32,4096]{1,0:T(8,128)(2,1)S(1)}, bf16[32,4096]{1,0:T(8,128)(2,1)S(1)}, u32[]{:S(2)}, u32[]{:S(2)}) collective-permute-start(bf16[32,4096]{1,0:T(8,128)(2,1)S(1)} %pad_maximum_fusion.4), channel_id=1, source_target_pairs={{0,2},{2,0},{1,3},{3,1},{4,6},{6,4},{5,7},{7,5},{8,10},{10,8},{9,1... | collective-permute-start | bytes 786440 | tf_op jit(solution)/shard_map/ppermute | solution.py:238
  8.5 5.9 %collective-permute-start.4 = (bf16[128,4096]{1,0:T(8,128)(2,1)}, bf16[128,4096]{1,0:T(8,128)(2,1)}, u32[]{:S(2)}, u32[]{:S(2)}) collective-permute-start(bf16[128,4096]{1,0:T(8,128)(2,1)} %bitcast.75), channel_id=1, source_target_pairs={{0,1},{1,0},{2,3},{3,2},{4,5},{5,4},{6,7},{7,6},{8,9},{9,8},{10,11... | collective-permute-start | bytes 3145736 | tf_op jit(solution)/shard_map/ppermute | solution.py:242
  17.2 3.3 %collective-permute-start.5 = (bf16[64,4096]{1,0:T(8,128)(2,1)S(1)}, bf16[64,4096]{1,0:T(8,128)(2,1)S(1)}, u32[]{:S(2)}, u32[]{:S(2)}) collective-permute-start(bf16[64,4096]{1,0:T(8,128)(2,1)S(1)} %pad_maximum_fusion.3.refs_0_), channel_id=1, source_target_pairs={{0,28},{4,0},{8,4},{12,8},{16,12},{20,16},{24,20},{28,24},{1,29},{... | collective-permute-start | bytes 1572872 | tf_op jit(solution)/shard_map/ppermute | solution.py:23
  24.6 3.6 %collective-permute-start.2 = (bf16[128,4096]{1,0:T(8,128)(2,1)}, bf16[128,4096]{1,0:T(8,128)(2,1)S(1)}, u32[]{:S(2)}, u32[]{:S(2)}) collective-permute-start(bf16[128,4096]{1,0:T(8,128)(2,1)} %bitcast.63), channel_id=1, source_target_pairs={{0,2},{2,0},{1,3},{3,1},{4,6},{6,4},{5,7},{7,5},{8,10},{10,8},{9,1... | collective-permute-start | bytes 3145736 | tf_op jit(solution)/shard_map/ppermute | solution.py:244
  30.5 5.3 %collective-permute-start.6 = (bf16[64,4096]{1,0:T(8,128)(2,1)S(1)}, bf16[64,4096]{1,0:T(8,128)(2,1)S(1)}, u32[]{:S(2)}, u32[]{:S(2)}) collective-permute-start(bf16[64,4096]{1,0:T(8,128)(2,1)S(1)} %collective-permute-done.5.refs_1_), channel_id=1, source_target_pairs={{0,28},{4,0},{8,4},{12,8},{16,12},{20,16},{24,20},{28,24},{1,29},{... | collective-permute-start | bytes 1572872 | tf_op jit(solution)/shard_map/ppermute | solution.py:23
  44.0 5.8 %collective-permute-done.2 = bf16[128,4096]{1,0:T(8,128)(2,1)S(1)} collective-permute-done((bf16[128,4096]{1,0:T(8,128)(2,1)}, bf16[128,4096]{1,0:T(8,128)(2,1)S(1)}, u32[]{:S(2)}, u32[]{:S(2)}) %collective-permute-start.2) | collective-permute-done | bytes 1048608 | tf_op jit(solution)/shard_map/ppermute | solution.py:244
  49.9 4.6 %collective-permute-start.3 = (bf16[128,4096]{1,0:T(8,128)(2,1)S(1)}, bf16[128,4096]{1,0:T(8,128)(2,1)S(1)}, u32[]{:S(2)}, u32[]{:S(2)}) collective-permute-start(bf16[128,4096]{1,0:T(8,128)(2,1)S(1)} %collective-permute-done.2), channel_id=1, source_target_pairs={{0,1},{1,0},{2,3},{3,2},{4,5},{5,4},{6,7},{7,6},{8,9},{9,8},{10,11... | collective-permute-start | bytes 3145736 | tf_op jit(solution)/shard_map/ppermute | solution.py:245
  54.5 4.2 %collective-permute-start.7 = (bf16[64,4096]{1,0:T(8,128)(2,1)S(1)}, bf16[64,4096]{1,0:T(8,128)(2,1)S(1)}, u32[]{:S(2)}, u32[]{:S(2)}) collective-permute-start(bf16[64,4096]{1,0:T(8,128)(2,1)S(1)} %collective-permute-done.6.refs_2_), channel_id=1, source_target_pairs={{0,28},{4,0},{8,4},{12,8},{16,12},{20,16},{24,20},{28,24},{1,29},{... | collective-permute-start | bytes 1572872 | tf_op jit(solution)/shard_map/ppermute | solution.py:23
  63.4 6.5 %collective-permute-done.7.refs_3_ = bf16[64,4096]{1,0:T(8,128)(2,1)S(1)} collective-permute-done((bf16[64,4096]{1,0:T(8,128)(2,1)S(1)}, bf16[64,4096]{1,0:T(8,128)(2,1)S(1)}, u32[]{:S(2)}, u32[]{:S(2)}) %collective-permute-start.7) | collective-permute-done | bytes 524320 | tf_op jit(solution)/shard_map/ppermute | solution.py:23
  69.9 5.3 %collective-permute-start.8 = (bf16[32,4096]{1,0:T(8,128)(2,1)S(1)}, bf16[32,4096]{1,0:T(8,128)(2,1)S(1)}, u32[]{:S(2)}, u32[]{:S(2)}) collective-permute-start(bf16[32,4096]{1,0:T(8,128)(2,1)S(1)} %slice.72), channel_id=1, source_target_pairs={{0,28},{4,0},{8,4},{12,8},{16,12},{20,16},{24,20},{28,24},{1,29},{... | collective-permute-start | bytes 786440 | tf_op jit(solution)/shard_map/ppermute | solution.py:23
  81.4 3.7 %collective-permute-done.12.refs_5_ = bf16[32,4096]{1,0:T(8,128)(2,1)S(1)} collective-permute-done((bf16[32,4096]{1,0:T(8,128)(2,1)S(1)}, bf16[32,4096]{1,0:T(8,128)(2,1)S(1)}, u32[]{:S(2)}, u32[]{:S(2)}) %collective-permute-start.12) | collective-permute-done | bytes 262176 | tf_op jit(solution)/shard_map/ppermute | solution.py:23
  86.5 4.1 %collective-permute-start.13 = (f32[2,2,8,16,128]{4,3,2,1,0:T(8,128)S(1)}, f32[2,2,8,16,128]{4,3,2,1,0:T(8,128)S(1)}, u32[]{:S(2)}, u32[]{:S(2)}) collective-permute-start(f32[2,2,8,16,128]{4,3,2,1,0:T(8,128)S(1)} %get-tuple-element.37), channel_id=1, source_target_pairs={{0,1},{1,0},{2,3},{3,2},{4,5},{5,4},{6,7},{7,6},{8,9},{9,8},{10,11... | collective-permute-start | bytes 786440 | tf_op jit(solution)/shard_map/ppermute | solution.py:257
  92.7 3.1 %collective-permute-start.14 = (bf16[128,128]{1,0:T(8,128)(2,1)S(1)}, bf16[128,128]{1,0:T(8,128)(2,1)S(1)}, u32[]{:S(2)}, u32[]{:S(2)}) collective-permute-start(bf16[128,128]{1,0:T(8,128)(2,1)S(1)} %get-tuple-element.74), channel_id=1, source_target_pairs={{0,2},{2,0},{1,3},{3,1},{4,6},{6,4},{5,7},{7,5},{8,10},{10,8},{9,1... | collective-permute-start | bytes 98312 | tf_op jit(solution)/shard_map/ppermute | solution.py:268
  101.7 3.8 %weight_gradients.1 = (f32[128,4096]{1,0:T(8,128)S(1)}, f32[128,4096]{1,0:T(8,128)S(1)}, bf16[2,128,4096]{2,1,0:T(8,128)(2,1)S(1)}, f32[1,4096]{1,0:T(1,128)S(1)}) custom-call(bf16[64,4096]{1,0:T(8,128)(2,1)S(1)} %pad_maximum_fusion.3.refs_0_, bf16[64,4096]{1,0:T(8,128)(2,1)S(1)} %collective-permute-done.5.refs_1_, ...), custom_call_target="tpu_custom_call" | custom-call | flops 1073741824 | bytes 13631488 | tf_op jit(solution)/shard_map/weight_gradients/pallas_call | solution.py:207
  112.9 4.3 %collective-permute-start.22 = (bf16[16,4096]{1,0:T(8,128)(2,1)S(1)}, bf16[16,4096]{1,0:T(8,128)(2,1)S(1)}, u32[]{:S(2)}, u32[]{:S(2)}) collective-permute-start(bf16[16,4096]{1,0:T(8,128)(2,1)S(1)} %get-tuple-element.69), channel_id=1, source_target_pairs={{0,20},{4,24},{8,28},{12,0},{16,4},{20,8},{24,12},{28,16},{1,21},{... | collective-permute-start | bytes 393224 | tf_op jit(solution)/shard_map/ppermute | solution.py:23
  125.7 3.1 %collective-permute-start.28 = (f32[1,4096]{1,0:T(1,128)S(1)}, f32[1,4096]{1,0:T(1,128)S(1)}, u32[]{:S(2)}, u32[]{:S(2)}) collective-permute-start(f32[1,4096]{1,0:T(1,128)S(1)} %add.68), channel_id=1, source_target_pairs={{0,4},{4,0},{8,12},{12,8},{16,20},{20,16},{24,28},{28,24},{1,5},{5... | collective-permute-start | bytes 49160 | tf_op jit(solution)/shard_map/ppermute | solution.py:28
  130.5 4.2 %collective-permute-start.29 = (f32[1,4096]{1,0:T(1,128)S(1)}, f32[1,4096]{1,0:T(1,128)S(1)}, u32[]{:S(2)}, u32[]{:S(2)}) collective-permute-start(f32[1,4096]{1,0:T(1,128)S(1)} %add.69), channel_id=1, source_target_pairs={{0,8},{4,12},{8,0},{12,4},{16,24},{20,28},{24,16},{28,20},{1,9},{5... | collective-permute-start | bytes 49160 | tf_op jit(solution)/shard_map/ppermute | solution.py:28
  135.9 4.7 %collective-permute-start.30 = (f32[1,4096]{1,0:T(1,128)S(1)}, f32[1,4096]{1,0:T(1,128)S(1)}, u32[]{:S(2)}, u32[]{:S(2)}) collective-permute-start(f32[1,4096]{1,0:T(1,128)S(1)} %add.70), channel_id=1, source_target_pairs={{0,16},{4,20},{8,24},{12,28},{16,0},{20,4},{24,8},{28,12},{1,17},{... | collective-permute-start | bytes 49160 | tf_op jit(solution)/shard_map/ppermute | solution.py:28
  144.3 4.7 %collective-permute-start.21 = (bf16[16,4096]{1,0:T(8,128)(2,1)S(1)}, bf16[16,4096]{1,0:T(8,128)(2,1)S(1)}, u32[]{:S(2)}, u32[]{:S(2)}) collective-permute-start(bf16[16,4096]{1,0:T(8,128)(2,1)S(1)} %get-tuple-element.70), channel_id=1, source_target_pairs={{0,16},{4,20},{8,24},{12,28},{16,0},{20,4},{24,8},{28,12},{1,17},{... | collective-permute-start | bytes 393224 | tf_op jit(solution)/shard_map/ppermute | solution.py:23
  149.0 4.3 %collective-permute-start.20 = (bf16[16,4096]{1,0:T(8,128)(2,1)S(1)}, bf16[16,4096]{1,0:T(8,128)(2,1)S(1)}, u32[]{:S(2)}, u32[]{:S(2)}) collective-permute-start(bf16[16,4096]{1,0:T(8,128)(2,1)S(1)} %get-tuple-element.71), channel_id=1, source_target_pairs={{0,12},{4,16},{8,20},{12,24},{16,28},{20,0},{24,4},{28,8},{1,13},{... | collective-permute-start | bytes 393224 | tf_op jit(solution)/shard_map/ppermute | solution.py:23
  156.3 3.6 %collective-permute-start.18 = (bf16[16,4096]{1,0:T(8,128)(2,1)S(1)}, bf16[16,4096]{1,0:T(8,128)(2,1)S(1)}, u32[]{:S(2)}, u32[]{:S(2)}) collective-permute-start(bf16[16,4096]{1,0:T(8,128)(2,1)S(1)} %get-tuple-element.66), channel_id=1, source_target_pairs={{0,4},{4,8},{8,12},{12,16},{16,20},{20,24},{24,28},{28,0},{1,5},{5... | collective-permute-start | bytes 393224 | tf_op jit(solution)/shard_map/ppermute | solution.py:23
  161.1 6.2 %collective-permute-done.19 = bf16[16,4096]{1,0:T(8,128)(2,1)S(1)} collective-permute-done((bf16[16,4096]{1,0:T(8,128)(2,1)S(1)}, bf16[16,4096]{1,0:T(8,128)(2,1)S(1)}, u32[]{:S(2)}, u32[]{:S(2)}) %collective-permute-start.19) | collective-permute-done | bytes 131104 | tf_op jit(solution)/shard_map/ppermute | solution.py:23
  167.3 7.7 %collective-permute-done.18 = bf16[16,4096]{1,0:T(8,128)(2,1)S(1)} collective-permute-done((bf16[16,4096]{1,0:T(8,128)(2,1)S(1)}, bf16[16,4096]{1,0:T(8,128)(2,1)S(1)}, u32[]{:S(2)}, u32[]{:S(2)}) %collective-permute-start.18) | collective-permute-done | bytes 131104 | tf_op jit(solution)/shard_map/ppermute | solution.py:23
  175.5 11.9 %collective-permute-start.25 = (bf16[16,4096]{1,0:T(8,128)(2,1)S(1)}, bf16[16,4096]{1,0:T(8,128)(2,1)S(1)}, u32[]{:S(2)}, u32[]{:S(2)}) collective-permute-start(bf16[16,4096]{1,0:T(8,128)(2,1)S(1)} %fusion.9), channel_id=1, source_target_pairs={{0,480},{32,0},{64,32},{96,64},{128,96},{160,128},{192,160},{224,1... | collective-permute-start | bytes 393224 | tf_op jit(solution)/shard_map/ppermute | solution.py:23
  (87 shorter events, 72.3 us)
Async XLA Ops:
  3.6 12.6 %collective-permute-start.1 = (bf16[32,4096]{1,0:T(8,128)(2,1)S(1)}, bf16[32,4096]{1,0:T(8,128)(2,1)S(1)}, u32[]{:S(2)}, u32[]{:S(2)}) collective-permute-start(bf16[32,4096]{1,0:T(8,128)(2,1)S(1)} %pad_maximum_fusion.4), channel_id=1, source_target_pairs={{0,2},{2,0},{1,3},{3,1},{4,6},{6,4},{5,7},{7,5},{8,10},{10,8},{9,1... | collective-permute-start | bytes 786440 | tf_op jit(solution)/shard_map/ppermute | solution.py:238
  8.5 29.3 %collective-permute-start.4 = (bf16[128,4096]{1,0:T(8,128)(2,1)}, bf16[128,4096]{1,0:T(8,128)(2,1)}, u32[]{:S(2)}, u32[]{:S(2)}) collective-permute-start(bf16[128,4096]{1,0:T(8,128)(2,1)} %bitcast.75), channel_id=1, source_target_pairs={{0,1},{1,0},{2,3},{3,2},{4,5},{5,4},{6,7},{7,6},{8,9},{9,8},{10,11... | collective-permute-start | bytes 3145736 | tf_op jit(solution)/shard_map/ppermute | solution.py:242
  14.3 23.5 %collective-permute-start = (bf16[128,4096]{1,0:T(8,128)(2,1)}, bf16[128,4096]{1,0:T(8,128)(2,1)S(1)}, u32[]{:S(2)}, u32[]{:S(2)}) collective-permute-start(bf16[128,4096]{1,0:T(8,128)(2,1)} %bitcast.62), channel_id=1, source_target_pairs={{0,1},{1,0},{2,3},{3,2},{4,5},{5,4},{6,7},{7,6},{8,9},{9,8},{10,11... | collective-permute-start | bytes 3145736 | tf_op jit(solution)/shard_map/ppermute | solution.py:241
  17.2 13.3 %collective-permute-start.5 = (bf16[64,4096]{1,0:T(8,128)(2,1)S(1)}, bf16[64,4096]{1,0:T(8,128)(2,1)S(1)}, u32[]{:S(2)}, u32[]{:S(2)}) collective-permute-start(bf16[64,4096]{1,0:T(8,128)(2,1)S(1)} %pad_maximum_fusion.3.refs_0_), channel_id=1, source_target_pairs={{0,28},{4,0},{8,4},{12,8},{16,12},{20,16},{24,20},{28,24},{1,29},{... | collective-permute-start | bytes 1572872 | tf_op jit(solution)/shard_map/ppermute | solution.py:23
  20.5 15.3 %collective-permute-start.9 = (bf16[64,4096]{1,0:T(8,128)(2,1)S(1)}, bf16[64,4096]{1,0:T(8,128)(2,1)S(1)}, u32[]{:S(2)}, u32[]{:S(2)}) collective-permute-start(bf16[64,4096]{1,0:T(8,128)(2,1)S(1)} %pad_maximum_fusion.3.refs_0_), channel_id=1, source_target_pairs={{0,4},{4,8},{8,12},{12,16},{16,20},{20,24},{24,28},{28,0},{1,5},{5... | collective-permute-start | bytes 1572872 | tf_op jit(solution)/shard_map/ppermute | solution.py:23
  24.6 25.3 %collective-permute-start.2 = (bf16[128,4096]{1,0:T(8,128)(2,1)}, bf16[128,4096]{1,0:T(8,128)(2,1)S(1)}, u32[]{:S(2)}, u32[]{:S(2)}) collective-permute-start(bf16[128,4096]{1,0:T(8,128)(2,1)} %bitcast.63), channel_id=1, source_target_pairs={{0,2},{2,0},{1,3},{3,1},{4,6},{6,4},{5,7},{7,5},{8,10},{10,8},{9,1... | collective-permute-start | bytes 3145736 | tf_op jit(solution)/shard_map/ppermute | solution.py:244
  30.5 23.9 %collective-permute-start.6 = (bf16[64,4096]{1,0:T(8,128)(2,1)S(1)}, bf16[64,4096]{1,0:T(8,128)(2,1)S(1)}, u32[]{:S(2)}, u32[]{:S(2)}) collective-permute-start(bf16[64,4096]{1,0:T(8,128)(2,1)S(1)} %collective-permute-done.5.refs_1_), channel_id=1, source_target_pairs={{0,28},{4,0},{8,4},{12,8},{16,12},{20,16},{24,20},{28,24},{1,29},{... | collective-permute-start | bytes 1572872 | tf_op jit(solution)/shard_map/ppermute | solution.py:23
  35.8 22.8 %collective-permute-start.10 = (bf16[64,4096]{1,0:T(8,128)(2,1)S(1)}, bf16[64,4096]{1,0:T(8,128)(2,1)S(1)}, u32[]{:S(2)}, u32[]{:S(2)}) collective-permute-start(bf16[64,4096]{1,0:T(8,128)(2,1)S(1)} %collective-permute-done.9.refs_8_), channel_id=1, source_target_pairs={{0,4},{4,8},{8,12},{12,16},{16,20},{20,24},{24,28},{28,0},{1,5},{5... | collective-permute-start | bytes 1572872 | tf_op jit(solution)/shard_map/ppermute | solution.py:23
  49.9 40.8 %collective-permute-start.3 = (bf16[128,4096]{1,0:T(8,128)(2,1)S(1)}, bf16[128,4096]{1,0:T(8,128)(2,1)S(1)}, u32[]{:S(2)}, u32[]{:S(2)}) collective-permute-start(bf16[128,4096]{1,0:T(8,128)(2,1)S(1)} %collective-permute-done.2), channel_id=1, source_target_pairs={{0,1},{1,0},{2,3},{3,2},{4,5},{5,4},{6,7},{7,6},{8,9},{9,8},{10,11... | collective-permute-start | bytes 3145736 | tf_op jit(solution)/shard_map/ppermute | solution.py:245
  54.5 15.5 %collective-permute-start.7 = (bf16[64,4096]{1,0:T(8,128)(2,1)S(1)}, bf16[64,4096]{1,0:T(8,128)(2,1)S(1)}, u32[]{:S(2)}, u32[]{:S(2)}) collective-permute-start(bf16[64,4096]{1,0:T(8,128)(2,1)S(1)} %collective-permute-done.6.refs_2_), channel_id=1, source_target_pairs={{0,28},{4,0},{8,4},{12,8},{16,12},{20,16},{24,20},{28,24},{1,29},{... | collective-permute-start | bytes 1572872 | tf_op jit(solution)/shard_map/ppermute | solution.py:23
  58.7 16.6 %collective-permute-start.11 = (bf16[64,4096]{1,0:T(8,128)(2,1)S(1)}, bf16[64,4096]{1,0:T(8,128)(2,1)S(1)}, u32[]{:S(2)}, u32[]{:S(2)}) collective-permute-start(bf16[64,4096]{1,0:T(8,128)(2,1)S(1)} %collective-permute-done.10.refs_7_), channel_id=1, source_target_pairs={{0,4},{4,8},{8,12},{12,16},{16,20},{20,24},{24,28},{28,0},{1,5},{5... | collective-permute-start | bytes 1572872 | tf_op jit(solution)/shard_map/ppermute | solution.py:23
  69.9 10.1 %collective-permute-start.8 = (bf16[32,4096]{1,0:T(8,128)(2,1)S(1)}, bf16[32,4096]{1,0:T(8,128)(2,1)S(1)}, u32[]{:S(2)}, u32[]{:S(2)}) collective-permute-start(bf16[32,4096]{1,0:T(8,128)(2,1)S(1)} %slice.72), channel_id=1, source_target_pairs={{0,28},{4,0},{8,4},{12,8},{16,12},{20,16},{24,20},{28,24},{1,29},{... | collective-permute-start | bytes 786440 | tf_op jit(solution)/shard_map/ppermute | solution.py:23
  75.3 9.8 %collective-permute-start.12 = (bf16[32,4096]{1,0:T(8,128)(2,1)S(1)}, bf16[32,4096]{1,0:T(8,128)(2,1)S(1)}, u32[]{:S(2)}, u32[]{:S(2)}) collective-permute-start(bf16[32,4096]{1,0:T(8,128)(2,1)S(1)} %slice.73), channel_id=1, source_target_pairs={{0,4},{4,8},{8,12},{12,16},{16,20},{20,24},{24,28},{28,0},{1,5},{5... | collective-permute-start | bytes 786440 | tf_op jit(solution)/shard_map/ppermute | solution.py:23
  92.7 12.9 %collective-permute-start.14 = (bf16[128,128]{1,0:T(8,128)(2,1)S(1)}, bf16[128,128]{1,0:T(8,128)(2,1)S(1)}, u32[]{:S(2)}, u32[]{:S(2)}) collective-permute-start(bf16[128,128]{1,0:T(8,128)(2,1)S(1)} %get-tuple-element.74), channel_id=1, source_target_pairs={{0,2},{2,0},{1,3},{3,1},{4,6},{6,4},{5,7},{7,5},{8,10},{10,8},{9,1... | collective-permute-start | bytes 98312 | tf_op jit(solution)/shard_map/ppermute | solution.py:268
  95.7 9.8 %collective-permute-start.15 = (bf16[128,128]{1,0:T(8,128)(2,1)S(1)}, bf16[128,128]{1,0:T(8,128)(2,1)S(1)}, u32[]{:S(2)}, u32[]{:S(2)}) collective-permute-start(bf16[128,128]{1,0:T(8,128)(2,1)S(1)} %get-tuple-element.73), channel_id=1, source_target_pairs={{0,3},{1,2},{2,1},{3,0},{4,7},{5,6},{6,5},{7,4},{8,11},{9,10},{10,... | collective-permute-start | bytes 98312 | tf_op jit(solution)/shard_map/ppermute | solution.py:269
  105.6 69.7 %collective-permute-start.17 = (bf16[2,128,4096]{2,1,0:T(8,128)(2,1)S(1)}, bf16[2,128,4096]{2,1,0:T(8,128)(2,1)S(1)}, u32[]{:S(2)}, u32[]{:S(2)}) collective-permute-start(bf16[2,128,4096]{2,1,0:T(8,128)(2,1)S(1)} %get-tuple-element.45), channel_id=1, source_target_pairs={{0,1},{1,0},{2,3},{3,2},{4,5},{5,4},{6,7},{7,6},{8,9},{9,8},{10,11... | collective-permute-start | bytes 6291464 | tf_op jit(solution)/shard_map/ppermute | solution.py:278
  108.6 40.4 %collective-permute-start.24 = (bf16[16,4096]{1,0:T(8,128)(2,1)S(1)}, bf16[16,4096]{1,0:T(8,128)(2,1)S(1)}, u32[]{:S(2)}, u32[]{:S(2)}) collective-permute-start(bf16[16,4096]{1,0:T(8,128)(2,1)S(1)} %get-tuple-element.67), channel_id=1, source_target_pairs={{0,28},{4,0},{8,4},{12,8},{16,12},{20,16},{24,20},{28,24},{1,29},{... | collective-permute-start | bytes 393224 | tf_op jit(solution)/shard_map/ppermute | solution.py:23
  110.6 42.8 %collective-permute-start.23 = (bf16[16,4096]{1,0:T(8,128)(2,1)S(1)}, bf16[16,4096]{1,0:T(8,128)(2,1)S(1)}, u32[]{:S(2)}, u32[]{:S(2)}) collective-permute-start(bf16[16,4096]{1,0:T(8,128)(2,1)S(1)} %get-tuple-element.68), channel_id=1, source_target_pairs={{0,24},{4,28},{8,0},{12,4},{16,8},{20,12},{24,16},{28,20},{1,25},{... | collective-permute-start | bytes 393224 | tf_op jit(solution)/shard_map/ppermute | solution.py:23
  112.9 43.4 %collective-permute-start.22 = (bf16[16,4096]{1,0:T(8,128)(2,1)S(1)}, bf16[16,4096]{1,0:T(8,128)(2,1)S(1)}, u32[]{:S(2)}, u32[]{:S(2)}) collective-permute-start(bf16[16,4096]{1,0:T(8,128)(2,1)S(1)} %get-tuple-element.69), channel_id=1, source_target_pairs={{0,20},{4,24},{8,28},{12,0},{16,4},{20,8},{24,12},{28,16},{1,21},{... | collective-permute-start | bytes 393224 | tf_op jit(solution)/shard_map/ppermute | solution.py:23
  144.3 16.9 %collective-permute-start.21 = (bf16[16,4096]{1,0:T(8,128)(2,1)S(1)}, bf16[16,4096]{1,0:T(8,128)(2,1)S(1)}, u32[]{:S(2)}, u32[]{:S(2)}) collective-permute-start(bf16[16,4096]{1,0:T(8,128)(2,1)S(1)} %get-tuple-element.70), channel_id=1, source_target_pairs={{0,16},{4,20},{8,24},{12,28},{16,0},{20,4},{24,8},{28,12},{1,17},{... | collective-permute-start | bytes 393224 | tf_op jit(solution)/shard_map/ppermute | solution.py:23
  149.0 12.1 %collective-permute-start.20 = (bf16[16,4096]{1,0:T(8,128)(2,1)S(1)}, bf16[16,4096]{1,0:T(8,128)(2,1)S(1)}, u32[]{:S(2)}, u32[]{:S(2)}) collective-permute-start(bf16[16,4096]{1,0:T(8,128)(2,1)S(1)} %get-tuple-element.71), channel_id=1, source_target_pairs={{0,12},{4,16},{8,20},{12,24},{16,28},{20,0},{24,4},{28,8},{1,13},{... | collective-permute-start | bytes 393224 | tf_op jit(solution)/shard_map/ppermute | solution.py:23
  153.3 14.0 %collective-permute-start.19 = (bf16[16,4096]{1,0:T(8,128)(2,1)S(1)}, bf16[16,4096]{1,0:T(8,128)(2,1)S(1)}, u32[]{:S(2)}, u32[]{:S(2)}) collective-permute-start(bf16[16,4096]{1,0:T(8,128)(2,1)S(1)} %get-tuple-element.72), channel_id=1, source_target_pairs={{0,8},{4,12},{8,16},{12,20},{16,24},{20,28},{24,0},{28,4},{1,9},{5... | collective-permute-start | bytes 393224 | tf_op jit(solution)/shard_map/ppermute | solution.py:23
  156.3 18.7 %collective-permute-start.18 = (bf16[16,4096]{1,0:T(8,128)(2,1)S(1)}, bf16[16,4096]{1,0:T(8,128)(2,1)S(1)}, u32[]{:S(2)}, u32[]{:S(2)}) collective-permute-start(bf16[16,4096]{1,0:T(8,128)(2,1)S(1)} %get-tuple-element.66), channel_id=1, source_target_pairs={{0,4},{4,8},{8,12},{12,16},{16,20},{20,24},{24,28},{28,0},{1,5},{5... | collective-permute-start | bytes 393224 | tf_op jit(solution)/shard_map/ppermute | solution.py:23
  175.5 16.9 %collective-permute-start.25 = (bf16[16,4096]{1,0:T(8,128)(2,1)S(1)}, bf16[16,4096]{1,0:T(8,128)(2,1)S(1)}, u32[]{:S(2)}, u32[]{:S(2)}) collective-permute-start(bf16[16,4096]{1,0:T(8,128)(2,1)S(1)} %fusion.9), channel_id=1, source_target_pairs={{0,480},{32,0},{64,32},{96,64},{128,96},{160,128},{192,160},{224,1... | collective-permute-start | bytes 393224 | tf_op jit(solution)/shard_map/ppermute | solution.py:23
  (11 other events, 127.9 us)

commit v6 on v5

--- a/solution.py
+++ b/solution.py
@@ -33,9 +33,12 @@
     found = {0: own}
     ahead = behind = own
     for step in range(1, half):
-        ahead, behind = along(ahead, "y", -1), along(behind, "y", 1)
+        behind = along(behind, "y", 1)
+        ahead = along(ahead, "y", -1)
         found[step], found[Y - step] = ahead, behind
-    found[half] = (along(ahead[:rows], "y", -1), along(behind[rows:], "y", 1))
+    behind = along(behind[rows:], "y", 1)
+    ahead = along(ahead[:rows], "y", -1)
+    found[half] = (ahead, behind)
     return found
 
 
@@ -279,7 +282,7 @@
     cot_late, taken = lax.optimization_barrier((cot_rows, taken))
     grad_wv = (kept_val + taken[0].astype(F32)).astype(BF16)
     grad_wo = (kept_out + taken[1].astype(F32)).astype(BF16)
-    grad_gain = with_partner(gain_term, "y", 4)
+    gain_other = lax.ppermute(gain_term, "y", [(i, i ^ 4) for i in range(Y)])
 
     scaled = gain_row * grad_normed
     grad_local = (
@@ -287,7 +290,10 @@
         + inv_rms * scaled
         - x_float * inv_rms**3 * jnp.mean(scaled * x_float, axis=-1, keepdims=True)
     )
-    received = along(grad_local.astype(BF16), "section", -1)
+    grad_local = grad_local.astype(BF16)
+    received = along(grad_local, "section", -1)
+    gain_other, grad_wv, grad_wo, _ = lax.optimization_barrier((gain_other, grad_wv, grad_wo, grad_local))
+    grad_gain = gain_term + gain_other
     return (
         received[None],
         grad_wv[None],

time: 194 us -> 186 us (0.959)
  waiting for transfers between devices: 45.6 us -> 37.8 us
    ppermute x0 -> x1, starting transfers between devices: none -> 4.75 us  [on_device(): gain_other = lax.ppermute(gain_term, 'y', [(i, i ^ 4) for i in range(Y)])]
    ppermute x5 -> x4, starting transfers between devices: 18 us -> 13.2 us  [with_partner(): return total + lax.ppermute(total, axis, [(i, i ^ apart) for i in devices])]
    ppermute x16, waiting for transfers between devices: 29.5 us -> 25.4 us  [along(): lax.ppermute(block, axis, [(i, (i + distance) % devices) for i in range(d...]
    ppermute x5 -> x4, waiting for transfers between devices: 8.41 us -> 4.77 us  [with_partner(): return total + lax.ppermute(total, axis, [(i, i ^ apart) for i in devices])]
  transfers between devices with their start and end apart: 31 -> 31, of which waited for: 14 -> 13; matrix products, arithmetic and copies ran while one was open for 11% -> 12% of each run, Pallas kernels for 2% -> 2%
where the time goes in v6:
time: 186 us; the launch traced here: 185 us
  starting transfers between devices  115 us (62%)
  waiting for transfers between devices  37.8 us (20%)
  matrix products  13.2 us (7%)
  other arithmetic  10.7 us (6%)
  Pallas kernels  4.91 us (3%)
  local copies, waits for them, and re-layouts  2.04 us (1%)
    ppermute x16, starting transfers between devices, along(): lax.ppermute(block, axis, [(i, (i + distance) % devices) for i in range(d...  62 us
    ppermute x16, waiting for transfers between devices, along(): lax.ppermute(block, axis, [(i, (i + distance) % devices) for i in range(d...  25.4 us
    ppermute x4, starting transfers between devices, with_partner(): return total + lax.ppermute(total, axis, [(i, i ^ apart) for i in devices])  13.2 us
    dot_general x10, matrix products, contract(): lax.dot_general(left, right, (dims, ((), ())), preferred_element_type=F32)  13.2 us
    ppermute x2, starting transfers between devices, on_device(): taken = lax.ppermute(given, 'core', SWAP)  6.28 us
    ppermute x1, starting transfers between devices, on_device(): out_core = lax.ppermute(out_weight, 'core', SWAP)  5.85 us
    ppermute x1, waiting for transfers between devices, on_device(): val_z = lax.ppermute(val_sent, 'z', SWAP)  5.81 us
    ppermute x1, starting transfers between devices, on_device(): mate = lax.ppermute(own, 'z', SWAP)  4.82 us
  transfers between devices with their start and end apart: 31, of which 13 were waited for; matrix products, arithmetic and copies ran while one was open for 12% of the time, Pallas kernels for 2%

profile of v6, /device:TPU:1, one launch (start us, length us, event | category | flops | bytes accessed | tf_op | source)
XLA Modules:
  0.0 185.3 jit_solution(11152583181979467217)
XLA Ops:
  3.6 4.8 %collective-permute-start.1 = (bf16[32,4096]{1,0:T(8,128)(2,1)S(1)}, bf16[32,4096]{1,0:T(8,128)(2,1)S(1)}, u32[]{:S(2)}, u32[]{:S(2)}) collective-permute-start(bf16[32,4096]{1,0:T(8,128)(2,1)S(1)} %pad_maximum_fusion.4), channel_id=1, source_target_pairs={{0,2},{2,0},{1,3},{3,1},{4,6},{6,4},{5,7},{7,5},{8,10},{10,8},{9,1... | collective-permute-start | bytes 786440 | tf_op jit(solution)/shard_map/ppermute | solution.py:241
  8.5 5.9 %collective-permute-start.4 = (bf16[128,4096]{1,0:T(8,128)(2,1)}, bf16[128,4096]{1,0:T(8,128)(2,1)}, u32[]{:S(2)}, u32[]{:S(2)}) collective-permute-start(bf16[128,4096]{1,0:T(8,128)(2,1)} %bitcast.73), channel_id=1, source_target_pairs={{0,1},{1,0},{2,3},{3,2},{4,5},{5,4},{6,7},{7,6},{8,9},{9,8},{10,11... | collective-permute-start | bytes 3145736 | tf_op jit(solution)/shard_map/ppermute | solution.py:245
  17.2 3.3 %collective-permute-start.5 = (bf16[64,4096]{1,0:T(8,128)(2,1)S(1)}, bf16[64,4096]{1,0:T(8,128)(2,1)S(1)}, u32[]{:S(2)}, u32[]{:S(2)}) collective-permute-start(bf16[64,4096]{1,0:T(8,128)(2,1)S(1)} %pad_maximum_fusion.3.refs_0_), channel_id=1, source_target_pairs={{0,28},{4,0},{8,4},{12,8},{16,12},{20,16},{24,20},{28,24},{1,29},{... | collective-permute-start | bytes 1572872 | tf_op jit(solution)/shard_map/ppermute | solution.py:23
  24.6 3.6 %collective-permute-start.2 = (bf16[128,4096]{1,0:T(8,128)(2,1)}, bf16[128,4096]{1,0:T(8,128)(2,1)S(1)}, u32[]{:S(2)}, u32[]{:S(2)}) collective-permute-start(bf16[128,4096]{1,0:T(8,128)(2,1)} %bitcast.61), channel_id=1, source_target_pairs={{0,2},{2,0},{1,3},{3,1},{4,6},{6,4},{5,7},{7,5},{8,10},{10,8},{9,1... | collective-permute-start | bytes 3145736 | tf_op jit(solution)/shard_map/ppermute | solution.py:247
  30.5 5.3 %collective-permute-start.6 = (bf16[64,4096]{1,0:T(8,128)(2,1)S(1)}, bf16[64,4096]{1,0:T(8,128)(2,1)S(1)}, u32[]{:S(2)}, u32[]{:S(2)}) collective-permute-start(bf16[64,4096]{1,0:T(8,128)(2,1)S(1)} %collective-permute-done.5.refs_1_), channel_id=1, source_target_pairs={{0,28},{4,0},{8,4},{12,8},{16,12},{20,16},{24,20},{28,24},{1,29},{... | collective-permute-start | bytes 1572872 | tf_op jit(solution)/shard_map/ppermute | solution.py:23
  44.0 5.8 %collective-permute-done.2 = bf16[128,4096]{1,0:T(8,128)(2,1)S(1)} collective-permute-done((bf16[128,4096]{1,0:T(8,128)(2,1)}, bf16[128,4096]{1,0:T(8,128)(2,1)S(1)}, u32[]{:S(2)}, u32[]{:S(2)}) %collective-permute-start.2) | collective-permute-done | bytes 1048608 | tf_op jit(solution)/shard_map/ppermute | solution.py:247
  49.9 4.6 %collective-permute-start.3 = (bf16[128,4096]{1,0:T(8,128)(2,1)S(1)}, bf16[128,4096]{1,0:T(8,128)(2,1)S(1)}, u32[]{:S(2)}, u32[]{:S(2)}) collective-permute-start(bf16[128,4096]{1,0:T(8,128)(2,1)S(1)} %collective-permute-done.2), channel_id=1, source_target_pairs={{0,1},{1,0},{2,3},{3,2},{4,5},{5,4},{6,7},{7,6},{8,9},{9,8},{10,11... | collective-permute-start | bytes 3145736 | tf_op jit(solution)/shard_map/ppermute | solution.py:248
  54.5 4.2 %collective-permute-start.7 = (bf16[64,4096]{1,0:T(8,128)(2,1)S(1)}, bf16[64,4096]{1,0:T(8,128)(2,1)S(1)}, u32[]{:S(2)}, u32[]{:S(2)}) collective-permute-start(bf16[64,4096]{1,0:T(8,128)(2,1)S(1)} %collective-permute-done.6.refs_2_), channel_id=1, source_target_pairs={{0,28},{4,0},{8,4},{12,8},{16,12},{20,16},{24,20},{28,24},{1,29},{... | collective-permute-start | bytes 1572872 | tf_op jit(solution)/shard_map/ppermute | solution.py:23
  63.4 6.5 %collective-permute-done.7.refs_3_ = bf16[64,4096]{1,0:T(8,128)(2,1)S(1)} collective-permute-done((bf16[64,4096]{1,0:T(8,128)(2,1)S(1)}, bf16[64,4096]{1,0:T(8,128)(2,1)S(1)}, u32[]{:S(2)}, u32[]{:S(2)}) %collective-permute-start.7) | collective-permute-done | bytes 524320 | tf_op jit(solution)/shard_map/ppermute | solution.py:23
  69.9 5.3 %collective-permute-start.8 = (bf16[32,4096]{1,0:T(8,128)(2,1)S(1)}, bf16[32,4096]{1,0:T(8,128)(2,1)S(1)}, u32[]{:S(2)}, u32[]{:S(2)}) collective-permute-start(bf16[32,4096]{1,0:T(8,128)(2,1)S(1)} %slice.72), channel_id=1, source_target_pairs={{0,28},{4,0},{8,4},{12,8},{16,12},{20,16},{24,20},{28,24},{1,29},{... | collective-permute-start | bytes 786440 | tf_op jit(solution)/shard_map/ppermute | solution.py:23
  81.4 3.7 %collective-permute-done.12.refs_5_ = bf16[32,4096]{1,0:T(8,128)(2,1)S(1)} collective-permute-done((bf16[32,4096]{1,0:T(8,128)(2,1)S(1)}, bf16[32,4096]{1,0:T(8,128)(2,1)S(1)}, u32[]{:S(2)}, u32[]{:S(2)}) %collective-permute-start.12) | collective-permute-done | bytes 262176 | tf_op jit(solution)/shard_map/ppermute | solution.py:23
  86.5 4.1 %collective-permute-start.13 = (f32[2,2,8,16,128]{4,3,2,1,0:T(8,128)S(1)}, f32[2,2,8,16,128]{4,3,2,1,0:T(8,128)S(1)}, u32[]{:S(2)}, u32[]{:S(2)}) collective-permute-start(f32[2,2,8,16,128]{4,3,2,1,0:T(8,128)S(1)} %get-tuple-element.40), channel_id=1, source_target_pairs={{0,1},{1,0},{2,3},{3,2},{4,5},{5,4},{6,7},{7,6},{8,9},{9,8},{10,11... | collective-permute-start | bytes 786440 | tf_op jit(solution)/shard_map/ppermute | solution.py:260
  92.7 3.1 %collective-permute-start.14 = (bf16[128,128]{1,0:T(8,128)(2,1)S(1)}, bf16[128,128]{1,0:T(8,128)(2,1)S(1)}, u32[]{:S(2)}, u32[]{:S(2)}) collective-permute-start(bf16[128,128]{1,0:T(8,128)(2,1)S(1)} %get-tuple-element.80), channel_id=1, source_target_pairs={{0,2},{2,0},{1,3},{3,1},{4,6},{6,4},{5,7},{7,5},{8,10},{10,8},{9,1... | collective-permute-start | bytes 98312 | tf_op jit(solution)/shard_map/ppermute | solution.py:271
  101.7 3.8 %weight_gradients.1 = (f32[128,4096]{1,0:T(8,128)S(1)}, f32[128,4096]{1,0:T(8,128)S(1)}, bf16[2,128,4096]{2,1,0:T(8,128)(2,1)S(1)}, f32[1,4096]{1,0:T(1,128)S(1)}) custom-call(bf16[64,4096]{1,0:T(8,128)(2,1)S(1)} %pad_maximum_fusion.3.refs_0_, bf16[64,4096]{1,0:T(8,128)(2,1)S(1)} %collective-permute-done.5.refs_1_, ...), custom_call_target="tpu_custom_call" | custom-call | flops 1073741824 | bytes 13631488 | tf_op jit(solution)/shard_map/weight_gradients/pallas_call | solution.py:210
  112.9 4.3 %collective-permute-start.22 = (bf16[16,4096]{1,0:T(8,128)(2,1)S(1)}, bf16[16,4096]{1,0:T(8,128)(2,1)S(1)}, u32[]{:S(2)}, u32[]{:S(2)}) collective-permute-start(bf16[16,4096]{1,0:T(8,128)(2,1)S(1)} %get-tuple-element.75), channel_id=1, source_target_pairs={{0,20},{4,24},{8,28},{12,0},{16,4},{20,8},{24,12},{28,16},{1,21},{... | collective-permute-start | bytes 393224 | tf_op jit(solution)/shard_map/ppermute | solution.py:23
  120.9 3.1 %collective-permute-start.27 = (f32[1,4096]{1,0:T(1,128)S(1)}, f32[1,4096]{1,0:T(1,128)S(1)}, u32[]{:S(2)}, u32[]{:S(2)}) collective-permute-start(f32[1,4096]{1,0:T(1,128)S(1)} %add.65), channel_id=1, source_target_pairs={{0,2},{2,0},{1,3},{3,1},{4,6},{6,4},{5,7},{7,5},{8,10},{10,8},{9,1... | collective-permute-start | bytes 49160 | tf_op jit(solution)/shard_map/ppermute | solution.py:28
  125.7 3.1 %collective-permute-start.28 = (f32[1,4096]{1,0:T(1,128)S(1)}, f32[1,4096]{1,0:T(1,128)S(1)}, u32[]{:S(2)}, u32[]{:S(2)}) collective-permute-start(f32[1,4096]{1,0:T(1,128)S(1)} %add.66), channel_id=1, source_target_pairs={{0,4},{4,0},{8,12},{12,8},{16,20},{20,16},{24,28},{28,24},{1,5},{5... | collective-permute-start | bytes 49160 | tf_op jit(solution)/shard_map/ppermute | solution.py:28
  130.5 4.2 %collective-permute-start.29 = (f32[1,4096]{1,0:T(1,128)S(1)}, f32[1,4096]{1,0:T(1,128)S(1)}, u32[]{:S(2)}, u32[]{:S(2)}) collective-permute-start(f32[1,4096]{1,0:T(1,128)S(1)} %add.67), channel_id=1, source_target_pairs={{0,8},{4,12},{8,0},{12,4},{16,24},{20,28},{24,16},{28,20},{1,9},{5... | collective-permute-start | bytes 49160 | tf_op jit(solution)/shard_map/ppermute | solution.py:28
  135.9 4.7 %collective-permute-start.21 = (bf16[16,4096]{1,0:T(8,128)(2,1)S(1)}, bf16[16,4096]{1,0:T(8,128)(2,1)S(1)}, u32[]{:S(2)}, u32[]{:S(2)}) collective-permute-start(bf16[16,4096]{1,0:T(8,128)(2,1)S(1)} %get-tuple-element.76), channel_id=1, source_target_pairs={{0,16},{4,20},{8,24},{12,28},{16,0},{20,4},{24,8},{28,12},{1,17},{... | collective-permute-start | bytes 393224 | tf_op jit(solution)/shard_map/ppermute | solution.py:23
  140.6 4.3 %collective-permute-start.20 = (bf16[16,4096]{1,0:T(8,128)(2,1)S(1)}, bf16[16,4096]{1,0:T(8,128)(2,1)S(1)}, u32[]{:S(2)}, u32[]{:S(2)}) collective-permute-start(bf16[16,4096]{1,0:T(8,128)(2,1)S(1)} %get-tuple-element.77), channel_id=1, source_target_pairs={{0,12},{4,16},{8,20},{12,24},{16,28},{20,0},{24,4},{28,8},{1,13},{... | collective-permute-start | bytes 393224 | tf_op jit(solution)/shard_map/ppermute | solution.py:23
  147.9 3.6 %collective-permute-start.18 = (bf16[16,4096]{1,0:T(8,128)(2,1)S(1)}, bf16[16,4096]{1,0:T(8,128)(2,1)S(1)}, u32[]{:S(2)}, u32[]{:S(2)}) collective-permute-start(bf16[16,4096]{1,0:T(8,128)(2,1)S(1)} %get-tuple-element.72), channel_id=1, source_target_pairs={{0,4},{4,8},{8,12},{12,16},{16,20},{20,24},{24,28},{28,0},{1,5},{5... | collective-permute-start | bytes 393224 | tf_op jit(solution)/shard_map/ppermute | solution.py:23
  152.2 4.8 %collective-permute-start.30 = (f32[1,4096]{1,0:T(1,128)S(1)}, f32[1,4096]{1,0:T(1,128)S(1)}, u32[]{:S(2)}, u32[]{:S(2)}) collective-permute-start(f32[1,4096]{1,0:T(1,128)S(1)} %add.68), channel_id=1, source_target_pairs={{0,16},{4,20},{8,24},{12,28},{16,0},{20,4},{24,8},{28,12},{1,17},{... | collective-permute-start | bytes 49160 | tf_op jit(solution)/shard_map/ppermute | solution.py:285
  159.3 8.1 %collective-permute-done.18 = bf16[16,4096]{1,0:T(8,128)(2,1)S(1)} collective-permute-done((bf16[16,4096]{1,0:T(8,128)(2,1)S(1)}, bf16[16,4096]{1,0:T(8,128)(2,1)S(1)}, u32[]{:S(2)}, u32[]{:S(2)}) %collective-permute-start.18) | collective-permute-done | bytes 131104 | tf_op jit(solution)/shard_map/ppermute | solution.py:23
  167.7 11.9 %collective-permute-start.25 = (bf16[16,4096]{1,0:T(8,128)(2,1)S(1)}, bf16[16,4096]{1,0:T(8,128)(2,1)S(1)}, u32[]{:S(2)}, u32[]{:S(2)}) collective-permute-start(bf16[16,4096]{1,0:T(8,128)(2,1)S(1)} %fusion.7), channel_id=1, source_target_pairs={{0,480},{32,0},{64,32},{96,64},{128,96},{160,128},{192,160},{224,1... | collective-permute-start | bytes 393224 | tf_op jit(solution)/shard_map/ppermute | solution.py:23
  (87 shorter events, 67.3 us)
Async XLA Ops:
  3.6 12.6 %collective-permute-start.1 = (bf16[32,4096]{1,0:T(8,128)(2,1)S(1)}, bf16[32,4096]{1,0:T(8,128)(2,1)S(1)}, u32[]{:S(2)}, u32[]{:S(2)}) collective-permute-start(bf16[32,4096]{1,0:T(8,128)(2,1)S(1)} %pad_maximum_fusion.4), channel_id=1, source_target_pairs={{0,2},{2,0},{1,3},{3,1},{4,6},{6,4},{5,7},{7,5},{8,10},{10,8},{9,1... | collective-permute-start | bytes 786440 | tf_op jit(solution)/shard_map/ppermute | solution.py:241
  8.5 29.3 %collective-permute-start.4 = (bf16[128,4096]{1,0:T(8,128)(2,1)}, bf16[128,4096]{1,0:T(8,128)(2,1)}, u32[]{:S(2)}, u32[]{:S(2)}) collective-permute-start(bf16[128,4096]{1,0:T(8,128)(2,1)} %bitcast.73), channel_id=1, source_target_pairs={{0,1},{1,0},{2,3},{3,2},{4,5},{5,4},{6,7},{7,6},{8,9},{9,8},{10,11... | collective-permute-start | bytes 3145736 | tf_op jit(solution)/shard_map/ppermute | solution.py:245
  14.3 23.5 %collective-permute-start = (bf16[128,4096]{1,0:T(8,128)(2,1)}, bf16[128,4096]{1,0:T(8,128)(2,1)S(1)}, u32[]{:S(2)}, u32[]{:S(2)}) collective-permute-start(bf16[128,4096]{1,0:T(8,128)(2,1)} %bitcast.60), channel_id=1, source_target_pairs={{0,1},{1,0},{2,3},{3,2},{4,5},{5,4},{6,7},{7,6},{8,9},{9,8},{10,11... | collective-permute-start | bytes 3145736 | tf_op jit(solution)/shard_map/ppermute | solution.py:244
  17.2 13.3 %collective-permute-start.5 = (bf16[64,4096]{1,0:T(8,128)(2,1)S(1)}, bf16[64,4096]{1,0:T(8,128)(2,1)S(1)}, u32[]{:S(2)}, u32[]{:S(2)}) collective-permute-start(bf16[64,4096]{1,0:T(8,128)(2,1)S(1)} %pad_maximum_fusion.3.refs_0_), channel_id=1, source_target_pairs={{0,28},{4,0},{8,4},{12,8},{16,12},{20,16},{24,20},{28,24},{1,29},{... | collective-permute-start | bytes 1572872 | tf_op jit(solution)/shard_map/ppermute | solution.py:23
  20.5 15.3 %collective-permute-start.9 = (bf16[64,4096]{1,0:T(8,128)(2,1)S(1)}, bf16[64,4096]{1,0:T(8,128)(2,1)S(1)}, u32[]{:S(2)}, u32[]{:S(2)}) collective-permute-start(bf16[64,4096]{1,0:T(8,128)(2,1)S(1)} %pad_maximum_fusion.3.refs_0_), channel_id=1, source_target_pairs={{0,4},{4,8},{8,12},{12,16},{16,20},{20,24},{24,28},{28,0},{1,5},{5... | collective-permute-start | bytes 1572872 | tf_op jit(solution)/shard_map/ppermute | solution.py:23
  24.6 25.3 %collective-permute-start.2 = (bf16[128,4096]{1,0:T(8,128)(2,1)}, bf16[128,4096]{1,0:T(8,128)(2,1)S(1)}, u32[]{:S(2)}, u32[]{:S(2)}) collective-permute-start(bf16[128,4096]{1,0:T(8,128)(2,1)} %bitcast.61), channel_id=1, source_target_pairs={{0,2},{2,0},{1,3},{3,1},{4,6},{6,4},{5,7},{7,5},{8,10},{10,8},{9,1... | collective-permute-start | bytes 3145736 | tf_op jit(solution)/shard_map/ppermute | solution.py:247
  30.5 23.9 %collective-permute-start.6 = (bf16[64,4096]{1,0:T(8,128)(2,1)S(1)}, bf16[64,4096]{1,0:T(8,128)(2,1)S(1)}, u32[]{:S(2)}, u32[]{:S(2)}) collective-permute-start(bf16[64,4096]{1,0:T(8,128)(2,1)S(1)} %collective-permute-done.5.refs_1_), channel_id=1, source_target_pairs={{0,28},{4,0},{8,4},{12,8},{16,12},{20,16},{24,20},{28,24},{1,29},{... | collective-permute-start | bytes 1572872 | tf_op jit(solution)/shard_map/ppermute | solution.py:23
  35.8 22.8 %collective-permute-start.10 = (bf16[64,4096]{1,0:T(8,128)(2,1)S(1)}, bf16[64,4096]{1,0:T(8,128)(2,1)S(1)}, u32[]{:S(2)}, u32[]{:S(2)}) collective-permute-start(bf16[64,4096]{1,0:T(8,128)(2,1)S(1)} %collective-permute-done.9.refs_8_), channel_id=1, source_target_pairs={{0,4},{4,8},{8,12},{12,16},{16,20},{20,24},{24,28},{28,0},{1,5},{5... | collective-permute-start | bytes 1572872 | tf_op jit(solution)/shard_map/ppermute | solution.py:23
  49.9 40.8 %collective-permute-start.3 = (bf16[128,4096]{1,0:T(8,128)(2,1)S(1)}, bf16[128,4096]{1,0:T(8,128)(2,1)S(1)}, u32[]{:S(2)}, u32[]{:S(2)}) collective-permute-start(bf16[128,4096]{1,0:T(8,128)(2,1)S(1)} %collective-permute-done.2), channel_id=1, source_target_pairs={{0,1},{1,0},{2,3},{3,2},{4,5},{5,4},{6,7},{7,6},{8,9},{9,8},{10,11... | collective-permute-start | bytes 3145736 | tf_op jit(solution)/shard_map/ppermute | solution.py:248
  54.5 15.5 %collective-permute-start.7 = (bf16[64,4096]{1,0:T(8,128)(2,1)S(1)}, bf16[64,4096]{1,0:T(8,128)(2,1)S(1)}, u32[]{:S(2)}, u32[]{:S(2)}) collective-permute-start(bf16[64,4096]{1,0:T(8,128)(2,1)S(1)} %collective-permute-done.6.refs_2_), channel_id=1, source_target_pairs={{0,28},{4,0},{8,4},{12,8},{16,12},{20,16},{24,20},{28,24},{1,29},{... | collective-permute-start | bytes 1572872 | tf_op jit(solution)/shard_map/ppermute | solution.py:23
  58.7 16.6 %collective-permute-start.11 = (bf16[64,4096]{1,0:T(8,128)(2,1)S(1)}, bf16[64,4096]{1,0:T(8,128)(2,1)S(1)}, u32[]{:S(2)}, u32[]{:S(2)}) collective-permute-start(bf16[64,4096]{1,0:T(8,128)(2,1)S(1)} %collective-permute-done.10.refs_7_), channel_id=1, source_target_pairs={{0,4},{4,8},{8,12},{12,16},{16,20},{20,24},{24,28},{28,0},{1,5},{5... | collective-permute-start | bytes 1572872 | tf_op jit(solution)/shard_map/ppermute | solution.py:23
  69.9 10.1 %collective-permute-start.8 = (bf16[32,4096]{1,0:T(8,128)(2,1)S(1)}, bf16[32,4096]{1,0:T(8,128)(2,1)S(1)}, u32[]{:S(2)}, u32[]{:S(2)}) collective-permute-start(bf16[32,4096]{1,0:T(8,128)(2,1)S(1)} %slice.72), channel_id=1, source_target_pairs={{0,28},{4,0},{8,4},{12,8},{16,12},{20,16},{24,20},{28,24},{1,29},{... | collective-permute-start | bytes 786440 | tf_op jit(solution)/shard_map/ppermute | solution.py:23
  92.7 12.9 %collective-permute-start.14 = (bf16[128,128]{1,0:T(8,128)(2,1)S(1)}, bf16[128,128]{1,0:T(8,128)(2,1)S(1)}, u32[]{:S(2)}, u32[]{:S(2)}) collective-permute-start(bf16[128,128]{1,0:T(8,128)(2,1)S(1)} %get-tuple-element.80), channel_id=1, source_target_pairs={{0,2},{2,0},{1,3},{3,1},{4,6},{6,4},{5,7},{7,5},{8,10},{10,8},{9,1... | collective-permute-start | bytes 98312 | tf_op jit(solution)/shard_map/ppermute | solution.py:271
  95.7 9.9 %collective-permute-start.15 = (bf16[128,128]{1,0:T(8,128)(2,1)S(1)}, bf16[128,128]{1,0:T(8,128)(2,1)S(1)}, u32[]{:S(2)}, u32[]{:S(2)}) collective-permute-start(bf16[128,128]{1,0:T(8,128)(2,1)S(1)} %get-tuple-element.79), channel_id=1, source_target_pairs={{0,3},{1,2},{2,1},{3,0},{4,7},{5,6},{6,5},{7,4},{8,11},{9,10},{10,... | collective-permute-start | bytes 98312 | tf_op jit(solution)/shard_map/ppermute | solution.py:272
  105.6 62.0 %collective-permute-start.17 = (bf16[2,128,4096]{2,1,0:T(8,128)(2,1)S(1)}, bf16[2,128,4096]{2,1,0:T(8,128)(2,1)S(1)}, u32[]{:S(2)}, u32[]{:S(2)}) collective-permute-start(bf16[2,128,4096]{2,1,0:T(8,128)(2,1)S(1)} %get-tuple-element.48), channel_id=1, source_target_pairs={{0,1},{1,0},{2,3},{3,2},{4,5},{5,4},{6,7},{7,6},{8,9},{9,8},{10,11... | collective-permute-start | bytes 6291464 | tf_op jit(solution)/shard_map/ppermute | solution.py:281
  108.6 32.0 %collective-permute-start.24 = (bf16[16,4096]{1,0:T(8,128)(2,1)S(1)}, bf16[16,4096]{1,0:T(8,128)(2,1)S(1)}, u32[]{:S(2)}, u32[]{:S(2)}) collective-permute-start(bf16[16,4096]{1,0:T(8,128)(2,1)S(1)} %get-tuple-element.73), channel_id=1, source_target_pairs={{0,28},{4,0},{8,4},{12,8},{16,12},{20,16},{24,20},{28,24},{1,29},{... | collective-permute-start | bytes 393224 | tf_op jit(solution)/shard_map/ppermute | solution.py:23
  110.6 34.3 %collective-permute-start.23 = (bf16[16,4096]{1,0:T(8,128)(2,1)S(1)}, bf16[16,4096]{1,0:T(8,128)(2,1)S(1)}, u32[]{:S(2)}, u32[]{:S(2)}) collective-permute-start(bf16[16,4096]{1,0:T(8,128)(2,1)S(1)} %get-tuple-element.74), channel_id=1, source_target_pairs={{0,24},{4,28},{8,0},{12,4},{16,8},{20,12},{24,16},{28,20},{1,25},{... | collective-permute-start | bytes 393224 | tf_op jit(solution)/shard_map/ppermute | solution.py:23
  112.9 35.0 %collective-permute-start.22 = (bf16[16,4096]{1,0:T(8,128)(2,1)S(1)}, bf16[16,4096]{1,0:T(8,128)(2,1)S(1)}, u32[]{:S(2)}, u32[]{:S(2)}) collective-permute-start(bf16[16,4096]{1,0:T(8,128)(2,1)S(1)} %get-tuple-element.75), channel_id=1, source_target_pairs={{0,20},{4,24},{8,28},{12,0},{16,4},{20,8},{24,12},{28,16},{1,21},{... | collective-permute-start | bytes 393224 | tf_op jit(solution)/shard_map/ppermute | solution.py:23
  135.9 16.3 %collective-permute-start.21 = (bf16[16,4096]{1,0:T(8,128)(2,1)S(1)}, bf16[16,4096]{1,0:T(8,128)(2,1)S(1)}, u32[]{:S(2)}, u32[]{:S(2)}) collective-permute-start(bf16[16,4096]{1,0:T(8,128)(2,1)S(1)} %get-tuple-element.76), channel_id=1, source_target_pairs={{0,16},{4,20},{8,24},{12,28},{16,0},{20,4},{24,8},{28,12},{1,17},{... | collective-permute-start | bytes 393224 | tf_op jit(solution)/shard_map/ppermute | solution.py:23
  140.6 18.6 %collective-permute-start.20 = (bf16[16,4096]{1,0:T(8,128)(2,1)S(1)}, bf16[16,4096]{1,0:T(8,128)(2,1)S(1)}, u32[]{:S(2)}, u32[]{:S(2)}) collective-permute-start(bf16[16,4096]{1,0:T(8,128)(2,1)S(1)} %get-tuple-element.77), channel_id=1, source_target_pairs={{0,12},{4,16},{8,20},{12,24},{16,28},{20,0},{24,4},{28,8},{1,13},{... | collective-permute-start | bytes 393224 | tf_op jit(solution)/shard_map/ppermute | solution.py:23
  144.9 14.3 %collective-permute-start.19 = (bf16[16,4096]{1,0:T(8,128)(2,1)S(1)}, bf16[16,4096]{1,0:T(8,128)(2,1)S(1)}, u32[]{:S(2)}, u32[]{:S(2)}) collective-permute-start(bf16[16,4096]{1,0:T(8,128)(2,1)S(1)} %get-tuple-element.78), channel_id=1, source_target_pairs={{0,8},{4,12},{8,16},{12,20},{16,24},{20,28},{24,0},{28,4},{1,9},{5... | collective-permute-start | bytes 393224 | tf_op jit(solution)/shard_map/ppermute | solution.py:23
  147.9 19.4 %collective-permute-start.18 = (bf16[16,4096]{1,0:T(8,128)(2,1)S(1)}, bf16[16,4096]{1,0:T(8,128)(2,1)S(1)}, u32[]{:S(2)}, u32[]{:S(2)}) collective-permute-start(bf16[16,4096]{1,0:T(8,128)(2,1)S(1)} %get-tuple-element.72), channel_id=1, source_target_pairs={{0,4},{4,8},{8,12},{12,16},{16,20},{20,24},{24,28},{28,0},{1,5},{5... | collective-permute-start | bytes 393224 | tf_op jit(solution)/shard_map/ppermute | solution.py:23
  152.2 29.4 %collective-permute-start.30 = (f32[1,4096]{1,0:T(1,128)S(1)}, f32[1,4096]{1,0:T(1,128)S(1)}, u32[]{:S(2)}, u32[]{:S(2)}) collective-permute-start(f32[1,4096]{1,0:T(1,128)S(1)} %add.68), channel_id=1, source_target_pairs={{0,16},{4,20},{8,24},{12,28},{16,0},{20,4},{24,8},{28,12},{1,17},{... | collective-permute-start | bytes 49160 | tf_op jit(solution)/shard_map/ppermute | solution.py:285
  167.7 16.9 %collective-permute-start.25 = (bf16[16,4096]{1,0:T(8,128)(2,1)S(1)}, bf16[16,4096]{1,0:T(8,128)(2,1)S(1)}, u32[]{:S(2)}, u32[]{:S(2)}) collective-permute-start(bf16[16,4096]{1,0:T(8,128)(2,1)S(1)} %fusion.7), channel_id=1, source_target_pairs={{0,480},{32,0},{64,32},{96,64},{128,96},{160,128},{192,160},{224,1... | collective-permute-start | bytes 393224 | tf_op jit(solution)/shard_map/ppermute | solution.py:23
  (11 other events, 121.6 us)

commit v7 on v6

--- a/solution.py
+++ b/solution.py
@@ -40,22 +40,6 @@
     ahead = along(ahead[:rows], "y", -1)
     found[half] = (ahead, behind)
     return found
-
-
-def reduced(share, total):
-    found = {}
-
-    def send(apart):
-        found[apart] = along(share[apart], "y", apart)
-
-    for apart in range(1, Y):
-        send(apart)
-    for axis, apart in (("core", 1), ("z", 1), ("y", 1), ("y", 2)):
-        total = with_partner(total, axis, apart)
-    grad_normed = share[0].astype(F32)
-    for apart in range(1, Y):
-        grad_normed = grad_normed + found[apart].astype(F32)
-    return grad_normed, total
 
 
 def vmem_params(mib):
@@ -225,6 +209,75 @@
     )(*operands, own, taken, *val_pair, gain_row)
 
 
+def shares(factors, weights, total, rows):
+    width = total.shape[-1]
+    side = width // rows
+    column = 512
+
+    def body(*refs):
+        factors, weights, total, messages, square = refs[:4], refs[4:8], refs[8], refs[9:-1], refs[-1]
+        left = [ref[...] for ref in factors]
+        for at in range(0, width, column):
+            share = contract(left[0], weights[0][:, at : at + column], ((1,), (0,)))
+            for i in range(1, 4):
+                share += contract(left[i], weights[i][:, at : at + column], ((1,), (0,)))
+            share = share.astype(BF16)
+            for y in range(Y):
+                messages[y][:, at : at + column] = share[y * rows : (y + 1) * rows]
+        for row in range(rows):
+            square[row : row + 1, :] = total[:, row * side : (row + 1) * side]
+        first = square[...].astype(BF16)
+        second = (square[...] - first.astype(F32)).astype(BF16)
+        for y in range(Y):
+            messages[y][:, width : width + side] = first
+            messages[y][:, width + side :] = second
+
+    return pl.pallas_call(
+        body,
+        out_shape=[jax.ShapeDtypeStruct((rows, width + 2 * side), BF16)] * Y,
+        scratch_shapes=[pltpu.VMEM((rows, side), F32)],
+        compiler_params=vmem_params(16),
+        cost_estimate=pl.CostEstimate(flops=1 << 29, bytes_accessed=6 << 20, transcendentals=0),
+        name="shares",
+    )(*factors, *weights, total)
+
+
+def ended(place, messages, x_rows, cot_rows, gain_row, inv_rms):
+    rows, width = x_rows.shape
+    side = (messages[0].shape[1] - width) // 2
+
+    def body(place, *refs):
+        messages, (x_rows, cot_rows, gain, inv_rms, grad_local, total, terms) = refs[:Y], refs[Y:]
+        grad_normed = messages[0][:, :width].astype(F32)
+        for back in range(1, Y):
+            grad_normed = grad_normed + messages[back][:, :width].astype(F32)
+        for back in range(Y):
+            sender = lax.rem(place[0] + (Y - back), Y)
+            first = messages[back][:, width : width + side].astype(F32)
+            terms[sender] = first + messages[back][:, width + side :].astype(F32)
+        added = terms[0]
+        for y in range(1, Y):
+            added = added + terms[y]
+        total[...] = added
+        x_float = x_rows[...].astype(F32)
+        inv = inv_rms[...]
+        scaled = gain[...] * grad_normed
+        mean = jnp.sum(scaled * x_float, axis=-1, keepdims=True) / width
+        grad_local[...] = (cot_rows[...].astype(F32) + inv * scaled - x_float * (inv * inv * inv * mean)).astype(BF16)
+
+    vmem = pl.BlockSpec(memory_space=pltpu.VMEM)
+    return pl.pallas_call(
+        body,
+        in_specs=[pl.BlockSpec(memory_space=pltpu.SMEM)] + [vmem] * (Y + 4),
+        out_specs=[vmem, vmem],
+        out_shape=(jax.ShapeDtypeStruct((rows, width), BF16), jax.ShapeDtypeStruct((rows, side), F32)),
+        scratch_shapes=[pltpu.VMEM((Y, rows, side), F32)],
+        compiler_params=vmem_params(16),
+        cost_estimate=pl.CostEstimate(flops=2 << 20, bytes_accessed=2 << 20, transcendentals=0),
+        name="ended",
+    )(place, *messages, x_rows, cot_rows, gain_row, inv_rms)
+
+
 def on_device(x_in, grad_out, gain, w_val, w_out, filt, tail, micro_index):
     x_rows, cot_rows, gain_row = x_in[0], grad_out[0], gain[0]
     val_weight, out_weight = w_val[0], w_out[0]
@@ -259,8 +312,6 @@
     kept, given = sorted_products(products, rows, channels)
     taken = lax.ppermute(given, "core", SWAP)
     val_z, val_z_core, kept = lax.optimization_barrier((val_z, val_z_core, kept))
-    val_weights = jnp.concatenate([val_weight, val_core, val_z, val_z_core], axis=0)
-    val_weights, kept = lax.optimization_barrier((val_weights, kept))
 
     place = jnp.stack([lax.axis_index(axis) for axis in TENSOR]).astype(jnp.int32)
     lead_rows = jnp.where(has_tail, tail_rows, jnp.zeros_like(tail_rows)).astype(F32)
@@ -274,26 +325,21 @@
     from_z, from_z_core, partial = lax.optimization_barrier((from_z, from_z_core, partial))
     kept_val, kept_out, given, gain_term = partial
 
-    share = contract(
-        jnp.concatenate([own[0, 0], taken[0, 0], from_z, from_z_core], axis=1), val_weights, ((1,), (0,))
+    messages = shares(
+        (own[0, 0], taken[0, 0], from_z, from_z_core), (val_weight, val_core, val_z, val_z_core), gain_term, rows
     )
-    grad_normed, gain_term = reduced(share.astype(BF16).reshape(Y, rows, width), gain_term)
+    arrived = [messages[0]]
+    for apart in range(1, Y):
+        arrived.append(along(messages[apart], "y", apart))
     taken = lax.ppermute(given, "core", SWAP)
-    cot_late, taken = lax.optimization_barrier((cot_rows, taken))
+    arrived, taken = lax.optimization_barrier((arrived, taken))
+    grad_local, gain_term = ended(place, arrived, x_rows, cot_rows, gain_row[None], inv_rms)
+    received = along(grad_local, "section", -1)
+    gain_term = with_partner(gain_term, "z", 1)
+    grad_gain = with_partner(gain_term, "core", 1).reshape(1, width)
+    taken, grad_local = lax.optimization_barrier((taken, grad_local))
     grad_wv = (kept_val + taken[0].astype(F32)).astype(BF16)
     grad_wo = (kept_out + taken[1].astype(F32)).astype(BF16)
-    gain_other = lax.ppermute(gain_term, "y", [(i, i ^ 4) for i in range(Y)])
-
-    scaled = gain_row * grad_normed
-    grad_local = (
-        cot_late.astype(F32)
-        + inv_rms * scaled
-        - x_float * inv_rms**3 * jnp.mean(scaled * x_float, axis=-1, keepdims=True)
-    )
-    grad_local = grad_local.astype(BF16)
-    received = along(grad_local, "section", -1)
-    gain_other, grad_wv, grad_wo, _ = lax.optimization_barrier((gain_other, grad_wv, grad_wo, grad_local))
-    grad_gain = gain_term + gain_other
     return (
         received[None],
         grad_wv[None],

time: 186 us -> 169 us (0.909)
  waiting for transfers between devices: 37.8 us -> 24.6 us
  starting transfers between devices: 115 us -> 107 us
  Pallas kernels: 4.91 us -> 8.44 us
    ppermute x4 -> x2, starting transfers between devices: 13.2 us -> 7.27 us  [with_partner(): return total + lax.ppermute(total, axis, [(i, i ^ apart) for i in devices])]
    ppermute x1, waiting for transfers between devices: 5.81 us -> 0.01 us  [on_device(): val_z = lax.ppermute(val_sent, 'z', SWAP)]
    ppermute x4 -> x2, waiting for transfers between devices: 4.77 us -> 0.01 us  [with_partner(): return total + lax.ppermute(total, axis, [(i, i ^ apart) for i in devices])]
    ppermute x1 -> x0, starting transfers between devices: 4.75 us -> none  [on_device(): gain_other = lax.ppermute(gain_term, 'y', [(i, i ^ 4) for i in range(Y)])]
    broadcast_in_dim x0 -> x1, other arithmetic: none -> 4.75 us  [on_device(): grad_wo[None]]
    ppermute x1, starting transfers between devices: 5.85 us -> 1.92 us  [on_device(): out_core = lax.ppermute(out_weight, 'core', SWAP)]
    ppermute x1, starting transfers between devices: 1.92 us -> 5.85 us  [on_device(): val_core = lax.ppermute(val_weight, 'core', SWAP)]
    pallas_call x0 -> x2, Pallas kernels: none -> 2.12 us  [the longest x1 1.24 us: shares(): pl.pallas_call(body, out_shape=[jax.ShapeDtypeStruct((rows, width + 2 * s...]
  transfers between devices with their start and end apart: 31 -> 28, of which waited for: 13 -> 8; matrix products, arithmetic and copies ran while one was open for 12% -> 13% of each run, Pallas kernels for 2% -> 4%
where the time goes in v7:
time: 169 us; the launch traced here: 168 us
  starting transfers between devices  107 us (63%)
  waiting for transfers between devices  24.6 us (15%)
  matrix products  12.5 us (7%)
  other arithmetic  11.4 us (7%)
  Pallas kernels  8.44 us (5%)
  local copies, waits for them, and re-layouts  2.02 us (1%)
  between operations  1.86 us (1%)
    ppermute x16, starting transfers between devices, along(): lax.ppermute(block, axis, [(i, (i + distance) % devices) for i in range(d...  62.4 us
    ppermute x16, waiting for transfers between devices, along(): lax.ppermute(block, axis, [(i, (i + distance) % devices) for i in range(d...  24.2 us
    dot_general x9, matrix products, contract(): lax.dot_general(left, right, (dims, ((), ())), preferred_element_type=F32)  12.5 us
    ppermute x2, starting transfers between devices, on_device(): taken = lax.ppermute(given, 'core', SWAP)  8.01 us
    ppermute x2, starting transfers between devices, with_partner(): return total + lax.ppermute(total, axis, [(i, i ^ apart) for i in devices])  7.27 us
    ppermute x1, starting transfers between devices, on_device(): val_core = lax.ppermute(val_weight, 'core', SWAP)  5.85 us
    pallas_call x1, Pallas kernels, weight_gradients(): pl.pallas_call(body, grid=(width // column,), in_specs=[by_column(o.shape...  5.24 us
    ppermute x1, starting transfers between devices, on_device(): val_z_core = lax.ppermute(val_z, 'core', SWAP)  5.15 us
  transfers between devices with their start and end apart: 28, of which 8 were waited for; matrix products, arithmetic and copies ran while one was open for 13% of the time, Pallas kernels for 4%

profile of v7, /device:TPU:1, one launch (start us, length us, event | category | flops | bytes accessed | tf_op | source)
XLA Modules:
  0.0 167.9 jit_solution(16340352178283723575)
XLA Ops:
  3.6 4.8 %collective-permute-start = (bf16[32,4096]{1,0:T(8,128)(2,1)S(1)}, bf16[32,4096]{1,0:T(8,128)(2,1)S(1)}, u32[]{:S(2)}, u32[]{:S(2)}) collective-permute-start(bf16[32,4096]{1,0:T(8,128)(2,1)S(1)} %pad_maximum_fusion.2), channel_id=1, source_target_pairs={{0,2},{2,0},{1,3},{3,1},{4,6},{6,4},{5,7},{7,5},{8,10},{10,8},{9,1... | collective-permute-start | bytes 786440 | tf_op jit(solution)/shard_map/ppermute | solution.py:294
  8.5 5.9 %collective-permute-start.3 = (bf16[128,4096]{1,0:T(8,128)(2,1)}, bf16[128,4096]{1,0:T(8,128)(2,1)S(1)}, u32[]{:S(2)}, u32[]{:S(2)}) collective-permute-start(bf16[128,4096]{1,0:T(8,128)(2,1)} %bitcast.64), channel_id=1, source_target_pairs={{0,1},{1,0},{2,3},{3,2},{4,5},{5,4},{6,7},{7,6},{8,9},{9,8},{10,11... | collective-permute-start | bytes 3145736 | tf_op jit(solution)/shard_map/ppermute | solution.py:297
  17.2 3.3 %collective-permute-start.5 = (bf16[64,4096]{1,0:T(8,128)(2,1)S(1)}, bf16[64,4096]{1,0:T(8,128)(2,1)S(1)}, u32[]{:S(2)}, u32[]{:S(2)}) collective-permute-start(bf16[64,4096]{1,0:T(8,128)(2,1)S(1)} %pad_maximum_fusion.1.refs_0_), channel_id=1, source_target_pairs={{0,28},{4,0},{8,4},{12,8},{16,12},{20,16},{24,20},{28,24},{1,29},{... | collective-permute-start | bytes 1572872 | tf_op jit(solution)/shard_map/ppermute | solution.py:23
  22.5 3.6 %collective-permute-start.1 = (bf16[128,4096]{1,0:T(8,128)(2,1)}, bf16[128,4096]{1,0:T(8,128)(2,1)S(1)}, u32[]{:S(2)}, u32[]{:S(2)}) collective-permute-start(bf16[128,4096]{1,0:T(8,128)(2,1)} %bitcast.65), channel_id=1, source_target_pairs={{0,2},{2,0},{1,3},{3,1},{4,6},{6,4},{5,7},{7,5},{8,10},{10,8},{9,1... | collective-permute-start | bytes 3145736 | tf_op jit(solution)/shard_map/ppermute | solution.py:300
  26.2 4.3 %collective-permute-done.5.refs_1_ = bf16[64,4096]{1,0:T(8,128)(2,1)S(1)} collective-permute-done((bf16[64,4096]{1,0:T(8,128)(2,1)S(1)}, bf16[64,4096]{1,0:T(8,128)(2,1)S(1)}, u32[]{:S(2)}, u32[]{:S(2)}) %collective-permute-start.5) | collective-permute-done | bytes 524320 | tf_op jit(solution)/shard_map/ppermute | solution.py:23
  30.5 5.3 %collective-permute-start.6 = (bf16[64,4096]{1,0:T(8,128)(2,1)S(1)}, bf16[64,4096]{1,0:T(8,128)(2,1)S(1)}, u32[]{:S(2)}, u32[]{:S(2)}) collective-permute-start(bf16[64,4096]{1,0:T(8,128)(2,1)S(1)} %collective-permute-done.5.refs_1_), channel_id=1, source_target_pairs={{0,28},{4,0},{8,4},{12,8},{16,12},{20,16},{24,20},{28,24},{1,29},{... | collective-permute-start | bytes 1572872 | tf_op jit(solution)/shard_map/ppermute | solution.py:23
  45.0 5.3 %collective-permute-start.7 = (bf16[64,4096]{1,0:T(8,128)(2,1)S(1)}, bf16[64,4096]{1,0:T(8,128)(2,1)S(1)}, u32[]{:S(2)}, u32[]{:S(2)}) collective-permute-start(bf16[64,4096]{1,0:T(8,128)(2,1)S(1)} %collective-permute-done.6.refs_2_), channel_id=1, source_target_pairs={{0,28},{4,0},{8,4},{12,8},{16,12},{20,16},{24,20},{28,24},{1,29},{... | collective-permute-start | bytes 1572872 | tf_op jit(solution)/shard_map/ppermute | solution.py:23
  52.3 5.2 %collective-permute-start.2 = (bf16[128,4096]{1,0:T(8,128)(2,1)S(1)}, bf16[128,4096]{1,0:T(8,128)(2,1)S(1)}, u32[]{:S(2)}, u32[]{:S(2)}) collective-permute-start(bf16[128,4096]{1,0:T(8,128)(2,1)S(1)} %collective-permute-done.1.refs_6_), channel_id=1, source_target_pairs={{0,1},{1,0},{2,3},{3,2},{4,5},{5,4},{6,7},{7,6},{8,9},{9,8},{10,11... | collective-permute-start | bytes 3145736 | tf_op jit(solution)/shard_map/ppermute | solution.py:301
  60.2 4.9 %collective-permute-start.8 = (bf16[32,4096]{1,0:T(8,128)(2,1)S(1)}, bf16[32,4096]{1,0:T(8,128)(2,1)S(1)}, u32[]{:S(2)}, u32[]{:S(2)}) collective-permute-start(bf16[32,4096]{1,0:T(8,128)(2,1)S(1)} %slice.32), channel_id=1, source_target_pairs={{0,28},{4,0},{8,4},{12,8},{16,12},{20,16},{24,20},{28,24},{1,29},{... | collective-permute-start | bytes 786440 | tf_op jit(solution)/shard_map/ppermute | solution.py:23
  74.9 6.0 %collective-permute-start.13 = (f32[2,2,8,16,128]{4,3,2,1,0:T(8,128)S(1)}, f32[2,2,8,16,128]{4,3,2,1,0:T(8,128)S(1)}, u32[]{:S(2)}, u32[]{:S(2)}) collective-permute-start(f32[2,2,8,16,128]{4,3,2,1,0:T(8,128)S(1)} %get-tuple-element.50), channel_id=1, source_target_pairs={{0,1},{1,0},{2,3},{3,2},{4,5},{5,4},{6,7},{7,6},{8,9},{9,8},{10,11... | collective-permute-start | bytes 786440 | tf_op jit(solution)/shard_map/ppermute | solution.py:313
  85.6 2.5 %collective-permute-start.15 = (bf16[128,128]{1,0:T(8,128)(2,1)S(1)}, bf16[128,128]{1,0:T(8,128)(2,1)S(1)}, u32[]{:S(2)}, u32[]{:S(2)}) collective-permute-start(bf16[128,128]{1,0:T(8,128)(2,1)S(1)} %get-tuple-element.97), channel_id=1, source_target_pairs={{0,2},{2,0},{1,3},{3,1},{4,6},{6,4},{5,7},{7,5},{8,10},{10,8},{9,1... | collective-permute-start | bytes 98312 | tf_op jit(solution)/shard_map/ppermute | solution.py:322
  88.1 3.1 %collective-permute-start.16 = (bf16[128,128]{1,0:T(8,128)(2,1)S(1)}, bf16[128,128]{1,0:T(8,128)(2,1)S(1)}, u32[]{:S(2)}, u32[]{:S(2)}) collective-permute-start(bf16[128,128]{1,0:T(8,128)(2,1)S(1)} %get-tuple-element.96), channel_id=1, source_target_pairs={{0,3},{1,2},{2,1},{3,0},{4,7},{5,6},{6,5},{7,4},{8,11},{9,10},{10,... | collective-permute-start | bytes 98312 | tf_op jit(solution)/shard_map/ppermute | solution.py:323
  91.2 5.2 %weight_gradients.1 = (f32[128,4096]{1,0:T(8,128)S(1)}, f32[128,4096]{1,0:T(8,128)S(1)}, bf16[2,128,4096]{2,1,0:T(8,128)(2,1)}, f32[1,4096]{1,0:T(1,128)S(1)}) custom-call(bf16[64,4096]{1,0:T(8,128)(2,1)S(1)} %pad_maximum_fusion.1.refs_0_, bf16[64,4096]{1,0:T(8,128)(2,1)S(1)} %collective-permute-done.5.refs_1_, ...), custom_call_target="tpu_custom_call" | custom-call | flops 1073741824 | bytes 13631488 | tf_op jit(solution)/shard_map/weight_gradients/pallas_call | solution.py:194
  103.6 4.7 %collective-permute-start.19 = (bf16[16,4608]{1,0:T(8,128)(2,1)S(1)}, bf16[16,4608]{1,0:T(8,128)(2,1)S(1)}, u32[]{:S(2)}, u32[]{:S(2)}) collective-permute-start(bf16[16,4608]{1,0:T(8,128)(2,1)S(1)} %get-tuple-element.66), channel_id=1, source_target_pairs={{0,12},{4,16},{8,20},{12,24},{16,28},{20,0},{24,4},{28,8},{1,13},{... | collective-permute-start | bytes 442376 | tf_op jit(solution)/shard_map/ppermute | solution.py:23
  108.3 4.8 %collective-permute-start.20 = (bf16[16,4608]{1,0:T(8,128)(2,1)S(1)}, bf16[16,4608]{1,0:T(8,128)(2,1)S(1)}, u32[]{:S(2)}, u32[]{:S(2)}) collective-permute-start(bf16[16,4608]{1,0:T(8,128)(2,1)S(1)} %get-tuple-element.67), channel_id=1, source_target_pairs={{0,16},{4,20},{8,24},{12,28},{16,0},{20,4},{24,8},{28,12},{1,17},{... | collective-permute-start | bytes 442376 | tf_op jit(solution)/shard_map/ppermute | solution.py:23
  113.1 3.6 %collective-permute-start.21 = (bf16[16,4608]{1,0:T(8,128)(2,1)S(1)}, bf16[16,4608]{1,0:T(8,128)(2,1)S(1)}, u32[]{:S(2)}, u32[]{:S(2)}) collective-permute-start(bf16[16,4608]{1,0:T(8,128)(2,1)S(1)} %get-tuple-element.68), channel_id=1, source_target_pairs={{0,20},{4,24},{8,28},{12,0},{16,4},{20,8},{24,12},{28,16},{1,21},{... | collective-permute-start | bytes 442376 | tf_op jit(solution)/shard_map/ppermute | solution.py:23
  116.7 5.2 %collective-permute-start.22 = (bf16[16,4608]{1,0:T(8,128)(2,1)S(1)}, bf16[16,4608]{1,0:T(8,128)(2,1)S(1)}, u32[]{:S(2)}, u32[]{:S(2)}) collective-permute-start(bf16[16,4608]{1,0:T(8,128)(2,1)S(1)} %get-tuple-element.69), channel_id=1, source_target_pairs={{0,24},{4,28},{8,0},{12,4},{16,8},{20,12},{24,16},{28,20},{1,25},{... | collective-permute-start | bytes 442376 | tf_op jit(solution)/shard_map/ppermute | solution.py:23
  121.9 5.4 %collective-permute-done.19.refs_3_ = bf16[16,4608]{1,0:T(8,128)(2,1)S(1)} collective-permute-done((bf16[16,4608]{1,0:T(8,128)(2,1)S(1)}, bf16[16,4608]{1,0:T(8,128)(2,1)S(1)}, u32[]{:S(2)}, u32[]{:S(2)}) %collective-permute-start.19) | collective-permute-done | bytes 147488 | tf_op jit(solution)/shard_map/ppermute | solution.py:23
  129.3 3.4 %collective-permute-done.21.refs_5_ = bf16[16,4608]{1,0:T(8,128)(2,1)S(1)} collective-permute-done((bf16[16,4608]{1,0:T(8,128)(2,1)S(1)}, bf16[16,4608]{1,0:T(8,128)(2,1)S(1)}, u32[]{:S(2)}, u32[]{:S(2)}) %collective-permute-start.21) | collective-permute-done | bytes 147488 | tf_op jit(solution)/shard_map/ppermute | solution.py:23
  132.8 6.0 %collective-permute-done.22.refs_6_ = bf16[16,4608]{1,0:T(8,128)(2,1)S(1)} collective-permute-done((bf16[16,4608]{1,0:T(8,128)(2,1)S(1)}, bf16[16,4608]{1,0:T(8,128)(2,1)S(1)}, u32[]{:S(2)}, u32[]{:S(2)}) %collective-permute-start.22) | collective-permute-done | bytes 147488 | tf_op jit(solution)/shard_map/ppermute | solution.py:23
  141.5 2.5 %collective-permute-start.26 = (f32[16,256]{1,0:T(8,128)S(1)}, f32[16,256]{1,0:T(8,128)S(1)}, u32[]{:S(2)}, u32[]{:S(2)}) collective-permute-start(f32[16,256]{1,0:T(8,128)S(1)} %get-tuple-element.87), channel_id=1, source_target_pairs={{0,2},{2,0},{1,3},{3,1},{4,6},{6,4},{5,7},{7,5},{8,10},{10,8},{9,1... | collective-permute-start | bytes 49160 | tf_op jit(solution)/shard_map/ppermute | solution.py:28
  145.1 11.9 %collective-permute-start.25 = (bf16[16,4096]{1,0:T(8,128)(2,1)S(1)}, bf16[16,4096]{1,0:T(8,128)(2,1)S(1)}, u32[]{:S(2)}, u32[]{:S(2)}) collective-permute-start(bf16[16,4096]{1,0:T(8,128)(2,1)S(1)} %get-tuple-element.80), channel_id=1, source_target_pairs={{0,480},{32,0},{64,32},{96,64},{128,96},{160,128},{192,160},{224,1... | collective-permute-start | bytes 393224 | tf_op jit(solution)/shard_map/ppermute | solution.py:23
  157.1 4.7 %collective-permute-start.27 = (f32[16,256]{1,0:T(8,128)S(1)}, f32[16,256]{1,0:T(8,128)S(1)}, u32[]{:S(2)}, u32[]{:S(2)}) collective-permute-start(f32[16,256]{1,0:T(8,128)S(1)} %add.28), channel_id=1, source_target_pairs={{0,1},{1,0},{2,3},{3,2},{4,5},{5,4},{6,7},{7,6},{8,9},{9,8},{10,11... | collective-permute-start | bytes 49160 | tf_op jit(solution)/shard_map/ppermute | solution.py:28
  161.9 4.8 %fusion.3 = (bf16[1,128,4096]{2,1,0:T(8,128)(2,1)}, bf16[1,128,4096]{2,1,0:T(8,128)(2,1)}) fusion(f32[128,4096]{1,0:T(8,128)} %copy-done.2, bf16[2,128,4096]{2,1,0:T(8,128)(2,1)} %collective-permute-done.24, f32[128,4096]{1,0:T(8,128)} %copy-done.1), kind=kLoop, calls=%fused_computation.6 | loop fusion | flops 3145728 | bytes 8388608 | tf_op jit(solution)/shard_map/broadcast_in_dim | solution.py:346
  (84 shorter events, 49.6 us)
Async XLA Ops:
  3.6 12.6 %collective-permute-start = (bf16[32,4096]{1,0:T(8,128)(2,1)S(1)}, bf16[32,4096]{1,0:T(8,128)(2,1)S(1)}, u32[]{:S(2)}, u32[]{:S(2)}) collective-permute-start(bf16[32,4096]{1,0:T(8,128)(2,1)S(1)} %pad_maximum_fusion.2), channel_id=1, source_target_pairs={{0,2},{2,0},{1,3},{3,1},{4,6},{6,4},{5,7},{7,5},{8,10},{10,8},{9,1... | collective-permute-start | bytes 786440 | tf_op jit(solution)/shard_map/ppermute | solution.py:294
  8.5 29.3 %collective-permute-start.3 = (bf16[128,4096]{1,0:T(8,128)(2,1)}, bf16[128,4096]{1,0:T(8,128)(2,1)S(1)}, u32[]{:S(2)}, u32[]{:S(2)}) collective-permute-start(bf16[128,4096]{1,0:T(8,128)(2,1)} %bitcast.64), channel_id=1, source_target_pairs={{0,1},{1,0},{2,3},{3,2},{4,5},{5,4},{6,7},{7,6},{8,9},{9,8},{10,11... | collective-permute-start | bytes 3145736 | tf_op jit(solution)/shard_map/ppermute | solution.py:297
  14.3 23.5 %collective-permute-start.4 = (bf16[128,4096]{1,0:T(8,128)(2,1)}, bf16[128,4096]{1,0:T(8,128)(2,1)}, u32[]{:S(2)}, u32[]{:S(2)}) collective-permute-start(bf16[128,4096]{1,0:T(8,128)(2,1)} %bitcast.77), channel_id=1, source_target_pairs={{0,1},{1,0},{2,3},{3,2},{4,5},{5,4},{6,7},{7,6},{8,9},{9,8},{10,11... | collective-permute-start | bytes 3145736 | tf_op jit(solution)/shard_map/ppermute | solution.py:298
  17.2 13.3 %collective-permute-start.5 = (bf16[64,4096]{1,0:T(8,128)(2,1)S(1)}, bf16[64,4096]{1,0:T(8,128)(2,1)S(1)}, u32[]{:S(2)}, u32[]{:S(2)}) collective-permute-start(bf16[64,4096]{1,0:T(8,128)(2,1)S(1)} %pad_maximum_fusion.1.refs_0_), channel_id=1, source_target_pairs={{0,28},{4,0},{8,4},{12,8},{16,12},{20,16},{24,20},{28,24},{1,29},{... | collective-permute-start | bytes 1572872 | tf_op jit(solution)/shard_map/ppermute | solution.py:23
  20.5 15.3 %collective-permute-start.9 = (bf16[64,4096]{1,0:T(8,128)(2,1)S(1)}, bf16[64,4096]{1,0:T(8,128)(2,1)S(1)}, u32[]{:S(2)}, u32[]{:S(2)}) collective-permute-start(bf16[64,4096]{1,0:T(8,128)(2,1)S(1)} %pad_maximum_fusion.1.refs_0_), channel_id=1, source_target_pairs={{0,4},{4,8},{8,12},{12,16},{16,20},{20,24},{24,28},{28,0},{1,5},{5... | collective-permute-start | bytes 1572872 | tf_op jit(solution)/shard_map/ppermute | solution.py:23
  22.5 29.7 %collective-permute-start.1 = (bf16[128,4096]{1,0:T(8,128)(2,1)}, bf16[128,4096]{1,0:T(8,128)(2,1)S(1)}, u32[]{:S(2)}, u32[]{:S(2)}) collective-permute-start(bf16[128,4096]{1,0:T(8,128)(2,1)} %bitcast.65), channel_id=1, source_target_pairs={{0,2},{2,0},{1,3},{3,1},{4,6},{6,4},{5,7},{7,5},{8,10},{10,8},{9,1... | collective-permute-start | bytes 3145736 | tf_op jit(solution)/shard_map/ppermute | solution.py:300
  30.5 14.5 %collective-permute-start.6 = (bf16[64,4096]{1,0:T(8,128)(2,1)S(1)}, bf16[64,4096]{1,0:T(8,128)(2,1)S(1)}, u32[]{:S(2)}, u32[]{:S(2)}) collective-permute-start(bf16[64,4096]{1,0:T(8,128)(2,1)S(1)} %collective-permute-done.5.refs_1_), channel_id=1, source_target_pairs={{0,28},{4,0},{8,4},{12,8},{16,12},{20,16},{24,20},{28,24},{1,29},{... | collective-permute-start | bytes 1572872 | tf_op jit(solution)/shard_map/ppermute | solution.py:23
  35.9 14.5 %collective-permute-start.10 = (bf16[64,4096]{1,0:T(8,128)(2,1)S(1)}, bf16[64,4096]{1,0:T(8,128)(2,1)S(1)}, u32[]{:S(2)}, u32[]{:S(2)}) collective-permute-start(bf16[64,4096]{1,0:T(8,128)(2,1)S(1)} %collective-permute-done.9.refs_8_), channel_id=1, source_target_pairs={{0,4},{4,8},{8,12},{12,16},{16,20},{20,24},{24,28},{28,0},{1,5},{5... | collective-permute-start | bytes 1572872 | tf_op jit(solution)/shard_map/ppermute | solution.py:23
  45.0 15.2 %collective-permute-start.7 = (bf16[64,4096]{1,0:T(8,128)(2,1)S(1)}, bf16[64,4096]{1,0:T(8,128)(2,1)S(1)}, u32[]{:S(2)}, u32[]{:S(2)}) collective-permute-start(bf16[64,4096]{1,0:T(8,128)(2,1)S(1)} %collective-permute-done.6.refs_2_), channel_id=1, source_target_pairs={{0,28},{4,0},{8,4},{12,8},{16,12},{20,16},{24,20},{28,24},{1,29},{... | collective-permute-start | bytes 1572872 | tf_op jit(solution)/shard_map/ppermute | solution.py:23
  50.3 14.8 %collective-permute-start.11 = (bf16[64,4096]{1,0:T(8,128)(2,1)S(1)}, bf16[64,4096]{1,0:T(8,128)(2,1)S(1)}, u32[]{:S(2)}, u32[]{:S(2)}) collective-permute-start(bf16[64,4096]{1,0:T(8,128)(2,1)S(1)} %collective-permute-done.10.refs_7_), channel_id=1, source_target_pairs={{0,4},{4,8},{8,12},{12,16},{16,20},{20,24},{24,28},{28,0},{1,5},{5... | collective-permute-start | bytes 1572872 | tf_op jit(solution)/shard_map/ppermute | solution.py:23
  52.3 29.4 %collective-permute-start.2 = (bf16[128,4096]{1,0:T(8,128)(2,1)S(1)}, bf16[128,4096]{1,0:T(8,128)(2,1)S(1)}, u32[]{:S(2)}, u32[]{:S(2)}) collective-permute-start(bf16[128,4096]{1,0:T(8,128)(2,1)S(1)} %collective-permute-done.1.refs_6_), channel_id=1, source_target_pairs={{0,1},{1,0},{2,3},{3,2},{4,5},{5,4},{6,7},{7,6},{8,9},{9,8},{10,11... | collective-permute-start | bytes 3145736 | tf_op jit(solution)/shard_map/ppermute | solution.py:301
  60.2 9.6 %collective-permute-start.8 = (bf16[32,4096]{1,0:T(8,128)(2,1)S(1)}, bf16[32,4096]{1,0:T(8,128)(2,1)S(1)}, u32[]{:S(2)}, u32[]{:S(2)}) collective-permute-start(bf16[32,4096]{1,0:T(8,128)(2,1)S(1)} %slice.32), channel_id=1, source_target_pairs={{0,28},{4,0},{8,4},{12,8},{16,12},{20,16},{24,20},{28,24},{1,29},{... | collective-permute-start | bytes 786440 | tf_op jit(solution)/shard_map/ppermute | solution.py:23
  85.6 10.9 %collective-permute-start.15 = (bf16[128,128]{1,0:T(8,128)(2,1)S(1)}, bf16[128,128]{1,0:T(8,128)(2,1)S(1)}, u32[]{:S(2)}, u32[]{:S(2)}) collective-permute-start(bf16[128,128]{1,0:T(8,128)(2,1)S(1)} %get-tuple-element.97), channel_id=1, source_target_pairs={{0,2},{2,0},{1,3},{3,1},{4,6},{6,4},{5,7},{7,5},{8,10},{10,8},{9,1... | collective-permute-start | bytes 98312 | tf_op jit(solution)/shard_map/ppermute | solution.py:322
  96.5 44.1 %collective-permute-start.24 = (bf16[2,128,4096]{2,1,0:T(8,128)(2,1)}, bf16[2,128,4096]{2,1,0:T(8,128)(2,1)}, u32[]{:S(2)}, u32[]{:S(2)}) collective-permute-start(bf16[2,128,4096]{2,1,0:T(8,128)(2,1)} %get-tuple-element.71), channel_id=1, source_target_pairs={{0,1},{1,0},{2,3},{3,2},{4,5},{5,4},{6,7},{7,6},{8,9},{9,8},{10,11... | collective-permute-start | bytes 6291464 | tf_op jit(solution)/shard_map/ppermute | solution.py:334
  99.8 13.3 %collective-permute-start.17 = (bf16[16,4608]{1,0:T(8,128)(2,1)S(1)}, bf16[16,4608]{1,0:T(8,128)(2,1)S(1)}, u32[]{:S(2)}, u32[]{:S(2)}) collective-permute-start(bf16[16,4608]{1,0:T(8,128)(2,1)S(1)} %get-tuple-element.64), channel_id=1, source_target_pairs={{0,4},{4,8},{8,12},{12,16},{16,20},{20,24},{24,28},{28,0},{1,5},{5... | collective-permute-start | bytes 442376 | tf_op jit(solution)/shard_map/ppermute | solution.py:23
  101.7 15.0 %collective-permute-start.18 = (bf16[16,4608]{1,0:T(8,128)(2,1)S(1)}, bf16[16,4608]{1,0:T(8,128)(2,1)S(1)}, u32[]{:S(2)}, u32[]{:S(2)}) collective-permute-start(bf16[16,4608]{1,0:T(8,128)(2,1)S(1)} %get-tuple-element.65), channel_id=1, source_target_pairs={{0,8},{4,12},{8,16},{12,20},{16,24},{20,28},{24,0},{28,4},{1,9},{5... | collective-permute-start | bytes 442376 | tf_op jit(solution)/shard_map/ppermute | solution.py:23
  103.6 23.7 %collective-permute-start.19 = (bf16[16,4608]{1,0:T(8,128)(2,1)S(1)}, bf16[16,4608]{1,0:T(8,128)(2,1)S(1)}, u32[]{:S(2)}, u32[]{:S(2)}) collective-permute-start(bf16[16,4608]{1,0:T(8,128)(2,1)S(1)} %get-tuple-element.66), channel_id=1, source_target_pairs={{0,12},{4,16},{8,20},{12,24},{16,28},{20,0},{24,4},{28,8},{1,13},{... | collective-permute-start | bytes 442376 | tf_op jit(solution)/shard_map/ppermute | solution.py:23
  108.3 21.0 %collective-permute-start.20 = (bf16[16,4608]{1,0:T(8,128)(2,1)S(1)}, bf16[16,4608]{1,0:T(8,128)(2,1)S(1)}, u32[]{:S(2)}, u32[]{:S(2)}) collective-permute-start(bf16[16,4608]{1,0:T(8,128)(2,1)S(1)} %get-tuple-element.67), channel_id=1, source_target_pairs={{0,16},{4,20},{8,24},{12,28},{16,0},{20,4},{24,8},{28,12},{1,17},{... | collective-permute-start | bytes 442376 | tf_op jit(solution)/shard_map/ppermute | solution.py:23
  113.1 19.6 %collective-permute-start.21 = (bf16[16,4608]{1,0:T(8,128)(2,1)S(1)}, bf16[16,4608]{1,0:T(8,128)(2,1)S(1)}, u32[]{:S(2)}, u32[]{:S(2)}) collective-permute-start(bf16[16,4608]{1,0:T(8,128)(2,1)S(1)} %get-tuple-element.68), channel_id=1, source_target_pairs={{0,20},{4,24},{8,28},{12,0},{16,4},{20,8},{24,12},{28,16},{1,21},{... | collective-permute-start | bytes 442376 | tf_op jit(solution)/shard_map/ppermute | solution.py:23
  116.7 22.0 %collective-permute-start.22 = (bf16[16,4608]{1,0:T(8,128)(2,1)S(1)}, bf16[16,4608]{1,0:T(8,128)(2,1)S(1)}, u32[]{:S(2)}, u32[]{:S(2)}) collective-permute-start(bf16[16,4608]{1,0:T(8,128)(2,1)S(1)} %get-tuple-element.69), channel_id=1, source_target_pairs={{0,24},{4,28},{8,0},{12,4},{16,8},{20,12},{24,16},{28,20},{1,25},{... | collective-permute-start | bytes 442376 | tf_op jit(solution)/shard_map/ppermute | solution.py:23
  127.3 13.3 %collective-permute-start.23 = (bf16[16,4608]{1,0:T(8,128)(2,1)S(1)}, bf16[16,4608]{1,0:T(8,128)(2,1)S(1)}, u32[]{:S(2)}, u32[]{:S(2)}) collective-permute-start(bf16[16,4608]{1,0:T(8,128)(2,1)S(1)} %get-tuple-element.70), channel_id=1, source_target_pairs={{0,28},{4,0},{8,4},{12,8},{16,12},{20,16},{24,20},{28,24},{1,29},{... | collective-permute-start | bytes 442376 | tf_op jit(solution)/shard_map/ppermute | solution.py:23
  141.5 15.6 %collective-permute-start.26 = (f32[16,256]{1,0:T(8,128)S(1)}, f32[16,256]{1,0:T(8,128)S(1)}, u32[]{:S(2)}, u32[]{:S(2)}) collective-permute-start(f32[16,256]{1,0:T(8,128)S(1)} %get-tuple-element.87), channel_id=1, source_target_pairs={{0,2},{2,0},{1,3},{3,1},{4,6},{6,4},{5,7},{7,5},{8,10},{10,8},{9,1... | collective-permute-start | bytes 49160 | tf_op jit(solution)/shard_map/ppermute | solution.py:28
  145.1 22.1 %collective-permute-start.25 = (bf16[16,4096]{1,0:T(8,128)(2,1)S(1)}, bf16[16,4096]{1,0:T(8,128)(2,1)S(1)}, u32[]{:S(2)}, u32[]{:S(2)}) collective-permute-start(bf16[16,4096]{1,0:T(8,128)(2,1)S(1)} %get-tuple-element.80), channel_id=1, source_target_pairs={{0,480},{32,0},{64,32},{96,64},{128,96},{160,128},{192,160},{224,1... | collective-permute-start | bytes 393224 | tf_op jit(solution)/shard_map/ppermute | solution.py:23
  157.1 9.5 %collective-permute-start.27 = (f32[16,256]{1,0:T(8,128)S(1)}, f32[16,256]{1,0:T(8,128)S(1)}, u32[]{:S(2)}, u32[]{:S(2)}) collective-permute-start(f32[16,256]{1,0:T(8,128)S(1)} %add.28), channel_id=1, source_target_pairs={{0,1},{1,0},{2,3},{3,2},{4,5},{5,4},{6,7},{7,6},{8,9},{9,8},{10,11... | collective-permute-start | bytes 49160 | tf_op jit(solution)/shard_map/ppermute | solution.py:28
  (12 other events, 152.7 us)

commit v8 on v7

--- a/solution.py
+++ b/solution.py
@@ -324,6 +324,7 @@
     partial = weight_gradients(found, own, taken, (val_weight, val_core), gain_row[None], rows)
     from_z, from_z_core, partial = lax.optimization_barrier((from_z, from_z_core, partial))
     kept_val, kept_out, given, gain_term = partial
+    swapped = lax.ppermute(given, "core", SWAP)
 
     messages = shares(
         (own[0, 0], taken[0, 0], from_z, from_z_core), (val_weight, val_core, val_z, val_z_core), gain_term, rows
@@ -331,15 +332,15 @@
     arrived = [messages[0]]
     for apart in range(1, Y):
         arrived.append(along(messages[apart], "y", apart))
-    taken = lax.ppermute(given, "core", SWAP)
-    arrived, taken = lax.optimization_barrier((arrived, taken))
+    grad_wv = (kept_val + swapped[0].astype(F32)).astype(BF16)
+    grad_wo = (kept_out + swapped[1].astype(F32)).astype(BF16)
+    arrived, grad_wv, grad_wo, grad_filter, grad_tail = lax.optimization_barrier(
+        (arrived, grad_wv, grad_wo, grad_filter, grad_tail)
+    )
     grad_local, gain_term = ended(place, arrived, x_rows, cot_rows, gain_row[None], inv_rms)
     received = along(grad_local, "section", -1)
     gain_term = with_partner(gain_term, "z", 1)
     grad_gain = with_partner(gain_term, "core", 1).reshape(1, width)
-    taken, grad_local = lax.optimization_barrier((taken, grad_local))
-    grad_wv = (kept_val + taken[0].astype(F32)).astype(BF16)
-    grad_wo = (kept_out + taken[1].astype(F32)).astype(BF16)
     return (
         received[None],
         grad_wv[None],

time: 169 us -> 182 us (1.077)
  local copies, waits for them, and re-layouts: 2.02 us -> 13.2 us
  starting transfers between devices: 107 us -> 109 us
    unnamed x20 -> x60, local copies, waits for them, and re-layouts: 1.89 us -> 12.4 us
    broadcast_in_dim x2 -> x0, other arithmetic: 5.32 us -> none  [the longest x1 4.75 us: on_device(): grad_wo[None]]
    convert_element_type x0 -> x1, other arithmetic: none -> 3.42 us  [on_device(): grad_wo = (kept_out + swapped[1].astype(F32)).astype(BF16)]
    ppermute x2, waiting for transfers between devices: 0.01 us -> 1.95 us  [with_partner(): return total + lax.ppermute(total, axis, [(i, i ^ apart) for i in devices])]
    ppermute x0 -> x1, starting transfers between devices: none -> 1.91 us  [on_device(): swapped = lax.ppermute(given, 'core', SWAP)]
    ppermute x2 -> x1, starting transfers between devices: 8.01 us -> 6.17 us  [on_device(): taken = lax.ppermute(given, 'core', SWAP)]
  transfers between devices with their start and end apart: 28 -> 28, of which waited for: 8 -> 8; matrix products, arithmetic and copies ran while one was open for 13% -> 12% of each run, Pallas kernels for 4% -> 4%
where the time goes in v8:
time: 182 us; the launch traced here: 181 us
  starting transfers between devices  109 us (60%)
  waiting for transfers between devices  25.3 us (14%)
  local copies, waits for them, and re-layouts  13.2 us (7%)
  matrix products  12.5 us (7%)
  other arithmetic  10.7 us (6%)
  Pallas kernels  8.46 us (5%)
  between operations  1.99 us (1%)
    ppermute x16, starting transfers between devices, along(): lax.ppermute(block, axis, [(i, (i + distance) % devices) for i in range(d...  63.4 us
    ppermute x16, waiting for transfers between devices, along(): lax.ppermute(block, axis, [(i, (i + distance) % devices) for i in range(d...  23.3 us
    dot_general x9, matrix products, contract(): lax.dot_general(left, right, (dims, ((), ())), preferred_element_type=F32)  12.5 us
    unnamed x60, local copies, waits for them, and re-layouts  12.4 us
    ppermute x2, starting transfers between devices, with_partner(): return total + lax.ppermute(total, axis, [(i, i ^ apart) for i in devices])  7.84 us
    ppermute x1, starting transfers between devices, on_device(): taken = lax.ppermute(given, 'core', SWAP)  6.17 us
    ppermute x1, starting transfers between devices, on_device(): val_core = lax.ppermute(val_weight, 'core', SWAP)  5.85 us
    pallas_call x1, Pallas kernels, weight_gradients(): pl.pallas_call(body, grid=(width // column,), in_specs=[by_column(o.shape...  5.26 us
  transfers between devices with their start and end apart: 28, of which 8 were waited for; matrix products, arithmetic and copies ran while one was open for 12% of the time, Pallas kernels for 4%

profile of v8, /device:TPU:1, one launch (start us, length us, event | category | flops | bytes accessed | tf_op | source)
XLA Modules:
  0.0 180.8 jit_solution(835230062060940925)
XLA Ops:
  4.2 4.8 %collective-permute-start = (bf16[32,4096]{1,0:T(8,128)(2,1)S(1)}, bf16[32,4096]{1,0:T(8,128)(2,1)S(1)}, u32[]{:S(2)}, u32[]{:S(2)}) collective-permute-start(bf16[32,4096]{1,0:T(8,128)(2,1)S(1)} %pad_maximum_fusion.2), channel_id=1, source_target_pairs={{0,2},{2,0},{1,3},{3,1},{4,6},{6,4},{5,7},{7,5},{8,10},{10,8},{9,1... | collective-permute-start | bytes 786440 | tf_op jit(solution)/shard_map/ppermute | solution.py:294
  9.1 5.9 %collective-permute-start.3 = (bf16[128,4096]{1,0:T(8,128)(2,1)}, bf16[128,4096]{1,0:T(8,128)(2,1)S(1)}, u32[]{:S(2)}, u32[]{:S(2)}) collective-permute-start(bf16[128,4096]{1,0:T(8,128)(2,1)} %bitcast.65), channel_id=1, source_target_pairs={{0,1},{1,0},{2,3},{3,2},{4,5},{5,4},{6,7},{7,6},{8,9},{9,8},{10,11... | collective-permute-start | bytes 3145736 | tf_op jit(solution)/shard_map/ppermute | solution.py:297
  17.8 3.3 %collective-permute-start.5 = (bf16[64,4096]{1,0:T(8,128)(2,1)S(1)}, bf16[64,4096]{1,0:T(8,128)(2,1)S(1)}, u32[]{:S(2)}, u32[]{:S(2)}) collective-permute-start(bf16[64,4096]{1,0:T(8,128)(2,1)S(1)} %pad_maximum_fusion.1.refs_0_), channel_id=1, source_target_pairs={{0,28},{4,0},{8,4},{12,8},{16,12},{20,16},{24,20},{28,24},{1,29},{... | collective-permute-start | bytes 1572872 | tf_op jit(solution)/shard_map/ppermute | solution.py:23
  23.1 3.6 %collective-permute-start.1 = (bf16[128,4096]{1,0:T(8,128)(2,1)}, bf16[128,4096]{1,0:T(8,128)(2,1)S(1)}, u32[]{:S(2)}, u32[]{:S(2)}) collective-permute-start(bf16[128,4096]{1,0:T(8,128)(2,1)} %bitcast.66), channel_id=1, source_target_pairs={{0,2},{2,0},{1,3},{3,1},{4,6},{6,4},{5,7},{7,5},{8,10},{10,8},{9,1... | collective-permute-start | bytes 3145736 | tf_op jit(solution)/shard_map/ppermute | solution.py:300
  26.8 4.3 %collective-permute-done.5.refs_1_ = bf16[64,4096]{1,0:T(8,128)(2,1)S(1)} collective-permute-done((bf16[64,4096]{1,0:T(8,128)(2,1)S(1)}, bf16[64,4096]{1,0:T(8,128)(2,1)S(1)}, u32[]{:S(2)}, u32[]{:S(2)}) %collective-permute-start.5) | collective-permute-done | bytes 524320 | tf_op jit(solution)/shard_map/ppermute | solution.py:23
  31.1 5.3 %collective-permute-start.6 = (bf16[64,4096]{1,0:T(8,128)(2,1)S(1)}, bf16[64,4096]{1,0:T(8,128)(2,1)S(1)}, u32[]{:S(2)}, u32[]{:S(2)}) collective-permute-start(bf16[64,4096]{1,0:T(8,128)(2,1)S(1)} %collective-permute-done.5.refs_1_), channel_id=1, source_target_pairs={{0,28},{4,0},{8,4},{12,8},{16,12},{20,16},{24,20},{28,24},{1,29},{... | collective-permute-start | bytes 1572872 | tf_op jit(solution)/shard_map/ppermute | solution.py:23
  45.6 5.3 %collective-permute-start.7 = (bf16[64,4096]{1,0:T(8,128)(2,1)S(1)}, bf16[64,4096]{1,0:T(8,128)(2,1)S(1)}, u32[]{:S(2)}, u32[]{:S(2)}) collective-permute-start(bf16[64,4096]{1,0:T(8,128)(2,1)S(1)} %collective-permute-done.6.refs_2_), channel_id=1, source_target_pairs={{0,28},{4,0},{8,4},{12,8},{16,12},{20,16},{24,20},{28,24},{1,29},{... | collective-permute-start | bytes 1572872 | tf_op jit(solution)/shard_map/ppermute | solution.py:23
  52.9 5.2 %collective-permute-start.2 = (bf16[128,4096]{1,0:T(8,128)(2,1)S(1)}, bf16[128,4096]{1,0:T(8,128)(2,1)S(1)}, u32[]{:S(2)}, u32[]{:S(2)}) collective-permute-start(bf16[128,4096]{1,0:T(8,128)(2,1)S(1)} %collective-permute-done.1.refs_6_), channel_id=1, source_target_pairs={{0,1},{1,0},{2,3},{3,2},{4,5},{5,4},{6,7},{7,6},{8,9},{9,8},{10,11... | collective-permute-start | bytes 3145736 | tf_op jit(solution)/shard_map/ppermute | solution.py:301
  60.9 4.9 %collective-permute-start.8 = (bf16[32,4096]{1,0:T(8,128)(2,1)S(1)}, bf16[32,4096]{1,0:T(8,128)(2,1)S(1)}, u32[]{:S(2)}, u32[]{:S(2)}) collective-permute-start(bf16[32,4096]{1,0:T(8,128)(2,1)S(1)} %slice.32), channel_id=1, source_target_pairs={{0,28},{4,0},{8,4},{12,8},{16,12},{20,16},{24,20},{28,24},{1,29},{... | collective-permute-start | bytes 786440 | tf_op jit(solution)/shard_map/ppermute | solution.py:23
  75.5 6.2 %collective-permute-start.13 = (f32[2,2,8,16,128]{4,3,2,1,0:T(8,128)S(1)}, f32[2,2,8,16,128]{4,3,2,1,0:T(8,128)S(1)}, u32[]{:S(2)}, u32[]{:S(2)}) collective-permute-start(f32[2,2,8,16,128]{4,3,2,1,0:T(8,128)S(1)} %get-tuple-element.52), channel_id=1, source_target_pairs={{0,1},{1,0},{2,3},{3,2},{4,5},{5,4},{6,7},{7,6},{8,9},{9,8},{10,11... | collective-permute-start | bytes 786440 | tf_op jit(solution)/shard_map/ppermute | solution.py:313
  89.0 3.4 %collective-permute-start.16 = (bf16[128,128]{1,0:T(8,128)(2,1)S(1)}, bf16[128,128]{1,0:T(8,128)(2,1)S(1)}, u32[]{:S(2)}, u32[]{:S(2)}) collective-permute-start(bf16[128,128]{1,0:T(8,128)(2,1)S(1)} %get-tuple-element.100), channel_id=1, source_target_pairs={{0,3},{1,2},{2,1},{3,0},{4,7},{5,6},{6,5},{7,4},{8,11},{9,10},{10,... | collective-permute-start | bytes 98312 | tf_op jit(solution)/shard_map/ppermute | solution.py:323
  92.5 5.3 %weight_gradients.1 = (f32[128,4096]{1,0:T(8,128)S(1)}, f32[128,4096]{1,0:T(8,128)S(1)}, bf16[2,128,4096]{2,1,0:T(8,128)(2,1)}, f32[1,4096]{1,0:T(1,128)S(1)}) custom-call(bf16[64,4096]{1,0:T(8,128)(2,1)S(1)} %copy-done.2, bf16[64,4096]{1,0:T(8,128)(2,1)S(1)} %collective-permute-done.5.refs_1_, bf16[64,4096]{1,0:T(8,128)(2,1)S(1)} %collective-permute-done.6.refs_2_, ...), custom_call_target="tpu_custom_call" | custom-call | flops 1073741824 | bytes 13631488 | tf_op jit(solution)/shard_map/weight_gradients/pallas_call | solution.py:194
  115.7 4.7 %collective-permute-start.19 = (bf16[16,4608]{1,0:T(8,128)(2,1)S(1)}, bf16[16,4608]{1,0:T(8,128)(2,1)S(1)}, u32[]{:S(2)}, u32[]{:S(2)}) collective-permute-start(bf16[16,4608]{1,0:T(8,128)(2,1)S(1)} %get-tuple-element.68), channel_id=1, source_target_pairs={{0,12},{4,16},{8,20},{12,24},{16,28},{20,0},{24,4},{28,8},{1,13},{... | collective-permute-start | bytes 442376 | tf_op jit(solution)/shard_map/ppermute | solution.py:23
  120.4 4.8 %collective-permute-start.20 = (bf16[16,4608]{1,0:T(8,128)(2,1)S(1)}, bf16[16,4608]{1,0:T(8,128)(2,1)S(1)}, u32[]{:S(2)}, u32[]{:S(2)}) collective-permute-start(bf16[16,4608]{1,0:T(8,128)(2,1)S(1)} %get-tuple-element.69), channel_id=1, source_target_pairs={{0,16},{4,20},{8,24},{12,28},{16,0},{20,4},{24,8},{28,12},{1,17},{... | collective-permute-start | bytes 442376 | tf_op jit(solution)/shard_map/ppermute | solution.py:23
  125.1 3.6 %collective-permute-start.21 = (bf16[16,4608]{1,0:T(8,128)(2,1)S(1)}, bf16[16,4608]{1,0:T(8,128)(2,1)S(1)}, u32[]{:S(2)}, u32[]{:S(2)}) collective-permute-start(bf16[16,4608]{1,0:T(8,128)(2,1)S(1)} %get-tuple-element.70), channel_id=1, source_target_pairs={{0,20},{4,24},{8,28},{12,0},{16,4},{20,8},{24,12},{28,16},{1,21},{... | collective-permute-start | bytes 442376 | tf_op jit(solution)/shard_map/ppermute | solution.py:23
  128.8 5.1 %collective-permute-start.22 = (bf16[16,4608]{1,0:T(8,128)(2,1)S(1)}, bf16[16,4608]{1,0:T(8,128)(2,1)S(1)}, u32[]{:S(2)}, u32[]{:S(2)}) collective-permute-start(bf16[16,4608]{1,0:T(8,128)(2,1)S(1)} %get-tuple-element.71), channel_id=1, source_target_pairs={{0,24},{4,28},{8,0},{12,4},{16,8},{20,12},{24,16},{28,20},{1,25},{... | collective-permute-start | bytes 442376 | tf_op jit(solution)/shard_map/ppermute | solution.py:23
  133.9 3.5 %collective-permute-start.23 = (bf16[16,4608]{1,0:T(8,128)(2,1)S(1)}, bf16[16,4608]{1,0:T(8,128)(2,1)S(1)}, u32[]{:S(2)}, u32[]{:S(2)}) collective-permute-start(bf16[16,4608]{1,0:T(8,128)(2,1)S(1)} %get-tuple-element.72), channel_id=1, source_target_pairs={{0,28},{4,0},{8,4},{12,8},{16,12},{20,16},{24,20},{28,24},{1,29},{... | collective-permute-start | bytes 442376 | tf_op jit(solution)/shard_map/ppermute | solution.py:23
  137.5 3.4 %fusion = (bf16[128,4096]{1,0:T(8,128)(2,1)}, bf16[128,4096]{1,0:T(8,128)(2,1)}) fusion(f32[128,4096]{1,0:T(8,128)S(1)} %copy-done.6, bf16[2,128,4096]{2,1,0:T(8,128)(2,1)} %collective-permute-done.24, f32[128,4096]{1,0:T(8,128)S(1)} %copy-done.4), kind=kLoop, calls=%fused_computation.2 | loop fusion | flops 3145728 | bytes 8388608 | tf_op jit(solution)/shard_map/convert_element_type | solution.py:336
  140.9 3.7 %collective-permute-done.21.refs_5_ = bf16[16,4608]{1,0:T(8,128)(2,1)S(1)} collective-permute-done((bf16[16,4608]{1,0:T(8,128)(2,1)S(1)}, bf16[16,4608]{1,0:T(8,128)(2,1)S(1)}, u32[]{:S(2)}, u32[]{:S(2)}) %collective-permute-start.21) | collective-permute-done | bytes 147488 | tf_op jit(solution)/shard_map/ppermute | solution.py:23
  144.6 6.3 %collective-permute-done.22.refs_6_ = bf16[16,4608]{1,0:T(8,128)(2,1)S(1)} collective-permute-done((bf16[16,4608]{1,0:T(8,128)(2,1)S(1)}, bf16[16,4608]{1,0:T(8,128)(2,1)S(1)}, u32[]{:S(2)}, u32[]{:S(2)}) %collective-permute-start.22) | collective-permute-done | bytes 147488 | tf_op jit(solution)/shard_map/ppermute | solution.py:23
  153.4 2.5 %collective-permute-start.26 = (f32[16,256]{1,0:T(8,128)S(1)}, f32[16,256]{1,0:T(8,128)S(1)}, u32[]{:S(2)}, u32[]{:S(2)}) collective-permute-start(f32[16,256]{1,0:T(8,128)S(1)} %get-tuple-element.91), channel_id=1, source_target_pairs={{0,2},{2,0},{1,3},{3,1},{4,6},{6,4},{5,7},{7,5},{8,10},{10,8},{9,1... | collective-permute-start | bytes 49160 | tf_op jit(solution)/shard_map/ppermute | solution.py:28
  157.9 5.3 %collective-permute-start.27 = (f32[16,256]{1,0:T(8,128)S(1)}, f32[16,256]{1,0:T(8,128)S(1)}, u32[]{:S(2)}, u32[]{:S(2)}) collective-permute-start(f32[16,256]{1,0:T(8,128)S(1)} %add.28), channel_id=1, source_target_pairs={{0,1},{1,0},{2,3},{3,2},{4,5},{5,4},{6,7},{7,6},{8,9},{9,8},{10,11... | collective-permute-start | bytes 49160 | tf_op jit(solution)/shard_map/ppermute | solution.py:28
  163.2 11.4 %collective-permute-start.25 = (bf16[16,4096]{1,0:T(8,128)(2,1)S(1)}, bf16[16,4096]{1,0:T(8,128)(2,1)S(1)}, u32[]{:S(2)}, u32[]{:S(2)}) collective-permute-start(bf16[16,4096]{1,0:T(8,128)(2,1)S(1)} %get-tuple-element.86), channel_id=1, source_target_pairs={{0,480},{32,0},{64,32},{96,64},{128,96},{160,128},{192,160},{224,1... | collective-permute-start | bytes 393224 | tf_op jit(solution)/shard_map/ppermute | solution.py:23
  175.8 4.3 %collective-permute-done.25 = bf16[16,4096]{1,0:T(8,128)(2,1)S(1)} collective-permute-done((bf16[16,4096]{1,0:T(8,128)(2,1)S(1)}, bf16[16,4096]{1,0:T(8,128)(2,1)S(1)}, u32[]{:S(2)}, u32[]{:S(2)}) %collective-permute-start.25) | collective-permute-done | bytes 131104 | tf_op jit(solution)/shard_map/ppermute | solution.py:23
  (124 shorter events, 62.8 us)
Async XLA Ops:
  4.2 12.6 %collective-permute-start = (bf16[32,4096]{1,0:T(8,128)(2,1)S(1)}, bf16[32,4096]{1,0:T(8,128)(2,1)S(1)}, u32[]{:S(2)}, u32[]{:S(2)}) collective-permute-start(bf16[32,4096]{1,0:T(8,128)(2,1)S(1)} %pad_maximum_fusion.2), channel_id=1, source_target_pairs={{0,2},{2,0},{1,3},{3,1},{4,6},{6,4},{5,7},{7,5},{8,10},{10,8},{9,1... | collective-permute-start | bytes 786440 | tf_op jit(solution)/shard_map/ppermute | solution.py:294
  9.1 29.3 %collective-permute-start.3 = (bf16[128,4096]{1,0:T(8,128)(2,1)}, bf16[128,4096]{1,0:T(8,128)(2,1)S(1)}, u32[]{:S(2)}, u32[]{:S(2)}) collective-permute-start(bf16[128,4096]{1,0:T(8,128)(2,1)} %bitcast.65), channel_id=1, source_target_pairs={{0,1},{1,0},{2,3},{3,2},{4,5},{5,4},{6,7},{7,6},{8,9},{9,8},{10,11... | collective-permute-start | bytes 3145736 | tf_op jit(solution)/shard_map/ppermute | solution.py:297
  14.9 23.5 %collective-permute-start.4 = (bf16[128,4096]{1,0:T(8,128)(2,1)}, bf16[128,4096]{1,0:T(8,128)(2,1)}, u32[]{:S(2)}, u32[]{:S(2)}) collective-permute-start(bf16[128,4096]{1,0:T(8,128)(2,1)} %bitcast.78), channel_id=1, source_target_pairs={{0,1},{1,0},{2,3},{3,2},{4,5},{5,4},{6,7},{7,6},{8,9},{9,8},{10,11... | collective-permute-start | bytes 3145736 | tf_op jit(solution)/shard_map/ppermute | solution.py:298
  17.8 13.3 %collective-permute-start.5 = (bf16[64,4096]{1,0:T(8,128)(2,1)S(1)}, bf16[64,4096]{1,0:T(8,128)(2,1)S(1)}, u32[]{:S(2)}, u32[]{:S(2)}) collective-permute-start(bf16[64,4096]{1,0:T(8,128)(2,1)S(1)} %pad_maximum_fusion.1.refs_0_), channel_id=1, source_target_pairs={{0,28},{4,0},{8,4},{12,8},{16,12},{20,16},{24,20},{28,24},{1,29},{... | collective-permute-start | bytes 1572872 | tf_op jit(solution)/shard_map/ppermute | solution.py:23
  21.1 15.3 %collective-permute-start.9 = (bf16[64,4096]{1,0:T(8,128)(2,1)S(1)}, bf16[64,4096]{1,0:T(8,128)(2,1)S(1)}, u32[]{:S(2)}, u32[]{:S(2)}) collective-permute-start(bf16[64,4096]{1,0:T(8,128)(2,1)S(1)} %pad_maximum_fusion.1.refs_0_), channel_id=1, source_target_pairs={{0,4},{4,8},{8,12},{12,16},{16,20},{20,24},{24,28},{28,0},{1,5},{5... | collective-permute-start | bytes 1572872 | tf_op jit(solution)/shard_map/ppermute | solution.py:23
  23.1 29.7 %collective-permute-start.1 = (bf16[128,4096]{1,0:T(8,128)(2,1)}, bf16[128,4096]{1,0:T(8,128)(2,1)S(1)}, u32[]{:S(2)}, u32[]{:S(2)}) collective-permute-start(bf16[128,4096]{1,0:T(8,128)(2,1)} %bitcast.66), channel_id=1, source_target_pairs={{0,2},{2,0},{1,3},{3,1},{4,6},{6,4},{5,7},{7,5},{8,10},{10,8},{9,1... | collective-permute-start | bytes 3145736 | tf_op jit(solution)/shard_map/ppermute | solution.py:300
  31.1 14.5 %collective-permute-start.6 = (bf16[64,4096]{1,0:T(8,128)(2,1)S(1)}, bf16[64,4096]{1,0:T(8,128)(2,1)S(1)}, u32[]{:S(2)}, u32[]{:S(2)}) collective-permute-start(bf16[64,4096]{1,0:T(8,128)(2,1)S(1)} %collective-permute-done.5.refs_1_), channel_id=1, source_target_pairs={{0,28},{4,0},{8,4},{12,8},{16,12},{20,16},{24,20},{28,24},{1,29},{... | collective-permute-start | bytes 1572872 | tf_op jit(solution)/shard_map/ppermute | solution.py:23
  36.4 14.5 %collective-permute-start.10 = (bf16[64,4096]{1,0:T(8,128)(2,1)S(1)}, bf16[64,4096]{1,0:T(8,128)(2,1)S(1)}, u32[]{:S(2)}, u32[]{:S(2)}) collective-permute-start(bf16[64,4096]{1,0:T(8,128)(2,1)S(1)} %collective-permute-done.9.refs_8_), channel_id=1, source_target_pairs={{0,4},{4,8},{8,12},{12,16},{16,20},{20,24},{24,28},{28,0},{1,5},{5... | collective-permute-start | bytes 1572872 | tf_op jit(solution)/shard_map/ppermute | solution.py:23
  45.6 15.2 %collective-permute-start.7 = (bf16[64,4096]{1,0:T(8,128)(2,1)S(1)}, bf16[64,4096]{1,0:T(8,128)(2,1)S(1)}, u32[]{:S(2)}, u32[]{:S(2)}) collective-permute-start(bf16[64,4096]{1,0:T(8,128)(2,1)S(1)} %collective-permute-done.6.refs_2_), channel_id=1, source_target_pairs={{0,28},{4,0},{8,4},{12,8},{16,12},{20,16},{24,20},{28,24},{1,29},{... | collective-permute-start | bytes 1572872 | tf_op jit(solution)/shard_map/ppermute | solution.py:23
  50.9 14.8 %collective-permute-start.11 = (bf16[64,4096]{1,0:T(8,128)(2,1)S(1)}, bf16[64,4096]{1,0:T(8,128)(2,1)S(1)}, u32[]{:S(2)}, u32[]{:S(2)}) collective-permute-start(bf16[64,4096]{1,0:T(8,128)(2,1)S(1)} %collective-permute-done.10.refs_7_), channel_id=1, source_target_pairs={{0,4},{4,8},{8,12},{12,16},{16,20},{20,24},{24,28},{28,0},{1,5},{5... | collective-permute-start | bytes 1572872 | tf_op jit(solution)/shard_map/ppermute | solution.py:23
  52.9 29.6 %collective-permute-start.2 = (bf16[128,4096]{1,0:T(8,128)(2,1)S(1)}, bf16[128,4096]{1,0:T(8,128)(2,1)S(1)}, u32[]{:S(2)}, u32[]{:S(2)}) collective-permute-start(bf16[128,4096]{1,0:T(8,128)(2,1)S(1)} %collective-permute-done.1.refs_6_), channel_id=1, source_target_pairs={{0,1},{1,0},{2,3},{3,2},{4,5},{5,4},{6,7},{7,6},{8,9},{9,8},{10,11... | collective-permute-start | bytes 3145736 | tf_op jit(solution)/shard_map/ppermute | solution.py:301
  60.9 9.6 %collective-permute-start.8 = (bf16[32,4096]{1,0:T(8,128)(2,1)S(1)}, bf16[32,4096]{1,0:T(8,128)(2,1)S(1)}, u32[]{:S(2)}, u32[]{:S(2)}) collective-permute-start(bf16[32,4096]{1,0:T(8,128)(2,1)S(1)} %slice.32), channel_id=1, source_target_pairs={{0,28},{4,0},{8,4},{12,8},{16,12},{20,16},{24,20},{28,24},{1,29},{... | collective-permute-start | bytes 786440 | tf_op jit(solution)/shard_map/ppermute | solution.py:23
  86.4 14.6 %collective-permute-start.15 = (bf16[128,128]{1,0:T(8,128)(2,1)S(1)}, bf16[128,128]{1,0:T(8,128)(2,1)S(1)}, u32[]{:S(2)}, u32[]{:S(2)}) collective-permute-start(bf16[128,128]{1,0:T(8,128)(2,1)S(1)} %get-tuple-element.101), channel_id=1, source_target_pairs={{0,2},{2,0},{1,3},{3,1},{4,6},{6,4},{5,7},{7,5},{8,10},{10,8},{9,1... | collective-permute-start | bytes 98312 | tf_op jit(solution)/shard_map/ppermute | solution.py:322
  89.0 12.7 %collective-permute-start.16 = (bf16[128,128]{1,0:T(8,128)(2,1)S(1)}, bf16[128,128]{1,0:T(8,128)(2,1)S(1)}, u32[]{:S(2)}, u32[]{:S(2)}) collective-permute-start(bf16[128,128]{1,0:T(8,128)(2,1)S(1)} %get-tuple-element.100), channel_id=1, source_target_pairs={{0,3},{1,2},{2,1},{3,0},{4,7},{5,6},{6,5},{7,4},{8,11},{9,10},{10,... | collective-permute-start | bytes 98312 | tf_op jit(solution)/shard_map/ppermute | solution.py:323
  102.3 31.6 %collective-permute-start.24 = (bf16[2,128,4096]{2,1,0:T(8,128)(2,1)}, bf16[2,128,4096]{2,1,0:T(8,128)(2,1)}, u32[]{:S(2)}, u32[]{:S(2)}) collective-permute-start(bf16[2,128,4096]{2,1,0:T(8,128)(2,1)} %get-tuple-element.74), channel_id=1, source_target_pairs={{0,1},{1,0},{2,3},{3,2},{4,5},{5,4},{6,7},{7,6},{8,9},{9,8},{10,11... | collective-permute-start | bytes 6291464 | tf_op jit(solution)/shard_map/ppermute | solution.py:327
  111.2 13.9 %collective-permute-start.17 = (bf16[16,4608]{1,0:T(8,128)(2,1)S(1)}, bf16[16,4608]{1,0:T(8,128)(2,1)S(1)}, u32[]{:S(2)}, u32[]{:S(2)}) collective-permute-start(bf16[16,4608]{1,0:T(8,128)(2,1)S(1)} %get-tuple-element.66), channel_id=1, source_target_pairs={{0,4},{4,8},{8,12},{12,16},{16,20},{20,24},{24,28},{28,0},{1,5},{5... | collective-permute-start | bytes 442376 | tf_op jit(solution)/shard_map/ppermute | solution.py:23
  113.2 15.6 %collective-permute-start.18 = (bf16[16,4608]{1,0:T(8,128)(2,1)S(1)}, bf16[16,4608]{1,0:T(8,128)(2,1)S(1)}, u32[]{:S(2)}, u32[]{:S(2)}) collective-permute-start(bf16[16,4608]{1,0:T(8,128)(2,1)S(1)} %get-tuple-element.67), channel_id=1, source_target_pairs={{0,8},{4,12},{8,16},{12,20},{16,24},{20,28},{24,0},{28,4},{1,9},{5... | collective-permute-start | bytes 442376 | tf_op jit(solution)/shard_map/ppermute | solution.py:23
  115.7 25.2 %collective-permute-start.19 = (bf16[16,4608]{1,0:T(8,128)(2,1)S(1)}, bf16[16,4608]{1,0:T(8,128)(2,1)S(1)}, u32[]{:S(2)}, u32[]{:S(2)}) collective-permute-start(bf16[16,4608]{1,0:T(8,128)(2,1)S(1)} %get-tuple-element.68), channel_id=1, source_target_pairs={{0,12},{4,16},{8,20},{12,24},{16,28},{20,0},{24,4},{28,8},{1,13},{... | collective-permute-start | bytes 442376 | tf_op jit(solution)/shard_map/ppermute | solution.py:23
  120.4 20.5 %collective-permute-start.20 = (bf16[16,4608]{1,0:T(8,128)(2,1)S(1)}, bf16[16,4608]{1,0:T(8,128)(2,1)S(1)}, u32[]{:S(2)}, u32[]{:S(2)}) collective-permute-start(bf16[16,4608]{1,0:T(8,128)(2,1)S(1)} %get-tuple-element.69), channel_id=1, source_target_pairs={{0,16},{4,20},{8,24},{12,28},{16,0},{20,4},{24,8},{28,12},{1,17},{... | collective-permute-start | bytes 442376 | tf_op jit(solution)/shard_map/ppermute | solution.py:23
  125.1 19.5 %collective-permute-start.21 = (bf16[16,4608]{1,0:T(8,128)(2,1)S(1)}, bf16[16,4608]{1,0:T(8,128)(2,1)S(1)}, u32[]{:S(2)}, u32[]{:S(2)}) collective-permute-start(bf16[16,4608]{1,0:T(8,128)(2,1)S(1)} %get-tuple-element.70), channel_id=1, source_target_pairs={{0,20},{4,24},{8,28},{12,0},{16,4},{20,8},{24,12},{28,16},{1,21},{... | collective-permute-start | bytes 442376 | tf_op jit(solution)/shard_map/ppermute | solution.py:23
  128.8 22.1 %collective-permute-start.22 = (bf16[16,4608]{1,0:T(8,128)(2,1)S(1)}, bf16[16,4608]{1,0:T(8,128)(2,1)S(1)}, u32[]{:S(2)}, u32[]{:S(2)}) collective-permute-start(bf16[16,4608]{1,0:T(8,128)(2,1)S(1)} %get-tuple-element.71), channel_id=1, source_target_pairs={{0,24},{4,28},{8,0},{12,4},{16,8},{20,12},{24,16},{28,20},{1,25},{... | collective-permute-start | bytes 442376 | tf_op jit(solution)/shard_map/ppermute | solution.py:23
  133.9 18.6 %collective-permute-start.23 = (bf16[16,4608]{1,0:T(8,128)(2,1)S(1)}, bf16[16,4608]{1,0:T(8,128)(2,1)S(1)}, u32[]{:S(2)}, u32[]{:S(2)}) collective-permute-start(bf16[16,4608]{1,0:T(8,128)(2,1)S(1)} %get-tuple-element.72), channel_id=1, source_target_pairs={{0,28},{4,0},{8,4},{12,8},{16,12},{20,16},{24,20},{28,24},{1,29},{... | collective-permute-start | bytes 442376 | tf_op jit(solution)/shard_map/ppermute | solution.py:23
  157.9 17.3 %collective-permute-start.27 = (f32[16,256]{1,0:T(8,128)S(1)}, f32[16,256]{1,0:T(8,128)S(1)}, u32[]{:S(2)}, u32[]{:S(2)}) collective-permute-start(f32[16,256]{1,0:T(8,128)S(1)} %add.28), channel_id=1, source_target_pairs={{0,1},{1,0},{2,3},{3,2},{4,5},{5,4},{6,7},{7,6},{8,9},{9,8},{10,11... | collective-permute-start | bytes 49160 | tf_op jit(solution)/shard_map/ppermute | solution.py:28
  163.2 16.9 %collective-permute-start.25 = (bf16[16,4096]{1,0:T(8,128)(2,1)S(1)}, bf16[16,4096]{1,0:T(8,128)(2,1)S(1)}, u32[]{:S(2)}, u32[]{:S(2)}) collective-permute-start(bf16[16,4096]{1,0:T(8,128)(2,1)S(1)} %get-tuple-element.86), channel_id=1, source_target_pairs={{0,480},{32,0},{64,32},{96,64},{128,96},{160,128},{192,160},{224,1... | collective-permute-start | bytes 393224 | tf_op jit(solution)/shard_map/ppermute | solution.py:23
  (32 other events, 340.4 us)
